TPU v7x, 512 devices: a whole 4x8x8 slice. The times are simulated.
512 devices in a mesh: row: 32 (over z_lo, y), col: 16 (over x, z_hi, core).
Axes of the slice: x: 4, y: 8, z: 8 (z_hi: 2, z_lo: 4; z = z_hi * 4 + z_lo), core: 2. Of those that a mesh axis runs over, the one named last changes fastest.
Arguments:
- features: bfloat16 [16, 4096, 128], P('col', 'row'), may hold values from -6 to 6
- weight: bfloat16 [128, 256], replicated, may hold values from -0.5 to 0.5
- tile_values: bfloat16 [32, 16, 32, 128, 128], P('row', 'col'), may hold values from -0.125 to 0.125
- tile_rows: int32 [32, 16, 32], P('row', 'col'), may hold values from 0 to 15
- tile_cols: int32 [32, 16, 32], P('row', 'col'), may hold values from 0 to 31
- tile_count: int32 [32, 16], P('row', 'col'), may hold values from 4 to 32, as said below
- cotangent: bfloat16 [32, 2048, 256], P('row', 'col'), may hold values from -6 to 6
Outputs:
- output: bfloat16 [32, 2048, 256], P('row', 'col')
- grad_features: bfloat16 [16, 4096, 128], P('col', 'row')
- weight_grad: float32 [128, 256], replicated
Inputs may be any that keep to these rules, and one draw needn't show every extreme that they name: Slots at or beyond a cell's tile_count are ignored; some cell is full in every draw. Tile coordinates within a cell may repeat, and repeated tiles add.
All inputs are finite; a program needn't handle non-finite values.
Results may differ from a plain program's by a relative error of at most 0.022.
Values may be sent and summed in bfloat16 or wider, within the bound.
No kernel may reach another device: no remote copies, remote signals or barrier semaphores. Data moves between devices by JAX's collectives and lax.ppermute only.
A program may use at most 64 MiB of HBM per device.

v0:
```python
import jax
import jax.numpy as jnp
from jax import lax
from jax.sharding import PartitionSpec as P


def tile_products(
    tile_block, target_ids, source_ids, tile_total, source, out_blocks, transpose, block_width
):
    source_blocks = source[source_ids]
    if transpose:
        products = jnp.einsum(
            "tij,tif->tjf", tile_block, source_blocks, preferred_element_type=jnp.float32
        )
    else:
        products = jnp.einsum(
            "tij,tjf->tif", tile_block, source_blocks, preferred_element_type=jnp.float32
        )
    slot_ids = jnp.arange(block_width, dtype=jnp.int32)
    live_mask = slot_ids < tile_total
    one_hot = (
        (target_ids[None, :] == jnp.arange(out_blocks, dtype=jnp.int32)[:, None])
        & live_mask[None, :]
    ).astype(jnp.float32)
    return jnp.einsum("rt,tif->rif", one_hot, products, precision=lax.Precision.HIGH)


def spread_tiles(tile_block, target_ids, source_ids, tile_total, source, out_blocks, transpose):
    capacity = tile_block.shape[0]
    return tile_products(
        tile_block, target_ids, source_ids, tile_total, source, out_blocks, transpose, capacity
    )


def on_device(features, weight, tile_values, tile_rows, tile_cols, tile_count, cotangent):
    rows_dev = features.shape[1]
    width_in = features.shape[2]
    tile_size = tile_values.shape[-1]
    row_devices = lax.axis_size("row")
    col_devices = lax.axis_size("col")
    row_tiles = rows_dev * col_devices // tile_size
    col_tiles = rows_dev * row_devices // tile_size
    node_total = rows_dev * row_devices * col_devices
    tile_block = tile_values[0, 0]
    row_ids = tile_rows[0, 0]
    col_ids = tile_cols[0, 0]
    tile_total = tile_count[0, 0]
    gathered = lax.all_gather(features, "row", axis=1, tiled=True)
    col_source = gathered.reshape(col_tiles, tile_size, width_in)
    partial_value = spread_tiles(
        tile_block, row_ids, col_ids, tile_total, col_source, row_tiles, False
    )
    partial_value = partial_value.reshape(row_tiles * tile_size, width_in)
    aggregated = lax.psum_scatter(partial_value, "col", scatter_dimension=0, tiled=True).astype(
        jnp.bfloat16
    )
    pre = jnp.dot(aggregated, weight, preferred_element_type=jnp.float32)
    sigma = jax.nn.sigmoid(pre)
    output = (pre * sigma).astype(jnp.bfloat16)[None]
    slope = sigma * (1.0 + pre * (1.0 - sigma))
    grad_pre = (cotangent[0].astype(jnp.float32) * slope).astype(jnp.bfloat16)
    local_grad = lax.dot_general(
        aggregated, grad_pre, (((0,), (0,)), ((), ())), preferred_element_type=jnp.float32
    )
    weight_grad = lax.psum(local_grad, ("row", "col")) * node_total ** (-0.5)
    full_pre = lax.all_gather(grad_pre, "col", axis=0, tiled=True)
    row_source = lax.dot_general(
        full_pre, weight, (((1,), (1,)), ((), ())), preferred_element_type=jnp.float32
    ).astype(jnp.bfloat16)
    row_source = row_source.reshape(row_tiles, tile_size, width_in)
    partial_back = spread_tiles(
        tile_block, col_ids, row_ids, tile_total, row_source, col_tiles, True
    )
    partial_back = partial_back.reshape(col_tiles * tile_size, width_in)
    grad_features = lax.psum_scatter(
        partial_back.astype(jnp.bfloat16), "row", scatter_dimension=0, tiled=True
    )[None]
    return (output, grad_features, weight_grad)


def solution(mesh):
    placed = (
        P("col", "row", None),
        P(),
        P("row", "col", None, None, None),
        P("row", "col", None),
        P("row", "col", None),
        P("row", "col"),
        P("row", "col", None),
    )
    return jax.shard_map(
        on_device,
        mesh=mesh,
        in_specs=placed,
        out_specs=(P("row", "col", None), P("col", "row", None), P()),
        check_vma=False,
    )
```

profile of v0, /device:TPU:2, one launch (start us, length us, event | category | flops | bytes accessed | tf_op | source)
XLA Modules:
  0.0 751.9 jit_solution(3322477829426455184)
XLA Ops:
  7.2 0.0 copy-start
  7.2 0.0 all-gather.3.cloned.1.call-start
  7.2 0.7 all-gather.3.cloned.1.call-update
  7.9 0.0 reduce-scatter.3.cloned.1.call-start
  8.6 0.7 fusion.27
  9.3 158.5 %all-gather.3.cloned.1.call-done = bf16[1,4096,128]{2,1,0:T(8,128)(2,1)} async-done(((bf16[1,128,128]{2,1,0:T(8,128)(2,1)}), bf16[1,4096,128]{2,1,0:T(8,128)(2,1)}) %all-gather.3.cloned.1.call-update) | async-done | bytes 1048592 | tf_op jit(solution)/shard_map/all_gather | solution.py:48
  167.8 2.9 gather_fusion
  170.7 0.0 copy-done
  170.7 2.1 fusion.9
  172.8 0.0 copy-start.2
  172.8 2.1 copy.12
  174.9 0.0 copy-done.2
  174.9 2.1 fusion.2
  177.0 0.0 copy-start.1
  177.0 0.0 copy-start.4
  177.0 1.3 copy.10
  178.3 0.0 reduce-scatter.3.cloned.1.call-update
  178.3 0.0 all-gather.5.cloned.1.call-start
  178.4 83.6 %reduce-scatter.3.cloned.1.call-done = f32[128,128]{1,0:T(8,128)} async-done(((f32[2048,128]{1,0:T(8,128)}), f32[128,128]{1,0:T(8,128)}) %reduce-scatter.3.cloned.1.call-update) | async-done | bytes 65552 | tf_op jit(solution)/shard_map/reduce_scatter | solution.py:54
  262.0 0.0 copy-done.1
  262.0 0.0 copy-done.4
  262.0 1.7 fusion.11
  263.7 0.0 all-gather.5.cloned.1.call-update
  263.7 0.0 all-reduce.2.cloned.1.call-start
  263.8 1.7 fusion.13
  265.5 0.0 all-reduce.2.cloned.1.call-update
  265.5 0.0 reduce-scatter.5.cloned.1.call-start
  265.6 57.5 %all-gather.5.cloned.1.call-done = bf16[2048,256]{1,0:T(8,128)(2,1)} async-done(((bf16[128,256]{1,0:T(8,128)(2,1)}), bf16[2048,256]{1,0:T(8,128)(2,1)}) %all-gather.5.cloned.1.call-update) | async-done | bytes 1048592 | tf_op jit(solution)/shard_map/all_gather | solution.py:66
  323.0 1.6 convolution_convert_fusion
  324.7 0.8 gather_fusion.1
  325.5 1.9 fusion.7
  327.3 0.0 copy-start.3
  327.3 2.4 copy.13
  329.7 0.0 copy-done.3
  329.7 0.7 fusion.4
  330.5 1.4 copy.11
  331.8 0.0 reduce-scatter.5.cloned.1.call-update
  331.9 252.5 %all-reduce.2.cloned.1.call-done = f32[128,256]{1,0:T(8,128)} async-done(((f32[128,256]{1,0:T(8,128)}), f32[128,256]{1,0:T(8,128)}) %all-reduce.2.cloned.1.call-update) | async-done | bytes 131088 | tf_op jit(solution)/shard_map/psum | solution.py:65
  584.4 1.6 broadcast_multiply_fusion
  586.0 159.4 %reduce-scatter.5.cloned.1.call-done = bf16[128,128]{1,0:T(8,128)(2,1)} async-done(((bf16[4096,128]{1,0:T(8,128)(2,1)}), bf16[128,128]{1,0:T(8,128)(2,1)}) %reduce-scatter.5.cloned.1.call-update) | async-done | bytes 32784 | tf_op jit(solution)/shard_map/reduce_scatter | solution.py:75
  (4 shorter events, 0.0 us)
Async XLA Ops:
  7.2 163.6 %copy-start = (bf16[1,1,32,128,128]{4,3,2,1,0:T(8,128)(2,1)S(1)}, bf16[1,1,32,128,128]{4,3,2,1,0:T(8,128)(2,1)}, u32[]{:S(2)}) copy-start(bf16[1,1,32,128,128]{4,3,2,1,0:T(8,128)(2,1)} %param.9) | copy-start | bytes 3145732
  7.2 160.6 %all-gather.3.cloned.1.call-start = ((), (), s32[]{:S(2)}) async-start(), calls=%async_computation.2 | async-start | bytes 1081344 | tf_op jit(solution)/shard_map/all_gather | solution.py:48
  7.9 254.1 %reduce-scatter.3.cloned.1.call-start = ((), (), s32[]{:S(2)}) async-start(), calls=%async_computation.3 | async-start | bytes 1114112 | tf_op jit(solution)/shard_map/reduce_scatter | solution.py:54
  172.8 2.1 copy-start.2
  177.0 85.0 %copy-start.1 = (bf16[128,256]{1,0:T(8,128)(2,1)S(1)}, bf16[128,256]{1,0:T(8,128)(2,1)}, u32[]{:S(2)}) copy-start(bf16[128,256]{1,0:T(8,128)(2,1)} %param.8) | copy-start | bytes 196612
  177.0 85.0 %copy-start.4 = (bf16[1,128,256]{2,1,0:T(8,128)(2,1)S(1)}, bf16[1,128,256]{2,1,0:T(8,128)(2,1)}, u32[]{:S(2)}) copy-start(bf16[1,128,256]{2,1,0:T(8,128)(2,1)} %param.13) | copy-start | bytes 196612
  178.3 144.7 %all-gather.5.cloned.1.call-start = ((), (), s32[]{:S(2)}) async-start(), calls=%async_computation.4 | async-start | bytes 1114112 | tf_op jit(solution)/shard_map/all_gather | solution.py:66
  263.7 320.7 %all-reduce.2.cloned.1.call-start = ((), (), s32[]{:S(2)}) async-start(), calls=%async_computation.6 | async-start | bytes 262144 | tf_op jit(solution)/shard_map/psum | solution.py:65
  265.5 479.9 %reduce-scatter.5.cloned.1.call-start = ((), (), s32[]{:S(2)}) async-start(), calls=%async_computation.5 | async-start | bytes 1081344 | tf_op jit(solution)/shard_map/reduce_scatter | solution.py:75
  327.3 2.4 copy-start.3
Sparse Core Ops, SparseCore 0:
  10.1 157.6 all-gather.2
  178.4 83.4 reduce-scatter.2
  265.8 57.2 all-gather.4
  329.2 255.1 all-reduce.1
  587.6 157.7 reduce-scatter.4
where the time goes:
time: 752 us
  waiting for transfers between devices  712 us (95%)
  between operations  14.5 us (2%)
  matrix products  11.8 us (2%)
  local copies, waits for them, and re-layouts  10.8 us (1%)
    psum x1, waiting for transfers between devices, on_device(): weight_grad = lax.psum(local_grad, ('row', 'col')) * node_total ** (-0.5)  253 us
    reduce_scatter x1, waiting for transfers between devices, on_device(): lax.psum_scatter(partial_back.astype(jnp.bfloat16), 'row', scatter_dimens...  159 us
    all_gather x1, waiting for transfers between devices, on_device(): gathered = lax.all_gather(features, 'row', axis=1, tiled=True)  159 us
    reduce_scatter x1, waiting for transfers between devices, on_device(): lax.psum_scatter(partial_value, 'col', scatter_dimension=0, tiled=True)  83.6 us
    all_gather x1, waiting for transfers between devices, on_device(): full_pre = lax.all_gather(grad_pre, 'col', axis=0, tiled=True)  57.5 us
  transfers between devices with their start and end apart: 5, of which 5 were waited for; matrix products, arithmetic and copies ran while one was open for 2% of the time, Pallas kernels for 0%

commit v1 on v0

v1 whole, which is shorter than its diff:
```python
import jax
import jax.numpy as jnp
from jax import lax
from jax.sharding import PartitionSpec as P


def tile_products(tile_block, target_ids, source_ids, tile_total, source, out_blocks, transpose):
    source_blocks = source[source_ids]
    if transpose:
        products = jnp.einsum(
            "tij,tif->tjf", tile_block, source_blocks, preferred_element_type=jnp.float32
        )
    else:
        products = jnp.einsum(
            "tij,tjf->tif", tile_block, source_blocks, preferred_element_type=jnp.float32
        )
    slot_ids = jnp.arange(tile_block.shape[0], dtype=jnp.int32)
    live_mask = slot_ids < tile_total
    one_hot = (
        (target_ids[None, :] == jnp.arange(out_blocks, dtype=jnp.int32)[:, None])
        & live_mask[None, :]
    ).astype(jnp.float32)
    return jnp.einsum("rt,tif->rif", one_hot, products, precision=lax.Precision.HIGH)


def split_f32(x):
    hi = x.astype(jnp.bfloat16)
    lo = (x - hi.astype(jnp.float32)).astype(jnp.bfloat16)
    return hi, lo


def on_device(features, weight, tile_values, tile_rows, tile_cols, tile_count, cotangent):
    rows_dev = features.shape[1]
    width_in = features.shape[2]
    width_out = weight.shape[1]
    tile_size = tile_values.shape[-1]
    n_row = lax.axis_size("row")
    n_col = lax.axis_size("col")
    row_tiles = rows_dev * n_col // tile_size
    col_tiles = rows_dev * n_row // tile_size
    node_total = rows_dev * n_row * n_col
    tile_block = tile_values[0, 0]
    row_ids = tile_rows[0, 0]
    col_ids = tile_cols[0, 0]
    tile_total = tile_count[0, 0]

    own = features[0]
    gathered = lax.all_to_all(
        jnp.broadcast_to(own[None], (n_row,) + own.shape), "row", 0, 0, tiled=False
    )
    col_source = gathered.reshape(col_tiles, tile_size, width_in)
    partial_value = tile_products(tile_block, row_ids, col_ids, tile_total, col_source, row_tiles, False)
    sent = partial_value.reshape(n_col, rows_dev, width_in).astype(jnp.bfloat16)
    got = lax.all_to_all(sent, "col", 0, 0, tiled=False)
    aggregated = got.astype(jnp.float32).sum(0).astype(jnp.bfloat16)

    pre = jnp.dot(aggregated, weight, preferred_element_type=jnp.float32)
    sigma = jax.nn.sigmoid(pre)
    output = (pre * sigma).astype(jnp.bfloat16)[None]
    slope = sigma * (1.0 + pre * (1.0 - sigma))
    grad_pre = (cotangent[0].astype(jnp.float32) * slope).astype(jnp.bfloat16)
    local_grad = lax.dot_general(
        aggregated, grad_pre, (((0,), (0,)), ((), ())), preferred_element_type=jnp.float32
    )
    grad_agg = lax.dot_general(
        grad_pre, weight, (((1,), (1,)), ((), ())), preferred_element_type=jnp.float32
    ).astype(jnp.bfloat16)

    wg_rows = width_in // n_col
    hi, lo = split_f32(local_grad.reshape(n_col, wg_rows, width_out))
    wg_words = jnp.stack([hi, lo], axis=1).reshape(n_col, -1, width_in)
    payload = jnp.concatenate(
        [jnp.broadcast_to(grad_agg[None], (n_col,) + grad_agg.shape), wg_words], axis=1
    )
    got = lax.all_to_all(payload, "col", 0, 0, tiled=False)
    row_source = got[:, :rows_dev].reshape(row_tiles, tile_size, width_in)
    wg_got = got[:, rows_dev:].reshape(n_col, 2, wg_rows * width_out).astype(jnp.float32)
    wg_col = (wg_got[:, 0] + wg_got[:, 1]).sum(0)

    partial_back = tile_products(tile_block, col_ids, row_ids, tile_total, row_source, col_tiles, True)
    piece = wg_col.shape[0] // n_row
    hi, lo = split_f32(wg_col.reshape(n_row, piece))
    wg_words = jnp.concatenate([hi, lo], axis=1).reshape(n_row, 1, 2 * piece)
    payload = jnp.concatenate(
        [partial_back.reshape(n_row, rows_dev, width_in).astype(jnp.bfloat16), wg_words], axis=1
    )
    got = lax.all_to_all(payload, "row", 0, 0, tiled=False)
    grad_features = got[:, :rows_dev].astype(jnp.float32).sum(0).astype(jnp.bfloat16)[None]
    wg_got = got[:, rows_dev].astype(jnp.float32)
    wg_piece = (wg_got[:, :piece] + wg_got[:, piece:]).sum(0)

    n_all = n_row * n_col
    everyone = lax.all_to_all(
        jnp.broadcast_to(wg_piece[None], (n_all, piece)), ("row", "col"), 0, 0, tiled=False
    )
    weight_grad = everyone.reshape(n_row, n_col, piece).transpose(1, 0, 2).reshape(width_in, width_out)
    weight_grad = weight_grad * node_total ** (-0.5)
    return (output, grad_features, weight_grad)


def solution(mesh):
    placed = (
        P("col", "row", None),
        P(),
        P("row", "col", None, None, None),
        P("row", "col", None),
        P("row", "col", None),
        P("row", "col"),
        P("row", "col", None),
    )
    return jax.shard_map(
        on_device,
        mesh=mesh,
        in_specs=placed,
        out_specs=(P("row", "col", None), P("col", "row", None), P()),
        check_vma=False,
    )
```

time: 752 us -> 182 us (0.24)
  the two profiles are of different devices: /device:TPU:2 before, /device:TPU:1 now
where the time goes in v1:
time: 182 us
  blocking collectives  69.2 us (38%)
  waiting for transfers between devices  59.9 us (33%)
  starting transfers between devices  29.4 us (16%)
  local copies, waits for them, and re-layouts  11.7 us (6%)
  matrix products  7.97 us (4%)
  other arithmetic  2.28 us (1%)
    all_to_all x1, blocking collectives, on_device(): got = lax.all_to_all(payload, 'row', 0, 0, tiled=False)  38.3 us
    all_to_all x1, blocking collectives, on_device(): got = lax.all_to_all(sent, 'col', 0, 0, tiled=False)  30.9 us
    all_to_all x1, waiting for transfers between devices, on_device(): lax.all_to_all(jnp.broadcast_to(own[None], (n_row,) + own.shape), 'row',...  25.2 us
    all_to_all x1, waiting for transfers between devices, on_device(): got = lax.all_to_all(payload, 'col', 0, 0, tiled=False)  18 us
    all_to_all x1, waiting for transfers between devices, on_device(): lax.all_to_all(jnp.broadcast_to(wg_piece[None], (n_all, piece)), ('row',...  16.8 us
    all_to_all x1, starting transfers between devices, on_device(): lax.all_to_all(jnp.broadcast_to(own[None], (n_row,) + own.shape), 'row',...  13.5 us
    all_to_all x1, starting transfers between devices, on_device(): lax.all_to_all(jnp.broadcast_to(wg_piece[None], (n_all, piece)), ('row',...  9.94 us
    all_to_all x1, starting transfers between devices, on_device(): got = lax.all_to_all(payload, 'col', 0, 0, tiled=False)  5.96 us
  transfers between devices with their start and end apart: 3, of which 3 were waited for; matrix products, arithmetic and copies ran while one was open for 0% of the time, Pallas kernels for 0%

profile of v1, /device:TPU:1, one launch (start us, length us, event | category | flops | bytes accessed | tf_op | source)
XLA Modules:
  0.0 181.9 jit_solution(2237153907328652105)
XLA Ops:
  0.6 0.0 copy-start
  0.6 0.0 copy-start.3
  0.7 2.1 %broadcast_in_dim.13 = bf16[32,128,128]{2,1,0:T(8,128)(2,1)} broadcast(bf16[128,128]{1,0:T(8,128)(2,1)} %bitcast.70), dimensions={1,2} | broadcast | bytes 1081344 | tf_op jit(solution)/shard_map/broadcast_in_dim | solution.py:49
  2.7 13.5 %all-to-all-start = ((bf16[32,128,128]{2,1,0:T(8,128)(2,1)}), bf16[32,128,128]{2,1,0:T(8,128)(2,1)S(1)}, u32[]{:S(2)}, u32[]{:S(2)}) async-start(bf16[32,128,128]{2,1,0:T(8,128)(2,1)} %broadcast_in_dim.13), calls=%async_computation | async-start | bytes 2097152 | tf_op jit(solution)/shard_map/all_to_all | solution.py:48
  16.9 0.0 copy-done.3
  16.9 25.2 %all-to-all-done = bf16[32,128,128]{2,1,0:T(8,128)(2,1)S(1)} async-done(((bf16[32,128,128]{2,1,0:T(8,128)(2,1)}), bf16[32,128,128]{2,1,0:T(8,128)(2,1)S(1)}, u32[]{:S(2)}, u32[]{:S(2)}) %all-to-all-start) | async-done | bytes 1048608 | tf_op jit(solution)/shard_map/all_to_all | solution.py:48
  42.1 1.7 gather_fusion
  43.7 0.0 copy-done
  43.7 2.1 %convolution_bitcast_fusion.1 = f32[32,128,128]{1,2,0:T(8,128)S(1)} fusion(bf16[32,128,128]{2,1,0:T(8,128)(2,1)} %gather_fusion, bf16[1,1,32,128,128]{4,3,2,1,0:T(8,128)(2,1)S(1)} %copy-done), kind=kOutput, calls=%fused_computation.3 | convolution fusion | flops 134217728 | bytes 4194304 | tf_op jit(solution)/shard_map/tij,tjf->tif/dot_general | solution.py:14
  45.8 0.0 copy-start.2
  45.8 2.0 %copy.33 = f32[32,128,128]{2,0,1:T(8,128)} copy(f32[32,128,128]{1,2,0:T(8,128)S(1)} %convolution_bitcast_fusion.1) | data formatting | bytes 4194304 | tf_op jit(solution)/shard_map/tij,tjf->tif/dot_general | solution.py:14
  47.9 0.0 copy-done.2
  47.9 0.0 copy-start.1
  47.9 0.0 copy-start.4
  47.9 2.1 %convolution_convert_fusion.1 = bf16[16,128,128]{2,0,1:T(8,128)(2,1)S(1)} fusion(f32[32,128,128]{2,0,1:T(8,128)} %copy.33, s32[32]{0:T(128)S(1)} %bitcast.72, pred[32]{0:T(512)(128)(4,1)S(1)} %iota_compare_fusion.2), kind=kOutput, calls=%fused_computation.5 | convolution fusion | flops 50594816 | bytes 2621600 | tf_op jit(solution)/shard_map/rt,tif->rif/dot_general | solution.py:23
  50.0 0.1 copy.34
  50.1 30.9 %all_to_all.26 = bf16[16,128,128]{2,1,0:T(8,128)(2,1)S(1)} all-to-all(bf16[16,128,128]{2,1,0:T(8,128)(2,1)S(1)} %copy.34), channel_id=1, replica_groups=mesh['row'=32,'col'=16] {'col'}, dimensions={0} | all-to-all | bytes 1048576 | tf_op jit(solution)/shard_map/all_to_all | solution.py:54
  81.0 0.1 reduce_sum.42
  81.1 0.1 copy.36
  81.2 0.0 copy-done.1
  81.2 0.0 copy-done.4
  81.2 0.8 fusion.2
  82.1 0.2 convolution_convert_fusion.2
  82.2 0.2 convert_bitcast_fusion
  82.5 0.1 broadcast_in_dim.15
  82.6 0.9 pad_maximum_fusion.1
  83.5 6.0 %all-to-all-start.2 = ((bf16[16,160,128]{2,1,0:T(8,128)(2,1)}), bf16[16,160,128]{2,1,0:T(8,128)(2,1)S(1)}, u32[]{:S(2)}, u32[]{:S(2)}) async-start(bf16[16,160,128]{2,1,0:T(8,128)(2,1)} %pad_maximum_fusion.1), calls=%async_computation.2 | async-start | bytes 1310720 | tf_op jit(solution)/shard_map/all_to_all | solution.py:75
  89.5 18.0 %all-to-all-done.2 = bf16[16,160,128]{2,1,0:T(8,128)(2,1)S(1)} async-done(((bf16[16,160,128]{2,1,0:T(8,128)(2,1)}), bf16[16,160,128]{2,1,0:T(8,128)(2,1)S(1)}, u32[]{:S(2)}, u32[]{:S(2)}) %all-to-all-start.2) | async-done | bytes 655392 | tf_op jit(solution)/shard_map/all_to_all | solution.py:75
  107.4 0.1 reshape.105
  107.6 0.2 fusion.3
  107.8 0.1 reshape.102
  107.9 0.7 gather_fusion.1
  108.7 1.9 %convolution_bitcast_fusion = f32[32,128,128]{1,2,0:T(8,128)} fusion(bf16[32,128,128]{2,1,0:T(8,128)(2,1)S(1)} %gather_fusion.1, bf16[1,1,32,128,128]{4,3,2,1,0:T(8,128)(2,1)S(1)} %copy-done), kind=kOutput, calls=%fused_computation.2 | convolution fusion | flops 134217728 | bytes 4194304 | tf_op jit(solution)/shard_map/tij,tif->tjf/dot_general | solution.py:10
  110.5 2.4 %copy.39 = f32[32,128,128]{2,0,1:T(8,128)S(1)} copy(f32[32,128,128]{1,2,0:T(8,128)} %convolution_bitcast_fusion) | data formatting | bytes 4194304 | tf_op jit(solution)/shard_map/tij,tif->tjf/dot_general | solution.py:10
  112.9 0.1 maximum_bitcast_fusion
  113.0 0.7 convolution_convert_fusion
  113.7 0.1 pad_maximum_fusion
  113.8 0.4 copy.40
  114.3 38.3 %all_to_all.27 = bf16[32,129,128]{2,1,0:T(8,128)(2,1)S(1)} all-to-all(bf16[32,129,128]{2,1,0:T(8,128)(2,1)S(1)} %copy.40), channel_id=1, replica_groups=mesh['row'=32,'col'=16] {'row'}, dimensions={0} | all-to-all | bytes 2113536 | tf_op jit(solution)/shard_map/all_to_all | solution.py:87
  152.6 0.1 fusion.9
  152.7 0.8 broadcast_in_dim.17
  153.5 9.9 %all-to-all-start.4 = ((f32[512,1,64]{2,1,0:T(1,128)}), f32[512,1,64]{2,1,0:T(1,128)S(1)}, u32[]{:S(2)}, u32[]{:S(2)}) async-start(f32[512,1,64]{2,1,0:T(1,128)} %broadcast_in_dim.17), calls=%async_computation.4 | async-start | bytes 524288 | tf_op jit(solution)/shard_map/all_to_all | solution.py:93
  163.5 0.8 slice_reduce_fusion
  164.2 16.8 %all-to-all-done.4 = f32[512,1,64]{2,1,0:T(1,128)S(1)} async-done(((f32[512,1,64]{2,1,0:T(1,128)}), f32[512,1,64]{2,1,0:T(1,128)S(1)}, u32[]{:S(2)}, u32[]{:S(2)}) %all-to-all-start.4) | async-done | bytes 131104 | tf_op jit(solution)/shard_map/all_to_all | solution.py:93
  181.0 0.1 copy.42
  181.1 0.8 mul.35
  (13 shorter events, 0.2 us)
Async XLA Ops:
  0.6 43.1 %copy-start = (bf16[1,1,32,128,128]{4,3,2,1,0:T(8,128)(2,1)S(1)}, bf16[1,1,32,128,128]{4,3,2,1,0:T(8,128)(2,1)}, u32[]{:S(2)}) copy-start(bf16[1,1,32,128,128]{4,3,2,1,0:T(8,128)(2,1)} %param.9) | copy-start | bytes 3145732
  0.6 16.2 %copy-start.3 = (s32[1,1,32]{2,1,0:T(1,128)S(1)}, s32[1,1,32]{2,1,0:T(1,128)}, u32[]{:S(2)}) copy-start(s32[1,1,32]{2,1,0:T(1,128)} %param.11) | copy-start | bytes 388
  2.7 39.3 %all-to-all-start = ((bf16[32,128,128]{2,1,0:T(8,128)(2,1)}), bf16[32,128,128]{2,1,0:T(8,128)(2,1)S(1)}, u32[]{:S(2)}, u32[]{:S(2)}) async-start(bf16[32,128,128]{2,1,0:T(8,128)(2,1)} %broadcast_in_dim.13), calls=%async_computation | async-start | bytes 2097152 | tf_op jit(solution)/shard_map/all_to_all | solution.py:48
  45.8 2.1 %copy-start.2 = (s32[1,1,32]{2,1,0:T(1,128)S(1)}, s32[1,1,32]{2,1,0:T(1,128)}, u32[]{:S(2)}) copy-start(s32[1,1,32]{2,1,0:T(1,128)} %param.10) | copy-start | bytes 388
  47.9 33.3 %copy-start.1 = (bf16[128,256]{1,0:T(8,128)(2,1)S(1)}, bf16[128,256]{1,0:T(8,128)(2,1)}, u32[]{:S(2)}) copy-start(bf16[128,256]{1,0:T(8,128)(2,1)} %param.8) | copy-start | bytes 196612
  47.9 33.4 %copy-start.4 = (bf16[1,128,256]{2,1,0:T(8,128)(2,1)S(1)}, bf16[1,128,256]{2,1,0:T(8,128)(2,1)}, u32[]{:S(2)}) copy-start(bf16[1,128,256]{2,1,0:T(8,128)(2,1)} %param.13) | copy-start | bytes 196612
  83.5 23.9 %all-to-all-start.2 = ((bf16[16,160,128]{2,1,0:T(8,128)(2,1)}), bf16[16,160,128]{2,1,0:T(8,128)(2,1)S(1)}, u32[]{:S(2)}, u32[]{:S(2)}) async-start(bf16[16,160,128]{2,1,0:T(8,128)(2,1)} %pad_maximum_fusion.1), calls=%async_computation.2 | async-start | bytes 1310720 | tf_op jit(solution)/shard_map/all_to_all | solution.py:75
  153.5 27.5 %all-to-all-start.4 = ((f32[512,1,64]{2,1,0:T(1,128)}), f32[512,1,64]{2,1,0:T(1,128)S(1)}, u32[]{:S(2)}, u32[]{:S(2)}) async-start(f32[512,1,64]{2,1,0:T(1,128)} %broadcast_in_dim.17), calls=%async_computation.4 | async-start | bytes 524288 | tf_op jit(solution)/shard_map/all_to_all | solution.py:93

commit v2 on v1

--- a/solution.py
+++ b/solution.py
@@ -1,26 +1,48 @@
+import functools
+
 import jax
 import jax.numpy as jnp
 from jax import lax
+from jax.experimental import pallas as pl
+from jax.experimental.pallas import tpu as pltpu
 from jax.sharding import PartitionSpec as P
 
 
-def tile_products(tile_block, target_ids, source_ids, tile_total, source, out_blocks, transpose):
-    source_blocks = source[source_ids]
-    if transpose:
-        products = jnp.einsum(
-            "tij,tif->tjf", tile_block, source_blocks, preferred_element_type=jnp.float32
-        )
-    else:
-        products = jnp.einsum(
-            "tij,tjf->tif", tile_block, source_blocks, preferred_element_type=jnp.float32
-        )
-    slot_ids = jnp.arange(tile_block.shape[0], dtype=jnp.int32)
-    live_mask = slot_ids < tile_total
-    one_hot = (
-        (target_ids[None, :] == jnp.arange(out_blocks, dtype=jnp.int32)[:, None])
-        & live_mask[None, :]
-    ).astype(jnp.float32)
-    return jnp.einsum("rt,tif->rif", one_hot, products, precision=lax.Precision.HIGH)
+def spread_kernel(transpose, rows_ref, cols_ref, count_ref, tiles_ref, src_ref, out_ref, acc_ref):
+    acc_ref[...] = jnp.zeros_like(acc_ref)
+    live = jnp.minimum(count_ref[0], tiles_ref.shape[0])
+
+    def body(t, carry):
+        target = rows_ref[t]
+        source = cols_ref[t]
+        tile = tiles_ref[t]
+        if transpose:
+            term = lax.dot_general(tile, src_ref[source], (((0,), (0,)), ((), ())),
+                                   preferred_element_type=jnp.float32)
+        else:
+            term = jnp.dot(tile, src_ref[source], preferred_element_type=jnp.float32)
+        acc_ref[target] += term
+        return carry
+
+    lax.fori_loop(0, live, body, 0)
+    out_ref[...] = acc_ref[...].astype(out_ref.dtype)
+
+
+def spread(tiles, target_ids, source_ids, count, source, out_blocks, transpose, out_dtype):
+    slots, tb, _ = tiles.shape
+    width = source.shape[-1]
+    smem = pl.BlockSpec(memory_space=pltpu.SMEM)
+    vmem = pl.BlockSpec(memory_space=pltpu.VMEM)
+    return pl.pallas_call(
+        functools.partial(spread_kernel, transpose),
+        out_shape=jax.ShapeDtypeStruct((out_blocks, tb, width), out_dtype),
+        in_specs=[smem, smem, smem, vmem, vmem],
+        out_specs=vmem,
+        scratch_shapes=[pltpu.VMEM((out_blocks, tb, width), jnp.float32)],
+        cost_estimate=pl.CostEstimate(
+            flops=2 * slots * tb * tb * width, transcendentals=0,
+            bytes_accessed=tiles.size * 2 + source.size * 2 + out_blocks * tb * width * 2),
+    )(target_ids, source_ids, count.reshape(1), tiles, source)
 
 
 def split_f32(x):
@@ -49,8 +71,8 @@
         jnp.broadcast_to(own[None], (n_row,) + own.shape), "row", 0, 0, tiled=False
     )
     col_source = gathered.reshape(col_tiles, tile_size, width_in)
-    partial_value = tile_products(tile_block, row_ids, col_ids, tile_total, col_source, row_tiles, False)
-    sent = partial_value.reshape(n_col, rows_dev, width_in).astype(jnp.bfloat16)
+    partial_value = spread(tile_block, row_ids, col_ids, tile_total, col_source, row_tiles, False, jnp.bfloat16)
+    sent = partial_value.reshape(n_col, rows_dev, width_in)
     got = lax.all_to_all(sent, "col", 0, 0, tiled=False)
     aggregated = got.astype(jnp.float32).sum(0).astype(jnp.bfloat16)
 
@@ -77,12 +99,12 @@
     wg_got = got[:, rows_dev:].reshape(n_col, 2, wg_rows * width_out).astype(jnp.float32)
     wg_col = (wg_got[:, 0] + wg_got[:, 1]).sum(0)
 
-    partial_back = tile_products(tile_block, col_ids, row_ids, tile_total, row_source, col_tiles, True)
+    partial_back = spread(tile_block, col_ids, row_ids, tile_total, row_source, col_tiles, True, jnp.bfloat16)
     piece = wg_col.shape[0] // n_row
     hi, lo = split_f32(wg_col.reshape(n_row, piece))
     wg_words = jnp.concatenate([hi, lo], axis=1).reshape(n_row, 1, 2 * piece)
     payload = jnp.concatenate(
-        [partial_back.reshape(n_row, rows_dev, width_in).astype(jnp.bfloat16), wg_words], axis=1
+        [partial_back.reshape(n_row, rows_dev, width_in), wg_words], axis=1
     )
     got = lax.all_to_all(payload, "row", 0, 0, tiled=False)
     grad_features = got[:, :rows_dev].astype(jnp.float32).sum(0).astype(jnp.bfloat16)[None]

time: 182 us -> 183 us (level)
  blocking collectives: 69.2 us -> 93.1 us
  waiting for transfers between devices: 59.9 us -> 41.9 us
  Pallas kernels: 0 us -> 10.3 us
  matrix products: 7.97 us -> 1.15 us
  local copies, waits for them, and re-layouts: 11.7 us -> 6.07 us
  starting transfers between devices: 29.4 us -> 26.3 us
    all_to_all x0 -> x1, blocking collectives: none -> 23.1 us  [on_device(): got = lax.all_to_all(payload, 'col', 0, 0, tiled=False)]
    all_to_all x1 -> x0, waiting for transfers between devices: 18 us -> none  [on_device(): got = lax.all_to_all(payload, 'col', 0, 0, tiled=False)]
    pallas_call x0 -> x2, Pallas kernels: none -> 10.3 us  [spread(): pl.pallas_call(functools.partial(spread_kernel, transpose), out_shape=jax...]
    dot_general x4 -> x0, matrix products: 6.82 us -> none  [the longest x2 2.86 us: tile_products(): jnp.einsum('rt,tif->rif', one_hot, products, precision=lax.Precision.HIGH)]
    all_to_all x1 -> x0, starting transfers between devices: 5.96 us -> none  [on_device(): got = lax.all_to_all(payload, 'col', 0, 0, tiled=False)]
    dot_general x2 -> x0, local copies, waits for them, and re-layouts: 4.42 us -> none  [the longest x1 2.37 us: tile_products(): jnp.einsum('tij,tif->tjf', tile_block, source_blocks, preferred_element_t...]
    all_to_all x1, starting transfers between devices: 9.94 us -> 12.8 us  [on_device(): lax.all_to_all(jnp.broadcast_to(wg_piece[None], (n_all, piece)), ('row',...]
    gather x2 -> x0, local copies, waits for them, and re-layouts: 2.4 us -> none  [tile_products(): source_blocks = source[source_ids]]
  transfers between devices with their start and end apart: 3 -> 2, of which waited for: 3 -> 2; matrix products, arithmetic and copies ran while one was open for 0% -> 0% of each run, Pallas kernels for 0% -> 0%
where the time goes in v2:
time: 183 us
  blocking collectives  93.1 us (51%)
  waiting for transfers between devices  41.9 us (23%)
  starting transfers between devices  26.3 us (14%)
  Pallas kernels  10.3 us (6%)
  local copies, waits for them, and re-layouts  6.07 us (3%)
  other arithmetic  2.64 us (1%)
    all_to_all x1, blocking collectives, on_device(): got = lax.all_to_all(payload, 'row', 0, 0, tiled=False)  39 us
    all_to_all x1, blocking collectives, on_device(): got = lax.all_to_all(sent, 'col', 0, 0, tiled=False)  31 us
    all_to_all x1, waiting for transfers between devices, on_device(): lax.all_to_all(jnp.broadcast_to(own[None], (n_row,) + own.shape), 'row',...  25.2 us
    all_to_all x1, blocking collectives, on_device(): got = lax.all_to_all(payload, 'col', 0, 0, tiled=False)  23.1 us
    all_to_all x1, waiting for transfers between devices, on_device(): lax.all_to_all(jnp.broadcast_to(wg_piece[None], (n_all, piece)), ('row',...  16.7 us
    all_to_all x1, starting transfers between devices, on_device(): lax.all_to_all(jnp.broadcast_to(own[None], (n_row,) + own.shape), 'row',...  13.5 us
    all_to_all x1, starting transfers between devices, on_device(): lax.all_to_all(jnp.broadcast_to(wg_piece[None], (n_all, piece)), ('row',...  12.8 us
    pallas_call x2, Pallas kernels, spread(): pl.pallas_call(functools.partial(spread_kernel, transpose), out_shape=jax...  10.3 us
  transfers between devices with their start and end apart: 2, of which 2 were waited for; matrix products, arithmetic and copies ran while one was open for 0% of the time, Pallas kernels for 0%

profile of v2, /device:TPU:1, one launch (start us, length us, event | category | flops | bytes accessed | tf_op | source)
XLA Modules:
  0.0 182.9 jit_solution(1732815884292257257)
XLA Ops:
  0.6 0.0 copy-start
  0.6 2.0 %broadcast_in_dim.26 = bf16[32,128,128]{2,1,0:T(8,128)(2,1)} broadcast(bf16[128,128]{1,0:T(8,128)(2,1)} %bitcast.47), dimensions={1,2} | broadcast | bytes 1081344 | tf_op jit(solution)/shard_map/broadcast_in_dim | solution.py:71
  2.7 13.5 %all-to-all-start = ((bf16[32,128,128]{2,1,0:T(8,128)(2,1)}), bf16[32,128,128]{2,1,0:T(8,128)(2,1)S(1)}, u32[]{:S(2)}, u32[]{:S(2)}) async-start(bf16[32,128,128]{2,1,0:T(8,128)(2,1)} %broadcast_in_dim.26), calls=%async_computation | async-start | bytes 2097152 | tf_op jit(solution)/shard_map/all_to_all | solution.py:70
  16.8 25.2 %all-to-all-done.src_ref = bf16[32,128,128]{2,1,0:T(8,128)(2,1)S(1)} async-done(((bf16[32,128,128]{2,1,0:T(8,128)(2,1)}), bf16[32,128,128]{2,1,0:T(8,128)(2,1)S(1)}, u32[]{:S(2)}, u32[]{:S(2)}) %all-to-all-start) | async-done | bytes 1048608 | tf_op jit(solution)/shard_map/all_to_all | solution.py:70
  42.0 0.0 copy-start.1
  42.0 1.0 copy-done.1
  43.0 4.7 %shard_map.94 = bf16[16,128,128]{2,1,0:T(8,128)(2,1)} custom-call(s32[32]{0:T(128)} %bitcast.49, s32[32]{0:T(128)} %bitcast.51, s32[1]{0:T(128)} %bitcast.39.count_ref, bf16[32,128,128]{2,1,0:T(8,128)(2,1)} %bitcast.41, bf16[32,128,128]{2,1,0:T(8,128)(2,1)} %copy-done.1), custom_call_target="tpu_custom_call" | custom-call | flops 134217728 | bytes 2621440 | tf_op jit(solution)/shard_map/pallas_call | solution.py:36
  47.7 0.0 copy-start.2
  47.7 31.0 %all_to_all.26 = bf16[16,128,128]{2,1,0:T(8,128)(2,1)S(1)} all-to-all(bf16[16,128,128]{2,1,0:T(8,128)(2,1)} %shard_map.94), channel_id=1, replica_groups=mesh['row'=32,'col'=16] {'col'}, dimensions={0} | all-to-all | bytes 1048576 | tf_op jit(solution)/shard_map/all_to_all | solution.py:76
  78.7 0.1 reduce_sum.42
  78.8 0.1 copy.21
  78.9 0.0 copy-done
  78.9 0.0 copy-done.2
  78.9 0.8 fusion
  79.8 0.2 convolution_convert_fusion
  79.9 0.2 convert_bitcast_fusion
  80.2 0.1 broadcast_in_dim.28
  80.3 23.1 %all_to_all.27 = bf16[16,160,128]{2,1,0:T(8,128)(2,1)S(1)} all-to-all(bf16[16,160,128]{2,1,0:T(8,128)(2,1)S(1)} %pad_maximum_fusion.1), channel_id=1, replica_groups=mesh['row'=32,'col'=16] {'col'}, dimensions={0} | all-to-all | bytes 1310720 | tf_op jit(solution)/shard_map/all_to_all | solution.py:97
  103.4 0.1 reshape.43
  103.6 0.2 fusion.1
  103.8 0.1 reshape.40
  103.9 0.1 maximum_bitcast_fusion
  104.0 0.9 slice.32.src_ref
  104.8 5.6 %shard_map.95 = bf16[32,128,128]{2,1,0:T(8,128)(2,1)} custom-call(s32[32]{0:T(128)} %bitcast.52, s32[32]{0:T(128)} %bitcast.50, s32[1]{0:T(128)} %bitcast.40.count_ref, bf16[32,128,128]{2,1,0:T(8,128)(2,1)} %bitcast.42, bf16[16,128,128]{2,1,0:T(8,128)(2,1)} %slice.32.src_ref), custom_call_target="tpu_custom_call" | custom-call | flops 134217728 | bytes 2621440 | tf_op jit(solution)/shard_map/pallas_call | solution.py:36
  110.4 1.3 pad_maximum_fusion
  111.7 39.0 %all_to_all.28 = bf16[32,129,128]{2,1,0:T(8,128)(2,1)S(1)} all-to-all(bf16[32,129,128]{2,1,0:T(8,128)(2,1)S(1)} %pad_maximum_fusion), channel_id=1, replica_groups=mesh['row'=32,'col'=16] {'row'}, dimensions={0} | all-to-all | bytes 2113536 | tf_op jit(solution)/shard_map/all_to_all | solution.py:109
  150.8 0.1 fusion.7
  150.9 0.8 broadcast_in_dim.30
  151.7 12.8 %all-to-all-start.4 = ((f32[512,1,64]{2,1,0:T(1,128)}), f32[512,1,64]{2,1,0:T(1,128)S(1)}, u32[]{:S(2)}, u32[]{:S(2)}) async-start(f32[512,1,64]{2,1,0:T(1,128)} %broadcast_in_dim.30), calls=%async_computation.4 | async-start | bytes 524288 | tf_op jit(solution)/shard_map/all_to_all | solution.py:115
  164.5 0.8 slice_reduce_fusion
  165.3 16.7 %all-to-all-done.4 = f32[512,1,64]{2,1,0:T(1,128)S(1)} async-done(((f32[512,1,64]{2,1,0:T(1,128)}), f32[512,1,64]{2,1,0:T(1,128)S(1)}, u32[]{:S(2)}, u32[]{:S(2)}) %all-to-all-start.4) | async-done | bytes 131104 | tf_op jit(solution)/shard_map/all_to_all | solution.py:115
  182.0 0.1 copy.25
  182.1 0.8 mul.35
  (9 shorter events, 0.2 us)
Async XLA Ops:
  0.6 78.3 %copy-start = (bf16[128,256]{1,0:T(8,128)(2,1)S(1)}, bf16[128,256]{1,0:T(8,128)(2,1)}, u32[]{:S(2)}) copy-start(bf16[128,256]{1,0:T(8,128)(2,1)} %param.8) | copy-start | bytes 196612
  2.7 39.3 %all-to-all-start = ((bf16[32,128,128]{2,1,0:T(8,128)(2,1)}), bf16[32,128,128]{2,1,0:T(8,128)(2,1)S(1)}, u32[]{:S(2)}, u32[]{:S(2)}) async-start(bf16[32,128,128]{2,1,0:T(8,128)(2,1)} %broadcast_in_dim.26), calls=%async_computation | async-start | bytes 2097152 | tf_op jit(solution)/shard_map/all_to_all | solution.py:70
  42.0 1.0 copy-start.1
  47.7 31.2 %copy-start.2 = (bf16[1,128,256]{2,1,0:T(8,128)(2,1)S(1)}, bf16[1,128,256]{2,1,0:T(8,128)(2,1)}, u32[]{:S(2)}) copy-start(bf16[1,128,256]{2,1,0:T(8,128)(2,1)} %param.13) | copy-start | bytes 196612
  151.7 30.3 %all-to-all-start.4 = ((f32[512,1,64]{2,1,0:T(1,128)}), f32[512,1,64]{2,1,0:T(1,128)S(1)}, u32[]{:S(2)}, u32[]{:S(2)}) async-start(f32[512,1,64]{2,1,0:T(1,128)} %broadcast_in_dim.30), calls=%async_computation.4 | async-start | bytes 524288 | tf_op jit(solution)/shard_map/all_to_all | solution.py:115

commit v3 on v2

--- a/solution.py
+++ b/solution.py
@@ -8,41 +8,51 @@
 from jax.sharding import PartitionSpec as P
 
 
-def spread_kernel(transpose, rows_ref, cols_ref, count_ref, tiles_ref, src_ref, out_ref, acc_ref):
+def spread_kernel(transpose, rows_ref, cols_ref, count_ref, tiles_ref, src_ref, *rest):
+    if len(rest) == 3:
+        extra_ref, out_ref, acc_ref = rest
+    else:
+        extra_ref = None
+        out_ref, acc_ref = rest
+    tb = tiles_ref.shape[1]
     acc_ref[...] = jnp.zeros_like(acc_ref)
-    live = jnp.minimum(count_ref[0], tiles_ref.shape[0])
-
-    def body(t, carry):
-        target = rows_ref[t]
-        source = cols_ref[t]
+    live = count_ref[0]
+    for t in range(tiles_ref.shape[0]):
         tile = tiles_ref[t]
+        src = src_ref[cols_ref[t]]
         if transpose:
-            term = lax.dot_general(tile, src_ref[source], (((0,), (0,)), ((), ())),
+            term = lax.dot_general(tile, src, (((0,), (0,)), ((), ())),
                                    preferred_element_type=jnp.float32)
         else:
-            term = jnp.dot(tile, src_ref[source], preferred_element_type=jnp.float32)
-        acc_ref[target] += term
-        return carry
-
-    lax.fori_loop(0, live, body, 0)
-    out_ref[...] = acc_ref[...].astype(out_ref.dtype)
+            term = jnp.dot(tile, src, preferred_element_type=jnp.float32)
+        acc_ref[rows_ref[t]] += jnp.where(t < live, term, 0.0)
+    if extra_ref is None:
+        out_ref[...] = acc_ref[...].astype(out_ref.dtype)
+    else:
+        out_ref[:, :tb, :] = acc_ref[...].astype(out_ref.dtype)
+        out_ref[:, tb:, :] = extra_ref[...]
 
 
-def spread(tiles, target_ids, source_ids, count, source, out_blocks, transpose, out_dtype):
+def spread(tiles, target_ids, source_ids, count, source, out_blocks, transpose, out_dtype, extra=None):
     slots, tb, _ = tiles.shape
     width = source.shape[-1]
     smem = pl.BlockSpec(memory_space=pltpu.SMEM)
     vmem = pl.BlockSpec(memory_space=pltpu.VMEM)
+    args = [target_ids, source_ids, count.reshape(1), tiles, source]
+    out_rows = tb
+    if extra is not None:
+        args.append(extra)
+        out_rows += extra.shape[1]
     return pl.pallas_call(
         functools.partial(spread_kernel, transpose),
-        out_shape=jax.ShapeDtypeStruct((out_blocks, tb, width), out_dtype),
-        in_specs=[smem, smem, smem, vmem, vmem],
+        out_shape=jax.ShapeDtypeStruct((out_blocks, out_rows, width), out_dtype),
+        in_specs=[smem, smem, smem] + [vmem] * (len(args) - 3),
         out_specs=vmem,
         scratch_shapes=[pltpu.VMEM((out_blocks, tb, width), jnp.float32)],
         cost_estimate=pl.CostEstimate(
             flops=2 * slots * tb * tb * width, transcendentals=0,
-            bytes_accessed=tiles.size * 2 + source.size * 2 + out_blocks * tb * width * 2),
-    )(target_ids, source_ids, count.reshape(1), tiles, source)
+            bytes_accessed=tiles.size * 2 + source.size * 2 + out_blocks * out_rows * width * 2),
+    )(*args)
 
 
 def split_f32(x):
@@ -99,16 +109,17 @@
     wg_got = got[:, rows_dev:].reshape(n_col, 2, wg_rows * width_out).astype(jnp.float32)
     wg_col = (wg_got[:, 0] + wg_got[:, 1]).sum(0)
 
-    partial_back = spread(tile_block, col_ids, row_ids, tile_total, row_source, col_tiles, True, jnp.bfloat16)
     piece = wg_col.shape[0] // n_row
     hi, lo = split_f32(wg_col.reshape(n_row, piece))
-    wg_words = jnp.concatenate([hi, lo], axis=1).reshape(n_row, 1, 2 * piece)
-    payload = jnp.concatenate(
-        [partial_back.reshape(n_row, rows_dev, width_in), wg_words], axis=1
+    wg_words = jnp.concatenate([hi, lo], axis=1).reshape(n_row, -1, width_in)
+    pad_rows = 16 - wg_words.shape[1] % 16
+    wg_words = jnp.pad(wg_words, ((0, 0), (0, pad_rows), (0, 0)))
+    payload = spread(
+        tile_block, col_ids, row_ids, tile_total, row_source, col_tiles, True, jnp.bfloat16, wg_words
     )
     got = lax.all_to_all(payload, "row", 0, 0, tiled=False)
     grad_features = got[:, :rows_dev].astype(jnp.float32).sum(0).astype(jnp.bfloat16)[None]
-    wg_got = got[:, rows_dev].astype(jnp.float32)
+    wg_got = got[:, rows_dev:].reshape(n_row, -1)[:, : 2 * piece].astype(jnp.float32)
     wg_piece = (wg_got[:, :piece] + wg_got[:, piece:]).sum(0)
 
     n_all = n_row * n_col

time: 183 us -> 177 us (0.967)
  Pallas kernels: 10.3 us -> 6.01 us
  starting transfers between devices: 26.3 us -> 24 us
    pallas_call x2, Pallas kernels: 10.3 us -> 6.01 us  [spread(): pl.pallas_call(functools.partial(spread_kernel, transpose), out_shape=jax...]
    all_to_all x1, starting transfers between devices: 12.8 us -> 10.5 us  [on_device(): lax.all_to_all(jnp.broadcast_to(wg_piece[None], (n_all, piece)), ('row',...]
where the time goes in v3:
time: 177 us
  blocking collectives  93.8 us (53%)
  waiting for transfers between devices  41.9 us (24%)
  starting transfers between devices  24 us (14%)
  local copies, waits for them, and re-layouts  6.8 us (4%)
  Pallas kernels  6.01 us (3%)
    all_to_all x1, blocking collectives, on_device(): got = lax.all_to_all(payload, 'row', 0, 0, tiled=False)  39.6 us
    all_to_all x1, blocking collectives, on_device(): got = lax.all_to_all(sent, 'col', 0, 0, tiled=False)  31.2 us
    all_to_all x1, waiting for transfers between devices, on_device(): lax.all_to_all(jnp.broadcast_to(own[None], (n_row,) + own.shape), 'row',...  25.2 us
    all_to_all x1, blocking collectives, on_device(): got = lax.all_to_all(payload, 'col', 0, 0, tiled=False)  23.1 us
    all_to_all x1, waiting for transfers between devices, on_device(): lax.all_to_all(jnp.broadcast_to(wg_piece[None], (n_all, piece)), ('row',...  16.7 us
    all_to_all x1, starting transfers between devices, on_device(): lax.all_to_all(jnp.broadcast_to(own[None], (n_row,) + own.shape), 'row',...  13.5 us
    all_to_all x1, starting transfers between devices, on_device(): lax.all_to_all(jnp.broadcast_to(wg_piece[None], (n_all, piece)), ('row',...  10.5 us
    pallas_call x2, Pallas kernels, spread(): pl.pallas_call(functools.partial(spread_kernel, transpose), out_shape=jax...  6.01 us
  transfers between devices with their start and end apart: 2, of which 2 were waited for; matrix products, arithmetic and copies ran while one was open for 0% of the time, Pallas kernels for 0%

profile of v3, /device:TPU:1, one launch (start us, length us, event | category | flops | bytes accessed | tf_op | source)
XLA Modules:
  0.0 176.5 jit_solution(7758290787836046116)
XLA Ops:
  0.6 0.0 copy-start
  0.6 2.0 %broadcast_in_dim.26 = bf16[32,128,128]{2,1,0:T(8,128)(2,1)} broadcast(bf16[128,128]{1,0:T(8,128)(2,1)} %bitcast.51), dimensions={1,2} | broadcast | bytes 1081344 | tf_op jit(solution)/shard_map/broadcast_in_dim | solution.py:81
  2.7 13.5 %all-to-all-start = ((bf16[32,128,128]{2,1,0:T(8,128)(2,1)}), bf16[32,128,128]{2,1,0:T(8,128)(2,1)S(1)}, u32[]{:S(2)}, u32[]{:S(2)}) async-start(bf16[32,128,128]{2,1,0:T(8,128)(2,1)} %broadcast_in_dim.26), calls=%async_computation | async-start | bytes 2097152 | tf_op jit(solution)/shard_map/all_to_all | solution.py:80
  16.8 25.2 %all-to-all-done.src_ref = bf16[32,128,128]{2,1,0:T(8,128)(2,1)S(1)} async-done(((bf16[32,128,128]{2,1,0:T(8,128)(2,1)}), bf16[32,128,128]{2,1,0:T(8,128)(2,1)S(1)}, u32[]{:S(2)}, u32[]{:S(2)}) %all-to-all-start) | async-done | bytes 1048608 | tf_op jit(solution)/shard_map/all_to_all | solution.py:80
  42.0 0.0 copy-start.1
  42.0 1.0 copy-done.1
  43.0 2.9 %shard_map.94 = bf16[16,128,128]{2,1,0:T(8,128)(2,1)} custom-call(s32[32]{0:T(128)} %bitcast.53, s32[32]{0:T(128)} %bitcast.55, s32[1]{0:T(128)} %bitcast.42.count_ref, bf16[32,128,128]{2,1,0:T(8,128)(2,1)} %bitcast.44, bf16[32,128,128]{2,1,0:T(8,128)(2,1)} %copy-done.1), custom_call_target="tpu_custom_call" | custom-call | flops 134217728 | bytes 2621440 | tf_op jit(solution)/shard_map/pallas_call | solution.py:46
  45.9 0.0 copy-start.2
  45.9 31.2 %all_to_all.26 = bf16[16,128,128]{2,1,0:T(8,128)(2,1)S(1)} all-to-all(bf16[16,128,128]{2,1,0:T(8,128)(2,1)} %shard_map.94), channel_id=1, replica_groups=mesh['row'=32,'col'=16] {'col'}, dimensions={0} | all-to-all | bytes 1048576 | tf_op jit(solution)/shard_map/all_to_all | solution.py:86
  77.1 0.1 reduce_sum.42
  77.2 0.1 copy.21
  77.3 0.0 copy-done
  77.3 0.0 copy-done.2
  77.3 0.8 fusion
  78.1 0.2 convolution_convert_fusion
  78.3 0.2 convert_bitcast_fusion
  78.6 0.1 broadcast_in_dim.28
  78.7 23.1 %all_to_all.27 = bf16[16,160,128]{2,1,0:T(8,128)(2,1)S(1)} all-to-all(bf16[16,160,128]{2,1,0:T(8,128)(2,1)S(1)} %pad_maximum_fusion), channel_id=1, replica_groups=mesh['row'=32,'col'=16] {'col'}, dimensions={0} | all-to-all | bytes 1310720 | tf_op jit(solution)/shard_map/all_to_all | solution.py:107
  101.8 0.1 reshape.45
  102.0 0.2 fusion.1
  102.1 0.1 reshape.41
  102.2 0.1 maximum_bitcast_fusion
  102.3 0.7 pad.4.rest_0_
  103.0 0.9 slice.36.src_ref
  103.9 3.1 %shard_map.95 = bf16[32,144,128]{2,1,0:T(8,128)(2,1)} custom-call(s32[32]{0:T(128)} %bitcast.56, s32[32]{0:T(128)} %bitcast.54, s32[1]{0:T(128)} %bitcast.43.count_ref, bf16[32,128,128]{2,1,0:T(8,128)(2,1)} %bitcast.45, bf16[16,128,128]{2,1,0:T(8,128)(2,1)} %slice.36.src_ref, bf16[32,16,128]{2,1,0:T(8,128)(2,1)} %pad.4.rest_0_), custom_call_target="tpu_custom_call" | custom-call | flops 134217728 | bytes 2752512 | tf_op jit(solution)/shard_map/pallas_call | solution.py:46
  107.0 39.6 %all_to_all.28 = bf16[32,144,128]{2,1,0:T(8,128)(2,1)S(1)} all-to-all(bf16[32,144,128]{2,1,0:T(8,128)(2,1)} %shard_map.95), channel_id=1, replica_groups=mesh['row'=32,'col'=16] {'row'}, dimensions={0} | all-to-all | bytes 2359296 | tf_op jit(solution)/shard_map/all_to_all | solution.py:120
  146.6 0.1 fusion.7
  146.7 0.8 broadcast_in_dim.30
  147.6 10.5 %all-to-all-start.4 = ((f32[512,1,64]{2,1,0:T(1,128)}), f32[512,1,64]{2,1,0:T(1,128)S(1)}, u32[]{:S(2)}, u32[]{:S(2)}) async-start(f32[512,1,64]{2,1,0:T(1,128)} %broadcast_in_dim.30), calls=%async_computation.4 | async-start | bytes 524288 | tf_op jit(solution)/shard_map/all_to_all | solution.py:126
  158.1 0.8 slice_reduce_fusion
  158.9 16.7 %all-to-all-done.4 = f32[512,1,64]{2,1,0:T(1,128)S(1)} async-done(((f32[512,1,64]{2,1,0:T(1,128)}), f32[512,1,64]{2,1,0:T(1,128)S(1)}, u32[]{:S(2)}, u32[]{:S(2)}) %all-to-all-start.4) | async-done | bytes 131104 | tf_op jit(solution)/shard_map/all_to_all | solution.py:126
  175.6 0.1 copy.25
  175.7 0.8 mul.35
  (11 shorter events, 0.2 us)
Async XLA Ops:
  0.6 76.7 %copy-start = (bf16[128,256]{1,0:T(8,128)(2,1)S(1)}, bf16[128,256]{1,0:T(8,128)(2,1)}, u32[]{:S(2)}) copy-start(bf16[128,256]{1,0:T(8,128)(2,1)} %param.8) | copy-start | bytes 196612
  2.7 39.3 %all-to-all-start = ((bf16[32,128,128]{2,1,0:T(8,128)(2,1)}), bf16[32,128,128]{2,1,0:T(8,128)(2,1)S(1)}, u32[]{:S(2)}, u32[]{:S(2)}) async-start(bf16[32,128,128]{2,1,0:T(8,128)(2,1)} %broadcast_in_dim.26), calls=%async_computation | async-start | bytes 2097152 | tf_op jit(solution)/shard_map/all_to_all | solution.py:80
  42.0 1.0 copy-start.1
  45.9 31.4 %copy-start.2 = (bf16[1,128,256]{2,1,0:T(8,128)(2,1)S(1)}, bf16[1,128,256]{2,1,0:T(8,128)(2,1)}, u32[]{:S(2)}) copy-start(bf16[1,128,256]{2,1,0:T(8,128)(2,1)} %param.13) | copy-start | bytes 196612
  147.6 28.0 %all-to-all-start.4 = ((f32[512,1,64]{2,1,0:T(1,128)}), f32[512,1,64]{2,1,0:T(1,128)S(1)}, u32[]{:S(2)}, u32[]{:S(2)}) async-start(f32[512,1,64]{2,1,0:T(1,128)} %broadcast_in_dim.30), calls=%async_computation.4 | async-start | bytes 524288 | tf_op jit(solution)/shard_map/all_to_all | solution.py:126

commit v4 on v3

--- a/solution.py
+++ b/solution.py
@@ -19,7 +19,7 @@
     live = count_ref[0]
     for t in range(tiles_ref.shape[0]):
         tile = tiles_ref[t]
-        src = src_ref[cols_ref[t]]
+        src = src_ref[cols_ref[t], :tb, :]
         if transpose:
             term = lax.dot_general(tile, src, (((0,), (0,)), ((), ())),
                                    preferred_element_type=jnp.float32)
@@ -30,7 +30,10 @@
         out_ref[...] = acc_ref[...].astype(out_ref.dtype)
     else:
         out_ref[:, :tb, :] = acc_ref[...].astype(out_ref.dtype)
-        out_ref[:, tb:, :] = extra_ref[...]
+        words = extra_ref.shape[1]
+        out_ref[:, tb:tb + words, :] = extra_ref[...]
+        out_ref[:, tb + words:, :] = jnp.zeros(
+            (out_ref.shape[0], out_ref.shape[1] - tb - words, out_ref.shape[2]), out_ref.dtype)
 
 
 def spread(tiles, target_ids, source_ids, count, source, out_blocks, transpose, out_dtype, extra=None):
@@ -42,7 +45,7 @@
     out_rows = tb
     if extra is not None:
         args.append(extra)
-        out_rows += extra.shape[1]
+        out_rows += -(-extra.shape[1] // 16) * 16
     return pl.pallas_call(
         functools.partial(spread_kernel, transpose),
         out_shape=jax.ShapeDtypeStruct((out_blocks, out_rows, width), out_dtype),
@@ -105,15 +108,13 @@
         [jnp.broadcast_to(grad_agg[None], (n_col,) + grad_agg.shape), wg_words], axis=1
     )
     got = lax.all_to_all(payload, "col", 0, 0, tiled=False)
-    row_source = got[:, :rows_dev].reshape(row_tiles, tile_size, width_in)
+    row_source = got
     wg_got = got[:, rows_dev:].reshape(n_col, 2, wg_rows * width_out).astype(jnp.float32)
     wg_col = (wg_got[:, 0] + wg_got[:, 1]).sum(0)
 
     piece = wg_col.shape[0] // n_row
     hi, lo = split_f32(wg_col.reshape(n_row, piece))
     wg_words = jnp.concatenate([hi, lo], axis=1).reshape(n_row, -1, width_in)
-    pad_rows = 16 - wg_words.shape[1] % 16
-    wg_words = jnp.pad(wg_words, ((0, 0), (0, pad_rows), (0, 0)))
     payload = spread(
         tile_block, col_ids, row_ids, tile_total, row_source, col_tiles, True, jnp.bfloat16, wg_words
     )

time: 177 us -> 176 us (level)
  no operation moved by 1% of the time
where the time goes in v4:
time: 176 us
  blocking collectives  93.8 us (53%)
  waiting for transfers between devices  41.9 us (24%)
  starting transfers between devices  24 us (14%)
  Pallas kernels  6.08 us (3%)
  local copies, waits for them, and re-layouts  5.86 us (3%)
    all_to_all x1, blocking collectives, on_device(): got = lax.all_to_all(payload, 'row', 0, 0, tiled=False)  39.6 us
    all_to_all x1, blocking collectives, on_device(): got = lax.all_to_all(sent, 'col', 0, 0, tiled=False)  31.2 us
    all_to_all x1, waiting for transfers between devices, on_device(): lax.all_to_all(jnp.broadcast_to(own[None], (n_row,) + own.shape), 'row',...  25.2 us
    all_to_all x1, blocking collectives, on_device(): got = lax.all_to_all(payload, 'col', 0, 0, tiled=False)  23.1 us
    all_to_all x1, waiting for transfers between devices, on_device(): lax.all_to_all(jnp.broadcast_to(wg_piece[None], (n_all, piece)), ('row',...  16.7 us
    all_to_all x1, starting transfers between devices, on_device(): lax.all_to_all(jnp.broadcast_to(own[None], (n_row,) + own.shape), 'row',...  13.5 us
    all_to_all x1, starting transfers between devices, on_device(): lax.all_to_all(jnp.broadcast_to(wg_piece[None], (n_all, piece)), ('row',...  10.6 us
    pallas_call x2, Pallas kernels, spread(): pl.pallas_call(functools.partial(spread_kernel, transpose), out_shape=jax...  6.08 us
  transfers between devices with their start and end apart: 2, of which 2 were waited for; matrix products, arithmetic and copies ran while one was open for 0% of the time, Pallas kernels for 0%

profile of v4, /device:TPU:1, one launch (start us, length us, event | category | flops | bytes accessed | tf_op | source)
XLA Modules:
  0.0 175.7 jit_solution(9161701965179486850)
XLA Ops:
  0.6 0.0 copy-start
  0.6 2.0 %broadcast_in_dim.26 = bf16[32,128,128]{2,1,0:T(8,128)(2,1)} broadcast(bf16[128,128]{1,0:T(8,128)(2,1)} %bitcast.51), dimensions={1,2} | broadcast | bytes 1081344 | tf_op jit(solution)/shard_map/broadcast_in_dim | solution.py:84
  2.7 13.5 %all-to-all-start = ((bf16[32,128,128]{2,1,0:T(8,128)(2,1)}), bf16[32,128,128]{2,1,0:T(8,128)(2,1)S(1)}, u32[]{:S(2)}, u32[]{:S(2)}) async-start(bf16[32,128,128]{2,1,0:T(8,128)(2,1)} %broadcast_in_dim.26), calls=%async_computation | async-start | bytes 2097152 | tf_op jit(solution)/shard_map/all_to_all | solution.py:83
  16.8 25.2 %all-to-all-done.src_ref = bf16[32,128,128]{2,1,0:T(8,128)(2,1)S(1)} async-done(((bf16[32,128,128]{2,1,0:T(8,128)(2,1)}), bf16[32,128,128]{2,1,0:T(8,128)(2,1)S(1)}, u32[]{:S(2)}, u32[]{:S(2)}) %all-to-all-start) | async-done | bytes 1048608 | tf_op jit(solution)/shard_map/all_to_all | solution.py:83
  42.0 0.0 copy-start.1
  42.0 1.0 copy-done.1
  43.0 2.9 %shard_map.94 = bf16[16,128,128]{2,1,0:T(8,128)(2,1)} custom-call(s32[32]{0:T(128)} %bitcast.53, s32[32]{0:T(128)} %bitcast.55, s32[1]{0:T(128)} %bitcast.42.count_ref, bf16[32,128,128]{2,1,0:T(8,128)(2,1)} %bitcast.44, bf16[32,128,128]{2,1,0:T(8,128)(2,1)} %copy-done.1), custom_call_target="tpu_custom_call" | custom-call | flops 134217728 | bytes 2621440 | tf_op jit(solution)/shard_map/pallas_call | solution.py:49
  45.9 0.0 copy-start.3
  45.9 31.2 %all_to_all.26 = bf16[16,128,128]{2,1,0:T(8,128)(2,1)S(1)} all-to-all(bf16[16,128,128]{2,1,0:T(8,128)(2,1)} %shard_map.94), channel_id=1, replica_groups=mesh['row'=32,'col'=16] {'col'}, dimensions={0} | all-to-all | bytes 1048576 | tf_op jit(solution)/shard_map/all_to_all | solution.py:89
  77.1 0.1 reduce_sum.42
  77.2 0.1 copy.21
  77.3 0.0 copy-done
  77.3 0.0 copy-done.3
  77.3 0.8 fusion
  78.1 0.2 convolution_convert_fusion
  78.3 0.2 convert_bitcast_fusion
  78.5 0.1 broadcast_in_dim.28
  78.7 23.1 %all_to_all.27.src_ref = bf16[16,160,128]{2,1,0:T(8,128)(2,1)S(1)} all-to-all(bf16[16,160,128]{2,1,0:T(8,128)(2,1)S(1)} %pad_maximum_fusion), channel_id=1, replica_groups=mesh['row'=32,'col'=16] {'col'}, dimensions={0} | all-to-all | bytes 1310720 | tf_op jit(solution)/shard_map/all_to_all | solution.py:110
  101.8 0.0 copy-start.2
  101.8 0.1 reshape.45
  101.9 0.2 fusion.1
  102.1 0.1 reshape.41
  102.2 0.1 maximum_bitcast_fusion
  102.3 0.6 copy.23.rest_0_
  102.9 0.0 copy-done.2
  102.9 3.2 %shard_map.95 = bf16[32,144,128]{2,1,0:T(8,128)(2,1)} custom-call(s32[32]{0:T(128)} %bitcast.56, s32[32]{0:T(128)} %bitcast.54, s32[1]{0:T(128)} %bitcast.43.count_ref, bf16[32,128,128]{2,1,0:T(8,128)(2,1)} %bitcast.45, bf16[16,160,128]{2,1,0:T(8,128)(2,1)} %copy-done.2, bf16[32,1,128]{2,1,0:T(2,128)(2,1)} %copy.23.rest_0_), custom_call_target="tpu_custom_call" | custom-call | flops 134217728 | bytes 2883584 | tf_op jit(solution)/shard_map/pallas_call | solution.py:49
  106.1 39.6 %all_to_all.28 = bf16[32,144,128]{2,1,0:T(8,128)(2,1)S(1)} all-to-all(bf16[32,144,128]{2,1,0:T(8,128)(2,1)} %shard_map.95), channel_id=1, replica_groups=mesh['row'=32,'col'=16] {'row'}, dimensions={0} | all-to-all | bytes 2359296 | tf_op jit(solution)/shard_map/all_to_all | solution.py:121
  145.8 0.1 fusion.7
  145.8 0.8 broadcast_in_dim.30
  146.7 10.6 %all-to-all-start.4 = ((f32[512,1,64]{2,1,0:T(1,128)}), f32[512,1,64]{2,1,0:T(1,128)S(1)}, u32[]{:S(2)}, u32[]{:S(2)}) async-start(f32[512,1,64]{2,1,0:T(1,128)} %broadcast_in_dim.30), calls=%async_computation.4 | async-start | bytes 524288 | tf_op jit(solution)/shard_map/all_to_all | solution.py:127
  157.3 0.8 slice_reduce_fusion
  158.0 16.7 %all-to-all-done.4 = f32[512,1,64]{2,1,0:T(1,128)S(1)} async-done(((f32[512,1,64]{2,1,0:T(1,128)}), f32[512,1,64]{2,1,0:T(1,128)S(1)}, u32[]{:S(2)}, u32[]{:S(2)}) %all-to-all-start.4) | async-done | bytes 131104 | tf_op jit(solution)/shard_map/all_to_all | solution.py:127
  174.8 0.1 copy.25
  174.9 0.8 mul.35
  (10 shorter events, 0.2 us)
Async XLA Ops:
  0.6 76.6 %copy-start = (bf16[128,256]{1,0:T(8,128)(2,1)S(1)}, bf16[128,256]{1,0:T(8,128)(2,1)}, u32[]{:S(2)}) copy-start(bf16[128,256]{1,0:T(8,128)(2,1)} %param.8) | copy-start | bytes 196612
  2.7 39.3 %all-to-all-start = ((bf16[32,128,128]{2,1,0:T(8,128)(2,1)}), bf16[32,128,128]{2,1,0:T(8,128)(2,1)S(1)}, u32[]{:S(2)}, u32[]{:S(2)}) async-start(bf16[32,128,128]{2,1,0:T(8,128)(2,1)} %broadcast_in_dim.26), calls=%async_computation | async-start | bytes 2097152 | tf_op jit(solution)/shard_map/all_to_all | solution.py:83
  42.0 1.0 copy-start.1
  45.9 31.4 %copy-start.3 = (bf16[1,128,256]{2,1,0:T(8,128)(2,1)S(1)}, bf16[1,128,256]{2,1,0:T(8,128)(2,1)}, u32[]{:S(2)}) copy-start(bf16[1,128,256]{2,1,0:T(8,128)(2,1)} %param.13) | copy-start | bytes 196612
  101.8 1.2 copy-start.2
  146.7 28.1 %all-to-all-start.4 = ((f32[512,1,64]{2,1,0:T(1,128)}), f32[512,1,64]{2,1,0:T(1,128)S(1)}, u32[]{:S(2)}, u32[]{:S(2)}) async-start(f32[512,1,64]{2,1,0:T(1,128)} %broadcast_in_dim.30), calls=%async_computation.4 | async-start | bytes 524288 | tf_op jit(solution)/shard_map/all_to_all | solution.py:127

commit v5 on v4

--- a/solution.py
+++ b/solution.py
@@ -64,6 +64,22 @@
     return hi, lo
 
 
+def replicate_kernel(x_ref, out_ref):
+    out_ref[...] = jnp.broadcast_to(x_ref[...], out_ref.shape)
+
+
+def replicate(x, copies):
+    vmem = pl.BlockSpec(memory_space=pltpu.VMEM)
+    return pl.pallas_call(
+        replicate_kernel,
+        out_shape=jax.ShapeDtypeStruct((copies,) + x.shape[1:], x.dtype),
+        in_specs=[vmem],
+        out_specs=vmem,
+        cost_estimate=pl.CostEstimate(
+            flops=0, transcendentals=0, bytes_accessed=(copies + 1) * x.size * x.dtype.itemsize),
+    )(x)
+
+
 def on_device(features, weight, tile_values, tile_rows, tile_cols, tile_count, cotangent):
     rows_dev = features.shape[1]
     width_in = features.shape[2]
@@ -79,10 +95,7 @@
     col_ids = tile_cols[0, 0]
     tile_total = tile_count[0, 0]
 
-    own = features[0]
-    gathered = lax.all_to_all(
-        jnp.broadcast_to(own[None], (n_row,) + own.shape), "row", 0, 0, tiled=False
-    )
+    gathered = lax.all_to_all(replicate(features, n_row), "row", 0, 0, tiled=False)
     col_source = gathered.reshape(col_tiles, tile_size, width_in)
     partial_value = spread(tile_block, row_ids, col_ids, tile_total, col_source, row_tiles, False, jnp.bfloat16)
     sent = partial_value.reshape(n_col, rows_dev, width_in)
@@ -124,11 +137,11 @@
     wg_piece = (wg_got[:, :piece] + wg_got[:, piece:]).sum(0)
 
     n_all = n_row * n_col
+    wg_piece = wg_piece * node_total ** (-0.5)
     everyone = lax.all_to_all(
-        jnp.broadcast_to(wg_piece[None], (n_all, piece)), ("row", "col"), 0, 0, tiled=False
+        jnp.broadcast_to(wg_piece[None], (n_all, piece)), ("col", "row"), 0, 0, tiled=True
     )
-    weight_grad = everyone.reshape(n_row, n_col, piece).transpose(1, 0, 2).reshape(width_in, width_out)
-    weight_grad = weight_grad * node_total ** (-0.5)
+    weight_grad = everyone.reshape(width_in, width_out)
     return (output, grad_features, weight_grad)
 
 

time: 176 us -> 178 us (1.011)
  Pallas kernels: 6.08 us -> 8.1 us
    pallas_call x0 -> x1, Pallas kernels: none -> 2.02 us  [replicate(): pl.pallas_call(replicate_kernel, out_shape=jax.ShapeDtypeStruct((copies,)...]
    broadcast_in_dim x1 -> x0, local copies, waits for them, and re-layouts: 2.02 us -> none  [on_device(): jnp.broadcast_to(own[None], (n_row,) + own.shape)]
where the time goes in v5:
time: 178 us; the launch traced here: 177 us
  blocking collectives  93.9 us (53%)
  waiting for transfers between devices  41.9 us (24%)
  starting transfers between devices  24 us (13%)
  Pallas kernels  8.1 us (5%)
  local copies, waits for them, and re-layouts  4.26 us (2%)
  other arithmetic  2.6 us (1%)
    all_to_all x1, blocking collectives, on_device(): got = lax.all_to_all(payload, 'row', 0, 0, tiled=False)  39.6 us
    all_to_all x1, blocking collectives, on_device(): got = lax.all_to_all(sent, 'col', 0, 0, tiled=False)  31.2 us
    all_to_all x1, waiting for transfers between devices, on_device(): lax.all_to_all(replicate(features, n_row), 'row', 0, 0, tiled=False)  25.2 us
    all_to_all x1, blocking collectives, on_device(): got = lax.all_to_all(payload, 'col', 0, 0, tiled=False)  23.1 us
    all_to_all x1, waiting for transfers between devices, on_device(): lax.all_to_all(jnp.broadcast_to(wg_piece[None], (n_all, piece)), ('col',...  16.7 us
    all_to_all x1, starting transfers between devices, on_device(): lax.all_to_all(replicate(features, n_row), 'row', 0, 0, tiled=False)  13.5 us
    all_to_all x1, starting transfers between devices, on_device(): lax.all_to_all(jnp.broadcast_to(wg_piece[None], (n_all, piece)), ('col',...  10.5 us
    pallas_call x2, Pallas kernels, spread(): pl.pallas_call(functools.partial(spread_kernel, transpose), out_shape=jax...  6.08 us
  transfers between devices with their start and end apart: 2, of which 2 were waited for; matrix products, arithmetic and copies ran while one was open for 0% of the time, Pallas kernels for 0%

profile of v5, /device:TPU:1, one launch (start us, length us, event | category | flops | bytes accessed | tf_op | source)
XLA Modules:
  0.0 177.3 jit_solution(4854728118149225299)
XLA Ops:
  0.6 0.0 copy-start
  0.6 2.0 %shard_map.94 = bf16[32,128,128]{2,1,0:T(8,128)(2,1)} custom-call(bf16[1,128,128]{2,1,0:T(8,128)(2,1)} %x_ref.1), custom_call_target="tpu_custom_call" | custom-call | bytes 1081344 | tf_op jit(solution)/shard_map/pallas_call | solution.py:73
  2.7 13.5 %all-to-all-start = ((bf16[32,128,128]{2,1,0:T(8,128)(2,1)}), bf16[32,128,128]{2,1,0:T(8,128)(2,1)S(1)}, u32[]{:S(2)}, u32[]{:S(2)}) async-start(bf16[32,128,128]{2,1,0:T(8,128)(2,1)} %shard_map.94), calls=%async_computation | async-start | bytes 2097152 | tf_op jit(solution)/shard_map/all_to_all | solution.py:98
  16.8 25.2 %all-to-all-done.src_ref = bf16[32,128,128]{2,1,0:T(8,128)(2,1)S(1)} async-done(((bf16[32,128,128]{2,1,0:T(8,128)(2,1)}), bf16[32,128,128]{2,1,0:T(8,128)(2,1)S(1)}, u32[]{:S(2)}, u32[]{:S(2)}) %all-to-all-start) | async-done | bytes 1048608 | tf_op jit(solution)/shard_map/all_to_all | solution.py:98
  42.0 0.0 copy-start.1
  42.0 1.0 copy-done.1
  43.0 2.9 %shard_map.95 = bf16[16,128,128]{2,1,0:T(8,128)(2,1)} custom-call(s32[32]{0:T(128)} %bitcast.45, s32[32]{0:T(128)} %bitcast.47, s32[1]{0:T(128)} %bitcast.37.count_ref, bf16[32,128,128]{2,1,0:T(8,128)(2,1)} %bitcast.39, bf16[32,128,128]{2,1,0:T(8,128)(2,1)} %copy-done.1), custom_call_target="tpu_custom_call" | custom-call | flops 134217728 | bytes 2621440 | tf_op jit(solution)/shard_map/pallas_call | solution.py:49
  45.9 0.0 copy-start.3
  45.9 31.2 %all_to_all.26 = bf16[16,128,128]{2,1,0:T(8,128)(2,1)S(1)} all-to-all(bf16[16,128,128]{2,1,0:T(8,128)(2,1)} %shard_map.95), channel_id=1, replica_groups=mesh['row'=32,'col'=16] {'col'}, dimensions={0} | all-to-all | bytes 1048576 | tf_op jit(solution)/shard_map/all_to_all | solution.py:102
  77.1 0.1 reduce_sum.42
  77.2 0.1 copy.16
  77.3 0.0 copy-done
  77.3 0.0 copy-done.3
  77.3 0.8 fusion
  78.1 0.2 convolution_convert_fusion
  78.3 0.2 convert_bitcast_fusion
  78.5 0.1 broadcast_in_dim.9
  78.7 23.1 %all_to_all.27.src_ref = bf16[16,160,128]{2,1,0:T(8,128)(2,1)S(1)} all-to-all(bf16[16,160,128]{2,1,0:T(8,128)(2,1)S(1)} %pad_maximum_fusion), channel_id=1, replica_groups=mesh['row'=32,'col'=16] {'col'}, dimensions={0} | all-to-all | bytes 1310720 | tf_op jit(solution)/shard_map/all_to_all | solution.py:123
  101.8 0.0 copy-start.2
  101.8 0.1 reshape.46
  102.0 0.2 fusion.1
  102.2 0.1 reshape.41
  102.2 0.1 maximum_bitcast_fusion
  102.3 0.6 copy.18.rest_0_
  102.9 0.0 copy-done.2
  102.9 3.2 %shard_map.96 = bf16[32,144,128]{2,1,0:T(8,128)(2,1)} custom-call(s32[32]{0:T(128)} %bitcast.48, s32[32]{0:T(128)} %bitcast.46, s32[1]{0:T(128)} %bitcast.38.count_ref, bf16[32,128,128]{2,1,0:T(8,128)(2,1)} %bitcast.40, bf16[16,160,128]{2,1,0:T(8,128)(2,1)} %copy-done.2, bf16[32,1,128]{2,1,0:T(2,128)(2,1)} %copy.18.rest_0_), custom_call_target="tpu_custom_call" | custom-call | flops 134217728 | bytes 2883584 | tf_op jit(solution)/shard_map/pallas_call | solution.py:49
  106.1 39.6 %all_to_all.28 = bf16[32,144,128]{2,1,0:T(8,128)(2,1)S(1)} all-to-all(bf16[32,144,128]{2,1,0:T(8,128)(2,1)} %shard_map.96), channel_id=1, replica_groups=mesh['row'=32,'col'=16] {'row'}, dimensions={0} | all-to-all | bytes 2359296 | tf_op jit(solution)/shard_map/all_to_all | solution.py:134
  145.8 0.1 fusion.7
  145.9 0.8 broadcast_in_dim.21
  146.7 10.5 %all-to-all-start.4 = ((f32[512,1,64]{2,1,0:T(1,128)}), f32[512,1,64]{2,1,0:T(1,128)S(1)}, u32[]{:S(2)}, u32[]{:S(2)}) async-start(f32[512,1,64]{2,1,0:T(1,128)} %broadcast_in_dim.21), calls=%async_computation.4 | async-start | bytes 524288 | tf_op jit(solution)/shard_map/all_to_all | solution.py:141
  157.3 0.8 slice_reduce_fusion
  158.0 16.7 %all-to-all-done.4 = f32[512,1,64]{2,1,0:T(1,128)S(1)} async-done(((f32[512,1,64]{2,1,0:T(1,128)}), f32[512,1,64]{2,1,0:T(1,128)S(1)}, u32[]{:S(2)}, u32[]{:S(2)}) %all-to-all-start.4) | async-done | bytes 131104 | tf_op jit(solution)/shard_map/all_to_all | solution.py:141
  174.7 0.5 broadcast.20
  175.3 1.3 reduce.6
  176.6 0.8 reshape.44
  (10 shorter events, 0.2 us)
Async XLA Ops:
  0.6 76.6 %copy-start = (bf16[128,256]{1,0:T(8,128)(2,1)S(1)}, bf16[128,256]{1,0:T(8,128)(2,1)}, u32[]{:S(2)}) copy-start(bf16[128,256]{1,0:T(8,128)(2,1)} %param.8) | copy-start | bytes 196612
  2.7 39.3 %all-to-all-start = ((bf16[32,128,128]{2,1,0:T(8,128)(2,1)}), bf16[32,128,128]{2,1,0:T(8,128)(2,1)S(1)}, u32[]{:S(2)}, u32[]{:S(2)}) async-start(bf16[32,128,128]{2,1,0:T(8,128)(2,1)} %shard_map.94), calls=%async_computation | async-start | bytes 2097152 | tf_op jit(solution)/shard_map/all_to_all | solution.py:98
  42.0 1.0 copy-start.1
  45.9 31.4 %copy-start.3 = (bf16[1,128,256]{2,1,0:T(8,128)(2,1)S(1)}, bf16[1,128,256]{2,1,0:T(8,128)(2,1)}, u32[]{:S(2)}) copy-start(bf16[1,128,256]{2,1,0:T(8,128)(2,1)} %param.13) | copy-start | bytes 196612
  101.8 1.2 copy-start.2
  146.7 28.0 %all-to-all-start.4 = ((f32[512,1,64]{2,1,0:T(1,128)}), f32[512,1,64]{2,1,0:T(1,128)S(1)}, u32[]{:S(2)}, u32[]{:S(2)}) async-start(f32[512,1,64]{2,1,0:T(1,128)} %broadcast_in_dim.21), calls=%async_computation.4 | async-start | bytes 524288 | tf_op jit(solution)/shard_map/all_to_all | solution.py:141

commit v6 on v4

--- a/solution.py
+++ b/solution.py
@@ -30,10 +30,7 @@
         out_ref[...] = acc_ref[...].astype(out_ref.dtype)
     else:
         out_ref[:, :tb, :] = acc_ref[...].astype(out_ref.dtype)
-        words = extra_ref.shape[1]
-        out_ref[:, tb:tb + words, :] = extra_ref[...]
-        out_ref[:, tb + words:, :] = jnp.zeros(
-            (out_ref.shape[0], out_ref.shape[1] - tb - words, out_ref.shape[2]), out_ref.dtype)
+        out_ref[:, tb:, :] = jnp.broadcast_to(extra_ref[...][None], (out_ref.shape[0],) + extra_ref.shape)
 
 
 def spread(tiles, target_ids, source_ids, count, source, out_blocks, transpose, out_dtype, extra=None):
@@ -45,7 +42,7 @@
     out_rows = tb
     if extra is not None:
         args.append(extra)
-        out_rows += -(-extra.shape[1] // 16) * 16
+        out_rows += extra.shape[0]
     return pl.pallas_call(
         functools.partial(spread_kernel, transpose),
         out_shape=jax.ShapeDtypeStruct((out_blocks, out_rows, width), out_dtype),
@@ -112,23 +109,20 @@
     wg_got = got[:, rows_dev:].reshape(n_col, 2, wg_rows * width_out).astype(jnp.float32)
     wg_col = (wg_got[:, 0] + wg_got[:, 1]).sum(0)
 
-    piece = wg_col.shape[0] // n_row
-    hi, lo = split_f32(wg_col.reshape(n_row, piece))
-    wg_words = jnp.concatenate([hi, lo], axis=1).reshape(n_row, -1, width_in)
+    hi, lo = split_f32(wg_col)
+    wg_words = jnp.stack([hi, lo]).reshape(-1, width_in)
     payload = spread(
         tile_block, col_ids, row_ids, tile_total, row_source, col_tiles, True, jnp.bfloat16, wg_words
     )
     got = lax.all_to_all(payload, "row", 0, 0, tiled=False)
     grad_features = got[:, :rows_dev].astype(jnp.float32).sum(0).astype(jnp.bfloat16)[None]
-    wg_got = got[:, rows_dev:].reshape(n_row, -1)[:, : 2 * piece].astype(jnp.float32)
-    wg_piece = (wg_got[:, :piece] + wg_got[:, piece:]).sum(0)
+    wg_got = got[:, rows_dev:].reshape(n_row, 2, -1).astype(jnp.float32)
+    wg_part = (wg_got[:, 0] + wg_got[:, 1]).sum(0) * node_total ** (-0.5)
 
-    n_all = n_row * n_col
     everyone = lax.all_to_all(
-        jnp.broadcast_to(wg_piece[None], (n_all, piece)), ("row", "col"), 0, 0, tiled=False
+        jnp.broadcast_to(wg_part[None], (n_col,) + wg_part.shape), "col", 0, 0, tiled=False
     )
-    weight_grad = everyone.reshape(n_row, n_col, piece).transpose(1, 0, 2).reshape(width_in, width_out)
-    weight_grad = weight_grad * node_total ** (-0.5)
+    weight_grad = everyone.reshape(width_in, width_out)
     return (output, grad_features, weight_grad)
 
 

time: 176 us -> 166 us (0.943)
  waiting for transfers between devices: 41.9 us -> 34.6 us
  starting transfers between devices: 24 us -> 19.4 us
    all_to_all x1, waiting for transfers between devices: 16.7 us -> 9.39 us  [on_device(): lax.all_to_all(jnp.broadcast_to(wg_part[None], (n_col,) + wg_part.shape),...]
    all_to_all x1, starting transfers between devices: 10.6 us -> 5.98 us  [on_device(): lax.all_to_all(jnp.broadcast_to(wg_part[None], (n_col,) + wg_part.shape),...]
where the time goes in v6:
time: 166 us; the launch traced here: 165 us
  blocking collectives  94.8 us (57%)
  waiting for transfers between devices  34.6 us (21%)
  starting transfers between devices  19.4 us (12%)
  Pallas kernels  6.14 us (4%)
  local copies, waits for them, and re-layouts  5.72 us (3%)
  other arithmetic  1.87 us (1%)
    all_to_all x1, blocking collectives, on_device(): got = lax.all_to_all(payload, 'row', 0, 0, tiled=False)  40.5 us
    all_to_all x1, blocking collectives, on_device(): got = lax.all_to_all(sent, 'col', 0, 0, tiled=False)  31.2 us
    all_to_all x1, waiting for transfers between devices, on_device(): lax.all_to_all(jnp.broadcast_to(own[None], (n_row,) + own.shape), 'row',...  25.2 us
    all_to_all x1, blocking collectives, on_device(): got = lax.all_to_all(payload, 'col', 0, 0, tiled=False)  23.1 us
    all_to_all x1, starting transfers between devices, on_device(): lax.all_to_all(jnp.broadcast_to(own[None], (n_row,) + own.shape), 'row',...  13.5 us
    all_to_all x1, waiting for transfers between devices, on_device(): lax.all_to_all(jnp.broadcast_to(wg_part[None], (n_col,) + wg_part.shape),...  9.39 us
    pallas_call x2, Pallas kernels, spread(): pl.pallas_call(functools.partial(spread_kernel, transpose), out_shape=jax...  6.14 us
    all_to_all x1, starting transfers between devices, on_device(): lax.all_to_all(jnp.broadcast_to(wg_part[None], (n_col,) + wg_part.shape),...  5.98 us
  transfers between devices with their start and end apart: 2, of which 2 were waited for; matrix products, arithmetic and copies ran while one was open for 0% of the time, Pallas kernels for 0%

profile of v6, /device:TPU:1, one launch (start us, length us, event | category | flops | bytes accessed | tf_op | source)
XLA Modules:
  0.0 165.2 jit_solution(4799094244585405180)
XLA Ops:
  0.6 0.0 copy-start
  0.6 2.0 %broadcast_in_dim.26 = bf16[32,128,128]{2,1,0:T(8,128)(2,1)} broadcast(bf16[128,128]{1,0:T(8,128)(2,1)} %bitcast.40), dimensions={1,2} | broadcast | bytes 1081344 | tf_op jit(solution)/shard_map/broadcast_in_dim | solution.py:81
  2.7 13.5 %all-to-all-start = ((bf16[32,128,128]{2,1,0:T(8,128)(2,1)}), bf16[32,128,128]{2,1,0:T(8,128)(2,1)S(1)}, u32[]{:S(2)}, u32[]{:S(2)}) async-start(bf16[32,128,128]{2,1,0:T(8,128)(2,1)} %broadcast_in_dim.26), calls=%async_computation | async-start | bytes 2097152 | tf_op jit(solution)/shard_map/all_to_all | solution.py:80
  16.8 25.2 %all-to-all-done.src_ref = bf16[32,128,128]{2,1,0:T(8,128)(2,1)S(1)} async-done(((bf16[32,128,128]{2,1,0:T(8,128)(2,1)}), bf16[32,128,128]{2,1,0:T(8,128)(2,1)S(1)}, u32[]{:S(2)}, u32[]{:S(2)}) %all-to-all-start) | async-done | bytes 1048608 | tf_op jit(solution)/shard_map/all_to_all | solution.py:80
  42.0 0.0 copy-start.1
  42.0 1.0 copy-done.1
  43.0 2.9 %shard_map.94 = bf16[16,128,128]{2,1,0:T(8,128)(2,1)} custom-call(s32[32]{0:T(128)} %bitcast.42, s32[32]{0:T(128)} %bitcast.44, s32[1]{0:T(128)} %bitcast.33.count_ref, bf16[32,128,128]{2,1,0:T(8,128)(2,1)} %bitcast.35, bf16[32,128,128]{2,1,0:T(8,128)(2,1)} %copy-done.1), custom_call_target="tpu_custom_call" | custom-call | flops 134217728 | bytes 2621440 | tf_op jit(solution)/shard_map/pallas_call | solution.py:46
  45.9 0.0 copy-start.3
  45.9 31.2 %all_to_all.26 = bf16[16,128,128]{2,1,0:T(8,128)(2,1)S(1)} all-to-all(bf16[16,128,128]{2,1,0:T(8,128)(2,1)} %shard_map.94), channel_id=1, replica_groups=mesh['row'=32,'col'=16] {'col'}, dimensions={0} | all-to-all | bytes 1048576 | tf_op jit(solution)/shard_map/all_to_all | solution.py:86
  77.1 0.1 reduce_sum.44
  77.2 0.1 copy.13
  77.3 0.0 copy-done
  77.3 0.0 copy-done.3
  77.3 0.8 fusion.1
  78.1 0.2 convolution_convert_fusion
  78.3 0.2 convert_bitcast_fusion
  78.5 0.1 broadcast_in_dim.28
  78.7 23.1 %all_to_all.27.src_ref = bf16[16,160,128]{2,1,0:T(8,128)(2,1)S(1)} all-to-all(bf16[16,160,128]{2,1,0:T(8,128)(2,1)S(1)} %pad_maximum_fusion), channel_id=1, replica_groups=mesh['row'=32,'col'=16] {'col'}, dimensions={0} | all-to-all | bytes 1310720 | tf_op jit(solution)/shard_map/all_to_all | solution.py:107
  101.8 0.0 copy-start.2
  101.8 0.1 reshape.62
  101.9 0.2 fusion.2
  102.2 0.6 reshape.59.rest_0_
  102.8 0.0 copy-done.2
  102.8 3.2 %shard_map.95 = bf16[32,160,128]{2,1,0:T(8,128)(2,1)} custom-call(s32[32]{0:T(128)} %bitcast.45, s32[32]{0:T(128)} %bitcast.43, s32[1]{0:T(128)} %bitcast.34.count_ref, bf16[32,128,128]{2,1,0:T(8,128)(2,1)} %bitcast.36, bf16[16,160,128]{2,1,0:T(8,128)(2,1)} %copy-done.2, bf16[32,128]{1,0:T(8,128)(2,1)} %reshape.59.rest_0_), custom_call_target="tpu_custom_call" | custom-call | flops 134217728 | bytes 3014656 | tf_op jit(solution)/shard_map/pallas_call | solution.py:46
  106.1 40.5 %all_to_all.28 = bf16[32,160,128]{2,1,0:T(8,128)(2,1)S(1)} all-to-all(bf16[32,160,128]{2,1,0:T(8,128)(2,1)} %shard_map.95), channel_id=1, replica_groups=mesh['row'=32,'col'=16] {'row'}, dimensions={0} | all-to-all | bytes 2621440 | tf_op jit(solution)/shard_map/all_to_all | solution.py:117
  146.6 0.1 slice_convert_fusion
  146.7 0.3 reshape.63
  146.9 0.4 fusion
  147.3 0.7 broadcast_in_dim.30
  148.0 6.0 %all-to-all-start.4 = ((f32[16,1,2048]{2,1,0:T(1,128)}), f32[16,1,2048]{2,1,0:T(1,128)S(1)}, u32[]{:S(2)}, u32[]{:S(2)}) async-start(f32[16,1,2048]{2,1,0:T(1,128)} %broadcast_in_dim.30), calls=%async_computation.4 | async-start | bytes 262144 | tf_op jit(solution)/shard_map/all_to_all | solution.py:122
  154.0 0.8 slice_reduce_fusion
  154.8 9.4 %all-to-all-done.4 = f32[16,1,2048]{2,1,0:T(1,128)S(1)} async-done(((f32[16,1,2048]{2,1,0:T(1,128)}), f32[16,1,2048]{2,1,0:T(1,128)S(1)}, u32[]{:S(2)}, u32[]{:S(2)}) %all-to-all-start.4) | async-done | bytes 131104 | tf_op jit(solution)/shard_map/all_to_all | solution.py:122
  164.2 0.3 reduce.4
  164.5 0.7 reshape.60
  (9 shorter events, 0.2 us)
Async XLA Ops:
  0.6 76.6 %copy-start = (bf16[128,256]{1,0:T(8,128)(2,1)S(1)}, bf16[128,256]{1,0:T(8,128)(2,1)}, u32[]{:S(2)}) copy-start(bf16[128,256]{1,0:T(8,128)(2,1)} %param.8) | copy-start | bytes 196612
  2.7 39.3 %all-to-all-start = ((bf16[32,128,128]{2,1,0:T(8,128)(2,1)}), bf16[32,128,128]{2,1,0:T(8,128)(2,1)S(1)}, u32[]{:S(2)}, u32[]{:S(2)}) async-start(bf16[32,128,128]{2,1,0:T(8,128)(2,1)} %broadcast_in_dim.26), calls=%async_computation | async-start | bytes 2097152 | tf_op jit(solution)/shard_map/all_to_all | solution.py:80
  42.0 1.0 copy-start.1
  45.9 31.4 %copy-start.3 = (bf16[1,128,256]{2,1,0:T(8,128)(2,1)S(1)}, bf16[1,128,256]{2,1,0:T(8,128)(2,1)}, u32[]{:S(2)}) copy-start(bf16[1,128,256]{2,1,0:T(8,128)(2,1)} %param.13) | copy-start | bytes 196612
  101.8 1.0 copy-start.2
  148.0 16.1 %all-to-all-start.4 = ((f32[16,1,2048]{2,1,0:T(1,128)}), f32[16,1,2048]{2,1,0:T(1,128)S(1)}, u32[]{:S(2)}, u32[]{:S(2)}) async-start(f32[16,1,2048]{2,1,0:T(1,128)} %broadcast_in_dim.30), calls=%async_computation.4 | async-start | bytes 262144 | tf_op jit(solution)/shard_map/all_to_all | solution.py:122

commit v7 on v6

--- a/solution.py
+++ b/solution.py
@@ -118,6 +118,7 @@
     grad_features = got[:, :rows_dev].astype(jnp.float32).sum(0).astype(jnp.bfloat16)[None]
     wg_got = got[:, rows_dev:].reshape(n_row, 2, -1).astype(jnp.float32)
     wg_part = (wg_got[:, 0] + wg_got[:, 1]).sum(0) * node_total ** (-0.5)
+    wg_part = wg_part.reshape(wg_rows, width_out)
 
     everyone = lax.all_to_all(
         jnp.broadcast_to(wg_part[None], (n_col,) + wg_part.shape), "col", 0, 0, tiled=False

time: 166 us -> 165 us (level)
  no operation moved by 1% of the time
where the time goes in v7:
time: 165 us
  blocking collectives  94.8 us (57%)
  waiting for transfers between devices  34.6 us (21%)
  starting transfers between devices  19.5 us (12%)
  Pallas kernels  6.14 us (4%)
  local copies, waits for them, and re-layouts  5.63 us (3%)
    all_to_all x1, blocking collectives, on_device(): got = lax.all_to_all(payload, 'row', 0, 0, tiled=False)  40.5 us
    all_to_all x1, blocking collectives, on_device(): got = lax.all_to_all(sent, 'col', 0, 0, tiled=False)  31.2 us
    all_to_all x1, waiting for transfers between devices, on_device(): lax.all_to_all(jnp.broadcast_to(own[None], (n_row,) + own.shape), 'row',...  25.2 us
    all_to_all x1, blocking collectives, on_device(): got = lax.all_to_all(payload, 'col', 0, 0, tiled=False)  23.1 us
    all_to_all x1, starting transfers between devices, on_device(): lax.all_to_all(jnp.broadcast_to(own[None], (n_row,) + own.shape), 'row',...  13.5 us
    all_to_all x1, waiting for transfers between devices, on_device(): lax.all_to_all(jnp.broadcast_to(wg_part[None], (n_col,) + wg_part.shape),...  9.39 us
    pallas_call x2, Pallas kernels, spread(): pl.pallas_call(functools.partial(spread_kernel, transpose), out_shape=jax...  6.14 us
    all_to_all x1, starting transfers between devices, on_device(): lax.all_to_all(jnp.broadcast_to(wg_part[None], (n_col,) + wg_part.shape),...  5.99 us
  transfers between devices with their start and end apart: 2, of which 2 were waited for; matrix products, arithmetic and copies ran while one was open for 0% of the time, Pallas kernels for 0%

profile of v7, /device:TPU:1, one launch (start us, length us, event | category | flops | bytes accessed | tf_op | source)
XLA Modules:
  0.0 164.8 jit_solution(14989288336230748367)
XLA Ops:
  0.6 0.0 copy-start
  0.6 2.0 %broadcast_in_dim.25 = bf16[32,128,128]{2,1,0:T(8,128)(2,1)} broadcast(bf16[128,128]{1,0:T(8,128)(2,1)} %bitcast.42), dimensions={1,2} | broadcast | bytes 1081344 | tf_op jit(solution)/shard_map/broadcast_in_dim | solution.py:81
  2.7 13.5 %all-to-all-start = ((bf16[32,128,128]{2,1,0:T(8,128)(2,1)}), bf16[32,128,128]{2,1,0:T(8,128)(2,1)S(1)}, u32[]{:S(2)}, u32[]{:S(2)}) async-start(bf16[32,128,128]{2,1,0:T(8,128)(2,1)} %broadcast_in_dim.25), calls=%async_computation | async-start | bytes 2097152 | tf_op jit(solution)/shard_map/all_to_all | solution.py:80
  16.8 25.2 %all-to-all-done.src_ref = bf16[32,128,128]{2,1,0:T(8,128)(2,1)S(1)} async-done(((bf16[32,128,128]{2,1,0:T(8,128)(2,1)}), bf16[32,128,128]{2,1,0:T(8,128)(2,1)S(1)}, u32[]{:S(2)}, u32[]{:S(2)}) %all-to-all-start) | async-done | bytes 1048608 | tf_op jit(solution)/shard_map/all_to_all | solution.py:80
  42.0 0.0 copy-start.1
  42.0 1.0 copy-done.1
  43.0 2.9 %shard_map.94 = bf16[16,128,128]{2,1,0:T(8,128)(2,1)} custom-call(s32[32]{0:T(128)} %bitcast.44, s32[32]{0:T(128)} %bitcast.46, s32[1]{0:T(128)} %bitcast.34.count_ref, bf16[32,128,128]{2,1,0:T(8,128)(2,1)} %bitcast.36, bf16[32,128,128]{2,1,0:T(8,128)(2,1)} %copy-done.1), custom_call_target="tpu_custom_call" | custom-call | flops 134217728 | bytes 2621440 | tf_op jit(solution)/shard_map/pallas_call | solution.py:46
  45.9 0.0 copy-start.3
  45.9 31.2 %all_to_all.25 = bf16[16,128,128]{2,1,0:T(8,128)(2,1)S(1)} all-to-all(bf16[16,128,128]{2,1,0:T(8,128)(2,1)} %shard_map.94), channel_id=1, replica_groups=mesh['row'=32,'col'=16] {'col'}, dimensions={0} | all-to-all | bytes 1048576 | tf_op jit(solution)/shard_map/all_to_all | solution.py:86
  77.1 0.1 reduce_sum.44
  77.2 0.1 copy.13
  77.3 0.0 copy-done
  77.3 0.0 copy-done.3
  77.3 0.8 fusion.1
  78.1 0.2 convolution_convert_fusion
  78.3 0.2 convert_bitcast_fusion
  78.5 0.1 broadcast_in_dim.27
  78.7 23.1 %all_to_all.26.src_ref = bf16[16,160,128]{2,1,0:T(8,128)(2,1)S(1)} all-to-all(bf16[16,160,128]{2,1,0:T(8,128)(2,1)S(1)} %pad_maximum_fusion), channel_id=1, replica_groups=mesh['row'=32,'col'=16] {'col'}, dimensions={0} | all-to-all | bytes 1310720 | tf_op jit(solution)/shard_map/all_to_all | solution.py:107
  101.8 0.0 copy-start.2
  101.8 0.1 reshape.59
  102.0 0.2 fusion.2
  102.2 0.6 reshape.56.rest_0_
  102.8 0.0 copy-done.2
  102.8 3.3 %shard_map.95 = bf16[32,160,128]{2,1,0:T(8,128)(2,1)} custom-call(s32[32]{0:T(128)} %bitcast.47, s32[32]{0:T(128)} %bitcast.45, s32[1]{0:T(128)} %bitcast.35.count_ref, bf16[32,128,128]{2,1,0:T(8,128)(2,1)} %bitcast.37, bf16[16,160,128]{2,1,0:T(8,128)(2,1)} %copy-done.2, bf16[32,128]{1,0:T(8,128)(2,1)} %reshape.56.rest_0_), custom_call_target="tpu_custom_call" | custom-call | flops 134217728 | bytes 3014656 | tf_op jit(solution)/shard_map/pallas_call | solution.py:46
  106.1 40.5 %all_to_all.27 = bf16[32,160,128]{2,1,0:T(8,128)(2,1)S(1)} all-to-all(bf16[32,160,128]{2,1,0:T(8,128)(2,1)} %shard_map.95), channel_id=1, replica_groups=mesh['row'=32,'col'=16] {'row'}, dimensions={0} | all-to-all | bytes 2621440 | tf_op jit(solution)/shard_map/all_to_all | solution.py:117
  146.6 0.1 slice_convert_fusion
  146.7 0.3 reshape.60
  146.9 0.4 fusion
  147.3 0.7 broadcast_in_dim.29
  148.0 6.0 %all-to-all-start.4 = ((f32[16,8,256]{2,1,0:T(8,128)}), f32[16,8,256]{2,1,0:T(8,128)S(1)}, u32[]{:S(2)}, u32[]{:S(2)}) async-start(f32[16,8,256]{2,1,0:T(8,128)} %broadcast_in_dim.29), calls=%async_computation.4 | async-start | bytes 262144 | tf_op jit(solution)/shard_map/all_to_all | solution.py:123
  154.0 0.8 slice_reduce_fusion
  154.7 9.4 %all-to-all-done.4 = f32[16,8,256]{2,1,0:T(8,128)S(1)} async-done(((f32[16,8,256]{2,1,0:T(8,128)}), f32[16,8,256]{2,1,0:T(8,128)S(1)}, u32[]{:S(2)}, u32[]{:S(2)}) %all-to-all-start.4) | async-done | bytes 131104 | tf_op jit(solution)/shard_map/all_to_all | solution.py:123
  164.1 0.7 copy.17
  (10 shorter events, 0.2 us)
Async XLA Ops:
  0.6 76.6 %copy-start = (bf16[128,256]{1,0:T(8,128)(2,1)S(1)}, bf16[128,256]{1,0:T(8,128)(2,1)}, u32[]{:S(2)}) copy-start(bf16[128,256]{1,0:T(8,128)(2,1)} %param.8) | copy-start | bytes 196612
  2.7 39.3 %all-to-all-start = ((bf16[32,128,128]{2,1,0:T(8,128)(2,1)}), bf16[32,128,128]{2,1,0:T(8,128)(2,1)S(1)}, u32[]{:S(2)}, u32[]{:S(2)}) async-start(bf16[32,128,128]{2,1,0:T(8,128)(2,1)} %broadcast_in_dim.25), calls=%async_computation | async-start | bytes 2097152 | tf_op jit(solution)/shard_map/all_to_all | solution.py:80
  42.0 1.0 copy-start.1
  45.9 31.4 %copy-start.3 = (bf16[1,128,256]{2,1,0:T(8,128)(2,1)S(1)}, bf16[1,128,256]{2,1,0:T(8,128)(2,1)}, u32[]{:S(2)}) copy-start(bf16[1,128,256]{2,1,0:T(8,128)(2,1)} %param.13) | copy-start | bytes 196612
  101.8 1.0 copy-start.2
  148.0 16.1 %all-to-all-start.4 = ((f32[16,8,256]{2,1,0:T(8,128)}), f32[16,8,256]{2,1,0:T(8,128)S(1)}, u32[]{:S(2)}, u32[]{:S(2)}) async-start(f32[16,8,256]{2,1,0:T(8,128)} %broadcast_in_dim.29), calls=%async_computation.4 | async-start | bytes 262144 | tf_op jit(solution)/shard_map/all_to_all | solution.py:123

commit v8 on v7

--- a/solution.py
+++ b/solution.py
@@ -106,17 +106,17 @@
     )
     got = lax.all_to_all(payload, "col", 0, 0, tiled=False)
     row_source = got
-    wg_got = got[:, rows_dev:].reshape(n_col, 2, wg_rows * width_out).astype(jnp.float32)
+    wg_got = got[:, rows_dev:].reshape(n_col, 2, -1, width_in).astype(jnp.float32)
     wg_col = (wg_got[:, 0] + wg_got[:, 1]).sum(0)
 
     hi, lo = split_f32(wg_col)
-    wg_words = jnp.stack([hi, lo]).reshape(-1, width_in)
+    wg_words = jnp.concatenate([hi, lo], axis=0)
     payload = spread(
         tile_block, col_ids, row_ids, tile_total, row_source, col_tiles, True, jnp.bfloat16, wg_words
     )
     got = lax.all_to_all(payload, "row", 0, 0, tiled=False)
     grad_features = got[:, :rows_dev].astype(jnp.float32).sum(0).astype(jnp.bfloat16)[None]
-    wg_got = got[:, rows_dev:].reshape(n_row, 2, -1).astype(jnp.float32)
+    wg_got = got[:, rows_dev:].reshape(n_row, 2, -1, width_in).astype(jnp.float32)
     wg_part = (wg_got[:, 0] + wg_got[:, 1]).sum(0) * node_total ** (-0.5)
     wg_part = wg_part.reshape(wg_rows, width_out)
 

time: 165 us -> 165 us (level)
  no operation moved by 1% of the time
where the time goes in v8:
time: 165 us; the launch traced here: 164 us
  blocking collectives  94.8 us (57%)
  waiting for transfers between devices  34.6 us (21%)
  starting transfers between devices  19.5 us (12%)
  Pallas kernels  6.13 us (4%)
  local copies, waits for them, and re-layouts  4.71 us (3%)
  other arithmetic  1.76 us (1%)
    all_to_all x1, blocking collectives, on_device(): got = lax.all_to_all(payload, 'row', 0, 0, tiled=False)  40.5 us
    all_to_all x1, blocking collectives, on_device(): got = lax.all_to_all(sent, 'col', 0, 0, tiled=False)  31.2 us
    all_to_all x1, waiting for transfers between devices, on_device(): lax.all_to_all(jnp.broadcast_to(own[None], (n_row,) + own.shape), 'row',...  25.2 us
    all_to_all x1, blocking collectives, on_device(): got = lax.all_to_all(payload, 'col', 0, 0, tiled=False)  23.1 us
    all_to_all x1, starting transfers between devices, on_device(): lax.all_to_all(jnp.broadcast_to(own[None], (n_row,) + own.shape), 'row',...  13.5 us
    all_to_all x1, waiting for transfers between devices, on_device(): lax.all_to_all(jnp.broadcast_to(wg_part[None], (n_col,) + wg_part.shape),...  9.39 us
    pallas_call x2, Pallas kernels, spread(): pl.pallas_call(functools.partial(spread_kernel, transpose), out_shape=jax...  6.13 us
    all_to_all x1, starting transfers between devices, on_device(): lax.all_to_all(jnp.broadcast_to(wg_part[None], (n_col,) + wg_part.shape),...  6 us
  transfers between devices with their start and end apart: 2, of which 2 were waited for; matrix products, arithmetic and copies ran while one was open for 0% of the time, Pallas kernels for 0%

profile of v8, /device:TPU:1, one launch (start us, length us, event | category | flops | bytes accessed | tf_op | source)
XLA Modules:
  0.0 164.0 jit_solution(9060178892972763906)
XLA Ops:
  0.6 0.0 copy-start
  0.6 2.0 %broadcast_in_dim.25 = bf16[32,128,128]{2,1,0:T(8,128)(2,1)} broadcast(bf16[128,128]{1,0:T(8,128)(2,1)} %bitcast.45), dimensions={1,2} | broadcast | bytes 1081344 | tf_op jit(solution)/shard_map/broadcast_in_dim | solution.py:81
  2.7 13.5 %all-to-all-start = ((bf16[32,128,128]{2,1,0:T(8,128)(2,1)}), bf16[32,128,128]{2,1,0:T(8,128)(2,1)S(1)}, u32[]{:S(2)}, u32[]{:S(2)}) async-start(bf16[32,128,128]{2,1,0:T(8,128)(2,1)} %broadcast_in_dim.25), calls=%async_computation | async-start | bytes 2097152 | tf_op jit(solution)/shard_map/all_to_all | solution.py:80
  16.8 25.2 %all-to-all-done.src_ref = bf16[32,128,128]{2,1,0:T(8,128)(2,1)S(1)} async-done(((bf16[32,128,128]{2,1,0:T(8,128)(2,1)}), bf16[32,128,128]{2,1,0:T(8,128)(2,1)S(1)}, u32[]{:S(2)}, u32[]{:S(2)}) %all-to-all-start) | async-done | bytes 1048608 | tf_op jit(solution)/shard_map/all_to_all | solution.py:80
  42.0 0.0 copy-start.1
  42.0 1.0 copy-done.1
  43.0 2.9 %shard_map.94 = bf16[16,128,128]{2,1,0:T(8,128)(2,1)} custom-call(s32[32]{0:T(128)} %bitcast.47, s32[32]{0:T(128)} %bitcast.49, s32[1]{0:T(128)} %bitcast.39.count_ref, bf16[32,128,128]{2,1,0:T(8,128)(2,1)} %bitcast.41, bf16[32,128,128]{2,1,0:T(8,128)(2,1)} %copy-done.1), custom_call_target="tpu_custom_call" | custom-call | flops 134217728 | bytes 2621440 | tf_op jit(solution)/shard_map/pallas_call | solution.py:46
  45.9 0.0 copy-start.3
  45.9 31.2 %all_to_all.25 = bf16[16,128,128]{2,1,0:T(8,128)(2,1)S(1)} all-to-all(bf16[16,128,128]{2,1,0:T(8,128)(2,1)} %shard_map.94), channel_id=1, replica_groups=mesh['row'=32,'col'=16] {'col'}, dimensions={0} | all-to-all | bytes 1048576 | tf_op jit(solution)/shard_map/all_to_all | solution.py:86
  77.1 0.1 reduce_sum.42
  77.2 0.1 copy.13
  77.3 0.0 copy-done
  77.3 0.0 copy-done.3
  77.3 0.8 fusion.2
  78.1 0.2 convolution_convert_fusion
  78.3 0.2 convert_bitcast_fusion
  78.6 0.1 broadcast_in_dim.27
  78.7 23.1 %all_to_all.26.src_ref = bf16[16,160,128]{2,1,0:T(8,128)(2,1)S(1)} all-to-all(bf16[16,160,128]{2,1,0:T(8,128)(2,1)S(1)} %pad_maximum_fusion), channel_id=1, replica_groups=mesh['row'=32,'col'=16] {'col'}, dimensions={0} | all-to-all | bytes 1310720 | tf_op jit(solution)/shard_map/all_to_all | solution.py:107
  101.8 0.0 copy-start.2
  101.8 0.7 pad_maximum_fusion.2.rest_0_
  102.6 0.1 copy-done.2
  102.7 3.2 %shard_map.95 = bf16[32,160,128]{2,1,0:T(8,128)(2,1)} custom-call(s32[32]{0:T(128)} %bitcast.50, s32[32]{0:T(128)} %bitcast.48, s32[1]{0:T(128)} %bitcast.40.count_ref, bf16[32,128,128]{2,1,0:T(8,128)(2,1)} %bitcast.42, bf16[16,160,128]{2,1,0:T(8,128)(2,1)} %copy-done.2, bf16[32,128]{1,0:T(8,128)(2,1)} %pad_maximum_fusion.2.rest_0_), custom_call_target="tpu_custom_call" | custom-call | flops 134217728 | bytes 3014656 | tf_op jit(solution)/shard_map/pallas_call | solution.py:46
  105.9 40.5 %all_to_all.27 = bf16[32,160,128]{2,1,0:T(8,128)(2,1)S(1)} all-to-all(bf16[32,160,128]{2,1,0:T(8,128)(2,1)} %shard_map.95), channel_id=1, replica_groups=mesh['row'=32,'col'=16] {'row'}, dimensions={0} | all-to-all | bytes 2621440 | tf_op jit(solution)/shard_map/all_to_all | solution.py:117
  146.5 0.7 broadcast_in_dim.29
  147.2 6.0 %all-to-all-start.4 = ((f32[16,8,256]{2,1,0:T(8,128)}), f32[16,8,256]{2,1,0:T(8,128)S(1)}, u32[]{:S(2)}, u32[]{:S(2)}) async-start(f32[16,8,256]{2,1,0:T(8,128)} %broadcast_in_dim.29), calls=%async_computation.4 | async-start | bytes 262144 | tf_op jit(solution)/shard_map/all_to_all | solution.py:123
  153.2 0.8 slice_reduce_fusion
  154.0 9.4 %all-to-all-done.4 = f32[16,8,256]{2,1,0:T(8,128)S(1)} async-done(((f32[16,8,256]{2,1,0:T(8,128)}), f32[16,8,256]{2,1,0:T(8,128)S(1)}, u32[]{:S(2)}, u32[]{:S(2)}) %all-to-all-start.4) | async-done | bytes 131104 | tf_op jit(solution)/shard_map/all_to_all | solution.py:123
  163.4 0.7 copy.17
  (11 shorter events, 0.3 us)
Async XLA Ops:
  0.6 76.7 %copy-start = (bf16[128,256]{1,0:T(8,128)(2,1)S(1)}, bf16[128,256]{1,0:T(8,128)(2,1)}, u32[]{:S(2)}) copy-start(bf16[128,256]{1,0:T(8,128)(2,1)} %param.8) | copy-start | bytes 196612
  2.7 39.3 %all-to-all-start = ((bf16[32,128,128]{2,1,0:T(8,128)(2,1)}), bf16[32,128,128]{2,1,0:T(8,128)(2,1)S(1)}, u32[]{:S(2)}, u32[]{:S(2)}) async-start(bf16[32,128,128]{2,1,0:T(8,128)(2,1)} %broadcast_in_dim.25), calls=%async_computation | async-start | bytes 2097152 | tf_op jit(solution)/shard_map/all_to_all | solution.py:80
  42.0 1.0 copy-start.1
  45.9 31.4 %copy-start.3 = (bf16[1,128,256]{2,1,0:T(8,128)(2,1)S(1)}, bf16[1,128,256]{2,1,0:T(8,128)(2,1)}, u32[]{:S(2)}) copy-start(bf16[1,128,256]{2,1,0:T(8,128)(2,1)} %param.13) | copy-start | bytes 196612
  101.8 0.9 copy-start.2
  147.2 16.2 %all-to-all-start.4 = ((f32[16,8,256]{2,1,0:T(8,128)}), f32[16,8,256]{2,1,0:T(8,128)S(1)}, u32[]{:S(2)}, u32[]{:S(2)}) async-start(f32[16,8,256]{2,1,0:T(8,128)} %broadcast_in_dim.29), calls=%async_computation.4 | async-start | bytes 262144 | tf_op jit(solution)/shard_map/all_to_all | solution.py:123

commit v9 on v8

--- a/solution.py
+++ b/solution.py
@@ -8,12 +8,7 @@
 from jax.sharding import PartitionSpec as P
 
 
-def spread_kernel(transpose, rows_ref, cols_ref, count_ref, tiles_ref, src_ref, *rest):
-    if len(rest) == 3:
-        extra_ref, out_ref, acc_ref = rest
-    else:
-        extra_ref = None
-        out_ref, acc_ref = rest
+def spread_kernel(transpose, carry_words, rows_ref, cols_ref, count_ref, tiles_ref, src_ref, out_ref, acc_ref):
     tb = tiles_ref.shape[1]
     acc_ref[...] = jnp.zeros_like(acc_ref)
     live = count_ref[0]
@@ -26,25 +21,32 @@
         else:
             term = jnp.dot(tile, src, preferred_element_type=jnp.float32)
         acc_ref[rows_ref[t]] += jnp.where(t < live, term, 0.0)
-    if extra_ref is None:
+    if not carry_words:
         out_ref[...] = acc_ref[...].astype(out_ref.dtype)
     else:
         out_ref[:, :tb, :] = acc_ref[...].astype(out_ref.dtype)
-        out_ref[:, tb:, :] = jnp.broadcast_to(extra_ref[...][None], (out_ref.shape[0],) + extra_ref.shape)
+        words = src_ref.shape[1] - tb
+        half = words // 2
+        wg = jnp.zeros((half, src_ref.shape[2]), jnp.float32)
+        for j in range(src_ref.shape[0]):
+            wg = wg + src_ref[j, tb:tb + half, :].astype(jnp.float32)
+            wg = wg + src_ref[j, tb + half:, :].astype(jnp.float32)
+        hi = wg.astype(out_ref.dtype)
+        lo = (wg - hi.astype(jnp.float32)).astype(out_ref.dtype)
+        for j in range(out_ref.shape[0]):
+            out_ref[j, tb:tb + half, :] = hi
+            out_ref[j, tb + half:, :] = lo
 
 
-def spread(tiles, target_ids, source_ids, count, source, out_blocks, transpose, out_dtype, extra=None):
+def spread(tiles, target_ids, source_ids, count, source, out_blocks, transpose, out_dtype, carry_words=False):
     slots, tb, _ = tiles.shape
     width = source.shape[-1]
     smem = pl.BlockSpec(memory_space=pltpu.SMEM)
     vmem = pl.BlockSpec(memory_space=pltpu.VMEM)
     args = [target_ids, source_ids, count.reshape(1), tiles, source]
-    out_rows = tb
-    if extra is not None:
-        args.append(extra)
-        out_rows += extra.shape[0]
+    out_rows = source.shape[1] if carry_words else tb
     return pl.pallas_call(
-        functools.partial(spread_kernel, transpose),
+        functools.partial(spread_kernel, transpose, carry_words),
         out_shape=jax.ShapeDtypeStruct((out_blocks, out_rows, width), out_dtype),
         in_specs=[smem, smem, smem] + [vmem] * (len(args) - 3),
         out_specs=vmem,
@@ -100,19 +102,17 @@
 
     wg_rows = width_in // n_col
     hi, lo = split_f32(local_grad.reshape(n_col, wg_rows, width_out))
-    wg_words = jnp.stack([hi, lo], axis=1).reshape(n_col, -1, width_in)
+    wg_words = jnp.concatenate(
+        [hi.reshape(n_col, -1, width_in), lo.reshape(n_col, -1, width_in)], axis=1
+    )
     payload = jnp.concatenate(
         [jnp.broadcast_to(grad_agg[None], (n_col,) + grad_agg.shape), wg_words], axis=1
     )
     got = lax.all_to_all(payload, "col", 0, 0, tiled=False)
     row_source = got
-    wg_got = got[:, rows_dev:].reshape(n_col, 2, -1, width_in).astype(jnp.float32)
-    wg_col = (wg_got[:, 0] + wg_got[:, 1]).sum(0)
 
-    hi, lo = split_f32(wg_col)
-    wg_words = jnp.concatenate([hi, lo], axis=0)
     payload = spread(
-        tile_block, col_ids, row_ids, tile_total, row_source, col_tiles, True, jnp.bfloat16, wg_words
+        tile_block, col_ids, row_ids, tile_total, row_source, col_tiles, True, jnp.bfloat16, True
     )
     got = lax.all_to_all(payload, "row", 0, 0, tiled=False)
     grad_features = got[:, :rows_dev].astype(jnp.float32).sum(0).astype(jnp.bfloat16)[None]

time: 165 us -> 164 us (level)
  no operation moved by 1% of the time
where the time goes in v9:
time: 164 us
  blocking collectives  94.9 us (58%)
  waiting for transfers between devices  34.6 us (21%)
  starting transfers between devices  20 us (12%)
  Pallas kernels  6.12 us (4%)
  local copies, waits for them, and re-layouts  4.6 us (3%)
    all_to_all x1, blocking collectives, on_device(): got = lax.all_to_all(payload, 'row', 0, 0, tiled=False)  39.9 us
    all_to_all x1, blocking collectives, on_device(): got = lax.all_to_all(sent, 'col', 0, 0, tiled=False)  31.2 us
    all_to_all x1, waiting for transfers between devices, on_device(): lax.all_to_all(jnp.broadcast_to(own[None], (n_row,) + own.shape), 'row',...  25.2 us
    all_to_all x1, blocking collectives, on_device(): got = lax.all_to_all(payload, 'col', 0, 0, tiled=False)  23.8 us
    all_to_all x1, starting transfers between devices, on_device(): lax.all_to_all(jnp.broadcast_to(own[None], (n_row,) + own.shape), 'row',...  13.5 us
    all_to_all x1, waiting for transfers between devices, on_device(): lax.all_to_all(jnp.broadcast_to(wg_part[None], (n_col,) + wg_part.shape),...  9.39 us
    all_to_all x1, starting transfers between devices, on_device(): lax.all_to_all(jnp.broadcast_to(wg_part[None], (n_col,) + wg_part.shape),...  6.57 us
    pallas_call x2, Pallas kernels, spread(): pl.pallas_call(functools.partial(spread_kernel, transpose, carry_words),...  6.12 us
  transfers between devices with their start and end apart: 2, of which 2 were waited for; matrix products, arithmetic and copies ran while one was open for 0% of the time, Pallas kernels for 0%

profile of v9, /device:TPU:1, one launch (start us, length us, event | category | flops | bytes accessed | tf_op | source)
XLA Modules:
  0.0 163.8 jit_solution(8216268795429187325)
XLA Ops:
  0.6 0.0 copy-start
  0.6 2.0 %broadcast_in_dim.25 = bf16[32,128,128]{2,1,0:T(8,128)(2,1)} broadcast(bf16[128,128]{1,0:T(8,128)(2,1)} %bitcast.36), dimensions={1,2} | broadcast | bytes 1081344 | tf_op jit(solution)/shard_map/broadcast_in_dim | solution.py:83
  2.7 13.5 %all-to-all-start = ((bf16[32,128,128]{2,1,0:T(8,128)(2,1)}), bf16[32,128,128]{2,1,0:T(8,128)(2,1)S(1)}, u32[]{:S(2)}, u32[]{:S(2)}) async-start(bf16[32,128,128]{2,1,0:T(8,128)(2,1)} %broadcast_in_dim.25), calls=%async_computation | async-start | bytes 2097152 | tf_op jit(solution)/shard_map/all_to_all | solution.py:82
  16.8 25.2 %all-to-all-done.src_ref = bf16[32,128,128]{2,1,0:T(8,128)(2,1)S(1)} async-done(((bf16[32,128,128]{2,1,0:T(8,128)(2,1)}), bf16[32,128,128]{2,1,0:T(8,128)(2,1)S(1)}, u32[]{:S(2)}, u32[]{:S(2)}) %all-to-all-start) | async-done | bytes 1048608 | tf_op jit(solution)/shard_map/all_to_all | solution.py:82
  42.0 0.0 copy-start.1
  42.0 1.0 copy-done.1
  43.0 2.9 %shard_map.94 = bf16[16,128,128]{2,1,0:T(8,128)(2,1)} custom-call(s32[32]{0:T(128)} %bitcast.38, s32[32]{0:T(128)} %bitcast.40, s32[1]{0:T(128)} %bitcast.30.count_ref, bf16[32,128,128]{2,1,0:T(8,128)(2,1)} %bitcast.32, bf16[32,128,128]{2,1,0:T(8,128)(2,1)} %copy-done.1), custom_call_target="tpu_custom_call" | custom-call | flops 134217728 | bytes 2621440 | tf_op jit(solution)/shard_map/pallas_call | solution.py:48
  45.9 0.0 copy-start.2
  45.9 31.2 %all_to_all.25 = bf16[16,128,128]{2,1,0:T(8,128)(2,1)S(1)} all-to-all(bf16[16,128,128]{2,1,0:T(8,128)(2,1)} %shard_map.94), channel_id=1, replica_groups=mesh['row'=32,'col'=16] {'col'}, dimensions={0} | all-to-all | bytes 1048576 | tf_op jit(solution)/shard_map/all_to_all | solution.py:88
  77.1 0.1 reduce_sum.33
  77.2 0.1 copy.11
  77.3 0.0 copy-done
  77.3 0.0 copy-done.2
  77.3 0.8 fusion.1
  78.1 0.2 convolution_convert_fusion
  78.3 0.2 subtract_convert_fusion
  78.5 0.1 broadcast_in_dim.27
  78.7 23.8 %all_to_all.26.src_ref = bf16[16,160,128]{2,1,0:T(8,128)(2,1)} all-to-all(bf16[16,160,128]{2,1,0:T(8,128)(2,1)S(1)} %pad_maximum_fusion), channel_id=1, replica_groups=mesh['row'=32,'col'=16] {'col'}, dimensions={0} | all-to-all | bytes 1310720 | tf_op jit(solution)/shard_map/all_to_all | solution.py:111
  102.4 3.2 %shard_map.95 = bf16[32,160,128]{2,1,0:T(8,128)(2,1)} custom-call(s32[32]{0:T(128)} %bitcast.41, s32[32]{0:T(128)} %bitcast.39, s32[1]{0:T(128)} %bitcast.31.count_ref, bf16[32,128,128]{2,1,0:T(8,128)(2,1)} %bitcast.33, bf16[16,160,128]{2,1,0:T(8,128)(2,1)} %all_to_all.26.src_ref), custom_call_target="tpu_custom_call" | custom-call | flops 134217728 | bytes 3014656 | tf_op jit(solution)/shard_map/pallas_call | solution.py:48
  105.7 39.9 %all_to_all.27 = bf16[32,160,128]{2,1,0:T(8,128)(2,1)S(1)} all-to-all(bf16[32,160,128]{2,1,0:T(8,128)(2,1)} %shard_map.95), channel_id=1, replica_groups=mesh['row'=32,'col'=16] {'row'}, dimensions={0} | all-to-all | bytes 2621440 | tf_op jit(solution)/shard_map/all_to_all | solution.py:117
  145.7 0.7 broadcast_in_dim.29
  146.4 6.6 %all-to-all-start.4 = ((f32[16,8,256]{2,1,0:T(8,128)}), f32[16,8,256]{2,1,0:T(8,128)S(1)}, u32[]{:S(2)}, u32[]{:S(2)}) async-start(f32[16,8,256]{2,1,0:T(8,128)} %broadcast_in_dim.29), calls=%async_computation.4 | async-start | bytes 262144 | tf_op jit(solution)/shard_map/all_to_all | solution.py:123
  153.0 0.8 slice_reduce_fusion
  153.7 9.4 %all-to-all-done.4 = f32[16,8,256]{2,1,0:T(8,128)S(1)} async-done(((f32[16,8,256]{2,1,0:T(8,128)}), f32[16,8,256]{2,1,0:T(8,128)S(1)}, u32[]{:S(2)}, u32[]{:S(2)}) %all-to-all-start.4) | async-done | bytes 131104 | tf_op jit(solution)/shard_map/all_to_all | solution.py:123
  163.1 0.7 copy.14
  (7 shorter events, 0.2 us)
Async XLA Ops:
  0.6 76.6 %copy-start = (bf16[128,256]{1,0:T(8,128)(2,1)S(1)}, bf16[128,256]{1,0:T(8,128)(2,1)}, u32[]{:S(2)}) copy-start(bf16[128,256]{1,0:T(8,128)(2,1)} %param.8) | copy-start | bytes 196612
  2.7 39.3 %all-to-all-start = ((bf16[32,128,128]{2,1,0:T(8,128)(2,1)}), bf16[32,128,128]{2,1,0:T(8,128)(2,1)S(1)}, u32[]{:S(2)}, u32[]{:S(2)}) async-start(bf16[32,128,128]{2,1,0:T(8,128)(2,1)} %broadcast_in_dim.25), calls=%async_computation | async-start | bytes 2097152 | tf_op jit(solution)/shard_map/all_to_all | solution.py:82
  42.0 1.0 copy-start.1
  45.9 31.4 %copy-start.2 = (bf16[1,128,256]{2,1,0:T(8,128)(2,1)S(1)}, bf16[1,128,256]{2,1,0:T(8,128)(2,1)}, u32[]{:S(2)}) copy-start(bf16[1,128,256]{2,1,0:T(8,128)(2,1)} %param.13) | copy-start | bytes 196612
  146.4 16.7 %all-to-all-start.4 = ((f32[16,8,256]{2,1,0:T(8,128)}), f32[16,8,256]{2,1,0:T(8,128)S(1)}, u32[]{:S(2)}, u32[]{:S(2)}) async-start(f32[16,8,256]{2,1,0:T(8,128)} %broadcast_in_dim.29), calls=%async_computation.4 | async-start | bytes 262144 | tf_op jit(solution)/shard_map/all_to_all | solution.py:123

commit v10 on v9

--- a/solution.py
+++ b/solution.py
@@ -12,15 +12,17 @@
     tb = tiles_ref.shape[1]
     acc_ref[...] = jnp.zeros_like(acc_ref)
     live = count_ref[0]
+    n_src = src_ref.shape[0] - 1
+    n_acc = acc_ref.shape[0] - 1
     for t in range(tiles_ref.shape[0]):
         tile = tiles_ref[t]
-        src = src_ref[cols_ref[t], :tb, :]
+        src = src_ref[jnp.clip(cols_ref[t], 0, n_src), :tb, :]
         if transpose:
             term = lax.dot_general(tile, src, (((0,), (0,)), ((), ())),
                                    preferred_element_type=jnp.float32)
         else:
             term = jnp.dot(tile, src, preferred_element_type=jnp.float32)
-        acc_ref[rows_ref[t]] += jnp.where(t < live, term, 0.0)
+        acc_ref[jnp.clip(rows_ref[t], 0, n_acc)] += jnp.where(t < live, term, 0.0)
     if not carry_words:
         out_ref[...] = acc_ref[...].astype(out_ref.dtype)
     else:

time: 164 us -> 164 us (level)
  no operation moved by 1% of the time
where the time goes in v10:
time: 164 us
  blocking collectives  94.9 us (58%)
  waiting for transfers between devices  34.6 us (21%)
  starting transfers between devices  20.1 us (12%)
  Pallas kernels  6.14 us (4%)
  local copies, waits for them, and re-layouts  4.6 us (3%)
    all_to_all x1, blocking collectives, on_device(): got = lax.all_to_all(payload, 'row', 0, 0, tiled=False)  39.9 us
    all_to_all x1, blocking collectives, on_device(): got = lax.all_to_all(sent, 'col', 0, 0, tiled=False)  31.2 us
    all_to_all x1, waiting for transfers between devices, on_device(): lax.all_to_all(jnp.broadcast_to(own[None], (n_row,) + own.shape), 'row',...  25.2 us
    all_to_all x1, blocking collectives, on_device(): got = lax.all_to_all(payload, 'col', 0, 0, tiled=False)  23.8 us
    all_to_all x1, starting transfers between devices, on_device(): lax.all_to_all(jnp.broadcast_to(own[None], (n_row,) + own.shape), 'row',...  13.5 us
    all_to_all x1, waiting for transfers between devices, on_device(): lax.all_to_all(jnp.broadcast_to(wg_part[None], (n_col,) + wg_part.shape),...  9.39 us
    all_to_all x1, starting transfers between devices, on_device(): lax.all_to_all(jnp.broadcast_to(wg_part[None], (n_col,) + wg_part.shape),...  6.59 us
    pallas_call x2, Pallas kernels, spread(): pl.pallas_call(functools.partial(spread_kernel, transpose, carry_words),...  6.14 us
  transfers between devices with their start and end apart: 2, of which 2 were waited for; matrix products, arithmetic and copies ran while one was open for 0% of the time, Pallas kernels for 0%

profile of v10, /device:TPU:1, one launch (start us, length us, event | category | flops | bytes accessed | tf_op | source)
XLA Modules:
  0.0 163.8 jit_solution(630404657060279621)
XLA Ops:
  0.6 0.0 copy-start
  0.6 2.0 %broadcast_in_dim.25 = bf16[32,128,128]{2,1,0:T(8,128)(2,1)} broadcast(bf16[128,128]{1,0:T(8,128)(2,1)} %bitcast.36), dimensions={1,2} | broadcast | bytes 1081344 | tf_op jit(solution)/shard_map/broadcast_in_dim | solution.py:85
  2.7 13.5 %all-to-all-start = ((bf16[32,128,128]{2,1,0:T(8,128)(2,1)}), bf16[32,128,128]{2,1,0:T(8,128)(2,1)S(1)}, u32[]{:S(2)}, u32[]{:S(2)}) async-start(bf16[32,128,128]{2,1,0:T(8,128)(2,1)} %broadcast_in_dim.25), calls=%async_computation | async-start | bytes 2097152 | tf_op jit(solution)/shard_map/all_to_all | solution.py:84
  16.8 25.2 %all-to-all-done.src_ref = bf16[32,128,128]{2,1,0:T(8,128)(2,1)S(1)} async-done(((bf16[32,128,128]{2,1,0:T(8,128)(2,1)}), bf16[32,128,128]{2,1,0:T(8,128)(2,1)S(1)}, u32[]{:S(2)}, u32[]{:S(2)}) %all-to-all-start) | async-done | bytes 1048608 | tf_op jit(solution)/shard_map/all_to_all | solution.py:84
  42.0 0.0 copy-start.1
  42.0 1.0 copy-done.1
  43.0 2.9 %shard_map.94 = bf16[16,128,128]{2,1,0:T(8,128)(2,1)} custom-call(s32[32]{0:T(128)} %bitcast.38, s32[32]{0:T(128)} %bitcast.40, s32[1]{0:T(128)} %bitcast.30.count_ref, bf16[32,128,128]{2,1,0:T(8,128)(2,1)} %bitcast.32, bf16[32,128,128]{2,1,0:T(8,128)(2,1)} %copy-done.1), custom_call_target="tpu_custom_call" | custom-call | flops 134217728 | bytes 2621440 | tf_op jit(solution)/shard_map/pallas_call | solution.py:50
  45.9 0.0 copy-start.2
  45.9 31.2 %all_to_all.25 = bf16[16,128,128]{2,1,0:T(8,128)(2,1)S(1)} all-to-all(bf16[16,128,128]{2,1,0:T(8,128)(2,1)} %shard_map.94), channel_id=1, replica_groups=mesh['row'=32,'col'=16] {'col'}, dimensions={0} | all-to-all | bytes 1048576 | tf_op jit(solution)/shard_map/all_to_all | solution.py:90
  77.1 0.1 reduce_sum.33
  77.2 0.1 copy.11
  77.3 0.0 copy-done
  77.3 0.0 copy-done.2
  77.3 0.8 fusion.1
  78.1 0.2 convolution_convert_fusion
  78.3 0.2 subtract_convert_fusion
  78.5 0.1 broadcast_in_dim.27
  78.7 23.8 %all_to_all.26.src_ref = bf16[16,160,128]{2,1,0:T(8,128)(2,1)} all-to-all(bf16[16,160,128]{2,1,0:T(8,128)(2,1)S(1)} %pad_maximum_fusion), channel_id=1, replica_groups=mesh['row'=32,'col'=16] {'col'}, dimensions={0} | all-to-all | bytes 1310720 | tf_op jit(solution)/shard_map/all_to_all | solution.py:113
  102.4 3.3 %shard_map.95 = bf16[32,160,128]{2,1,0:T(8,128)(2,1)} custom-call(s32[32]{0:T(128)} %bitcast.41, s32[32]{0:T(128)} %bitcast.39, s32[1]{0:T(128)} %bitcast.31.count_ref, bf16[32,128,128]{2,1,0:T(8,128)(2,1)} %bitcast.33, bf16[16,160,128]{2,1,0:T(8,128)(2,1)} %all_to_all.26.src_ref), custom_call_target="tpu_custom_call" | custom-call | flops 134217728 | bytes 3014656 | tf_op jit(solution)/shard_map/pallas_call | solution.py:50
  105.7 39.9 %all_to_all.27 = bf16[32,160,128]{2,1,0:T(8,128)(2,1)S(1)} all-to-all(bf16[32,160,128]{2,1,0:T(8,128)(2,1)} %shard_map.95), channel_id=1, replica_groups=mesh['row'=32,'col'=16] {'row'}, dimensions={0} | all-to-all | bytes 2621440 | tf_op jit(solution)/shard_map/all_to_all | solution.py:119
  145.7 0.7 broadcast_in_dim.29
  146.4 6.6 %all-to-all-start.4 = ((f32[16,8,256]{2,1,0:T(8,128)}), f32[16,8,256]{2,1,0:T(8,128)S(1)}, u32[]{:S(2)}, u32[]{:S(2)}) async-start(f32[16,8,256]{2,1,0:T(8,128)} %broadcast_in_dim.29), calls=%async_computation.4 | async-start | bytes 262144 | tf_op jit(solution)/shard_map/all_to_all | solution.py:125
  153.0 0.8 slice_reduce_fusion
  153.8 9.4 %all-to-all-done.4 = f32[16,8,256]{2,1,0:T(8,128)S(1)} async-done(((f32[16,8,256]{2,1,0:T(8,128)}), f32[16,8,256]{2,1,0:T(8,128)S(1)}, u32[]{:S(2)}, u32[]{:S(2)}) %all-to-all-start.4) | async-done | bytes 131104 | tf_op jit(solution)/shard_map/all_to_all | solution.py:125
  163.2 0.7 copy.14
  (7 shorter events, 0.2 us)
Async XLA Ops:
  0.6 76.6 %copy-start = (bf16[128,256]{1,0:T(8,128)(2,1)S(1)}, bf16[128,256]{1,0:T(8,128)(2,1)}, u32[]{:S(2)}) copy-start(bf16[128,256]{1,0:T(8,128)(2,1)} %param.8) | copy-start | bytes 196612
  2.7 39.3 %all-to-all-start = ((bf16[32,128,128]{2,1,0:T(8,128)(2,1)}), bf16[32,128,128]{2,1,0:T(8,128)(2,1)S(1)}, u32[]{:S(2)}, u32[]{:S(2)}) async-start(bf16[32,128,128]{2,1,0:T(8,128)(2,1)} %broadcast_in_dim.25), calls=%async_computation | async-start | bytes 2097152 | tf_op jit(solution)/shard_map/all_to_all | solution.py:84
  42.0 1.0 copy-start.1
  45.9 31.4 %copy-start.2 = (bf16[1,128,256]{2,1,0:T(8,128)(2,1)S(1)}, bf16[1,128,256]{2,1,0:T(8,128)(2,1)}, u32[]{:S(2)}) copy-start(bf16[1,128,256]{2,1,0:T(8,128)(2,1)} %param.13) | copy-start | bytes 196612
  146.4 16.7 %all-to-all-start.4 = ((f32[16,8,256]{2,1,0:T(8,128)}), f32[16,8,256]{2,1,0:T(8,128)S(1)}, u32[]{:S(2)}, u32[]{:S(2)}) async-start(f32[16,8,256]{2,1,0:T(8,128)} %broadcast_in_dim.29), calls=%async_computation.4 | async-start | bytes 262144 | tf_op jit(solution)/shard_map/all_to_all | solution.py:125

commit v11 on v10

--- a/solution.py
+++ b/solution.py
@@ -8,13 +8,27 @@
 from jax.sharding import PartitionSpec as P
 
 
-def spread_kernel(transpose, carry_words, rows_ref, cols_ref, count_ref, tiles_ref, src_ref, out_ref, acc_ref):
+def spread_kernel(transpose, carry_words, chunks, rows_ref, cols_ref, count_ref, tiles_any, src_any,
+                  out_ref, acc_ref, tiles_ref, src_ref, sems):
+    slots = tiles_ref.shape[0]
+    per = slots // chunks
+    src_copy = pltpu.make_async_copy(src_any, src_ref, sems.at[chunks])
+    src_copy.start()
+    tile_copies = []
+    for k in range(chunks):
+        part = pl.ds(k * per, per)
+        copy = pltpu.make_async_copy(tiles_any.at[part], tiles_ref.at[part], sems.at[k])
+        copy.start()
+        tile_copies.append(copy)
     tb = tiles_ref.shape[1]
     acc_ref[...] = jnp.zeros_like(acc_ref)
     live = count_ref[0]
     n_src = src_ref.shape[0] - 1
     n_acc = acc_ref.shape[0] - 1
-    for t in range(tiles_ref.shape[0]):
+    src_copy.wait()
+    for t in range(slots):
+        if t % per == 0:
+            tile_copies[t // per].wait()
         tile = tiles_ref[t]
         src = src_ref[jnp.clip(cols_ref[t], 0, n_src), :tb, :]
         if transpose:
@@ -42,17 +56,23 @@
 
 def spread(tiles, target_ids, source_ids, count, source, out_blocks, transpose, out_dtype, carry_words=False):
     slots, tb, _ = tiles.shape
+    chunks = 4 if slots % 4 == 0 else 1
     width = source.shape[-1]
     smem = pl.BlockSpec(memory_space=pltpu.SMEM)
     vmem = pl.BlockSpec(memory_space=pltpu.VMEM)
     args = [target_ids, source_ids, count.reshape(1), tiles, source]
     out_rows = source.shape[1] if carry_words else tb
     return pl.pallas_call(
-        functools.partial(spread_kernel, transpose, carry_words),
+        functools.partial(spread_kernel, transpose, carry_words, chunks),
         out_shape=jax.ShapeDtypeStruct((out_blocks, out_rows, width), out_dtype),
-        in_specs=[smem, smem, smem] + [vmem] * (len(args) - 3),
+        in_specs=[smem, smem, smem, pl.BlockSpec(memory_space=pl.ANY), pl.BlockSpec(memory_space=pl.ANY)],
         out_specs=vmem,
-        scratch_shapes=[pltpu.VMEM((out_blocks, tb, width), jnp.float32)],
+        scratch_shapes=[
+            pltpu.VMEM((out_blocks, tb, width), jnp.float32),
+            pltpu.VMEM(tiles.shape, tiles.dtype),
+            pltpu.VMEM(source.shape, source.dtype),
+            pltpu.SemaphoreType.DMA((chunks + 1,)),
+        ],
         cost_estimate=pl.CostEstimate(
             flops=2 * slots * tb * tb * width, transcendentals=0,
             bytes_accessed=tiles.size * 2 + source.size * 2 + out_blocks * out_rows * width * 2),

time: 164 us -> 166 us (1.012)
  Pallas kernels: 6.14 us -> 7.97 us
    pallas_call x2, Pallas kernels: 6.14 us -> 7.97 us  [spread(): pl.pallas_call(functools.partial(spread_kernel, transpose, carry_words, c...]
where the time goes in v11:
time: 166 us
  blocking collectives  95 us (57%)
  waiting for transfers between devices  34.6 us (21%)
  starting transfers between devices  20 us (12%)
  Pallas kernels  7.97 us (5%)
  local copies, waits for them, and re-layouts  4.6 us (3%)
    all_to_all x1, blocking collectives, on_device(): got = lax.all_to_all(payload, 'row', 0, 0, tiled=False)  40 us
    all_to_all x1, blocking collectives, on_device(): got = lax.all_to_all(sent, 'col', 0, 0, tiled=False)  31.2 us
    all_to_all x1, waiting for transfers between devices, on_device(): lax.all_to_all(jnp.broadcast_to(own[None], (n_row,) + own.shape), 'row',...  25.2 us
    all_to_all x1, blocking collectives, on_device(): got = lax.all_to_all(payload, 'col', 0, 0, tiled=False)  23.8 us
    all_to_all x1, starting transfers between devices, on_device(): lax.all_to_all(jnp.broadcast_to(own[None], (n_row,) + own.shape), 'row',...  13.5 us
    all_to_all x1, waiting for transfers between devices, on_device(): lax.all_to_all(jnp.broadcast_to(wg_part[None], (n_col,) + wg_part.shape),...  9.39 us
    pallas_call x2, Pallas kernels, spread(): pl.pallas_call(functools.partial(spread_kernel, transpose, carry_words, c...  7.97 us
    all_to_all x1, starting transfers between devices, on_device(): lax.all_to_all(jnp.broadcast_to(wg_part[None], (n_col,) + wg_part.shape),...  6.57 us
  transfers between devices with their start and end apart: 2, of which 2 were waited for; matrix products, arithmetic and copies ran while one was open for 0% of the time, Pallas kernels for 0%

profile of v11, /device:TPU:1, one launch (start us, length us, event | category | flops | bytes accessed | tf_op | source)
XLA Modules:
  0.0 165.7 jit_solution(18017766536940337758)
XLA Ops:
  0.6 0.0 copy-start
  0.6 2.0 %broadcast_in_dim.25 = bf16[32,128,128]{2,1,0:T(8,128)(2,1)} broadcast(bf16[128,128]{1,0:T(8,128)(2,1)} %bitcast.36), dimensions={1,2} | broadcast | bytes 1081344 | tf_op jit(solution)/shard_map/broadcast_in_dim | solution.py:105
  2.7 13.5 %all-to-all-start = ((bf16[32,128,128]{2,1,0:T(8,128)(2,1)}), bf16[32,128,128]{2,1,0:T(8,128)(2,1)S(1)}, u32[]{:S(2)}, u32[]{:S(2)}) async-start(bf16[32,128,128]{2,1,0:T(8,128)(2,1)} %broadcast_in_dim.25), calls=%async_computation | async-start | bytes 2097152 | tf_op jit(solution)/shard_map/all_to_all | solution.py:104
  16.8 25.2 %all-to-all-done.src_any = bf16[32,128,128]{2,1,0:T(8,128)(2,1)S(1)} async-done(((bf16[32,128,128]{2,1,0:T(8,128)(2,1)}), bf16[32,128,128]{2,1,0:T(8,128)(2,1)S(1)}, u32[]{:S(2)}, u32[]{:S(2)}) %all-to-all-start) | async-done | bytes 1048608 | tf_op jit(solution)/shard_map/all_to_all | solution.py:104
  42.0 0.0 copy-start.1
  42.0 1.0 copy-done.1
  43.0 3.8 %shard_map.94 = bf16[16,128,128]{2,1,0:T(8,128)(2,1)} custom-call(s32[32]{0:T(128)} %bitcast.38, s32[32]{0:T(128)} %bitcast.40, s32[1]{0:T(128)} %bitcast.30.count_ref, bf16[32,128,128]{2,1,0:T(8,128)(2,1)} %bitcast.32, bf16[32,128,128]{2,1,0:T(8,128)(2,1)} %copy-done.1), custom_call_target="tpu_custom_call" | custom-call | flops 134217728 | bytes 2621440 | tf_op jit(solution)/shard_map/pallas_call | solution.py:65
  46.8 0.0 copy-start.2
  46.8 31.2 %all_to_all.25 = bf16[16,128,128]{2,1,0:T(8,128)(2,1)S(1)} all-to-all(bf16[16,128,128]{2,1,0:T(8,128)(2,1)} %shard_map.94), channel_id=1, replica_groups=mesh['row'=32,'col'=16] {'col'}, dimensions={0} | all-to-all | bytes 1048576 | tf_op jit(solution)/shard_map/all_to_all | solution.py:110
  78.0 0.1 reduce_sum.33
  78.1 0.1 copy.11
  78.2 0.0 copy-done
  78.2 0.0 copy-done.2
  78.2 0.8 fusion.1
  79.1 0.2 convolution_convert_fusion
  79.2 0.2 subtract_convert_fusion
  79.5 0.1 broadcast_in_dim.27
  79.6 23.8 %all_to_all.26.src_any = bf16[16,160,128]{2,1,0:T(8,128)(2,1)} all-to-all(bf16[16,160,128]{2,1,0:T(8,128)(2,1)S(1)} %pad_maximum_fusion), channel_id=1, replica_groups=mesh['row'=32,'col'=16] {'col'}, dimensions={0} | all-to-all | bytes 1310720 | tf_op jit(solution)/shard_map/all_to_all | solution.py:133
  103.4 4.2 %shard_map.95 = bf16[32,160,128]{2,1,0:T(8,128)(2,1)} custom-call(s32[32]{0:T(128)} %bitcast.41, s32[32]{0:T(128)} %bitcast.39, s32[1]{0:T(128)} %bitcast.31.count_ref, bf16[32,128,128]{2,1,0:T(8,128)(2,1)} %bitcast.33, bf16[16,160,128]{2,1,0:T(8,128)(2,1)} %all_to_all.26.src_any), custom_call_target="tpu_custom_call" | custom-call | flops 134217728 | bytes 3014656 | tf_op jit(solution)/shard_map/pallas_call | solution.py:65
  107.6 40.0 %all_to_all.27 = bf16[32,160,128]{2,1,0:T(8,128)(2,1)S(1)} all-to-all(bf16[32,160,128]{2,1,0:T(8,128)(2,1)} %shard_map.95), channel_id=1, replica_groups=mesh['row'=32,'col'=16] {'row'}, dimensions={0} | all-to-all | bytes 2621440 | tf_op jit(solution)/shard_map/all_to_all | solution.py:139
  147.7 0.7 broadcast_in_dim.29
  148.3 6.6 %all-to-all-start.4 = ((f32[16,8,256]{2,1,0:T(8,128)}), f32[16,8,256]{2,1,0:T(8,128)S(1)}, u32[]{:S(2)}, u32[]{:S(2)}) async-start(f32[16,8,256]{2,1,0:T(8,128)} %broadcast_in_dim.29), calls=%async_computation.4 | async-start | bytes 262144 | tf_op jit(solution)/shard_map/all_to_all | solution.py:145
  154.9 0.8 slice_reduce_fusion
  155.6 9.4 %all-to-all-done.4 = f32[16,8,256]{2,1,0:T(8,128)S(1)} async-done(((f32[16,8,256]{2,1,0:T(8,128)}), f32[16,8,256]{2,1,0:T(8,128)S(1)}, u32[]{:S(2)}, u32[]{:S(2)}) %all-to-all-start.4) | async-done | bytes 131104 | tf_op jit(solution)/shard_map/all_to_all | solution.py:145
  165.0 0.7 copy.14
  (7 shorter events, 0.2 us)
Async XLA Ops:
  0.6 77.6 %copy-start = (bf16[128,256]{1,0:T(8,128)(2,1)S(1)}, bf16[128,256]{1,0:T(8,128)(2,1)}, u32[]{:S(2)}) copy-start(bf16[128,256]{1,0:T(8,128)(2,1)} %param.8) | copy-start | bytes 196612
  2.7 39.3 %all-to-all-start = ((bf16[32,128,128]{2,1,0:T(8,128)(2,1)}), bf16[32,128,128]{2,1,0:T(8,128)(2,1)S(1)}, u32[]{:S(2)}, u32[]{:S(2)}) async-start(bf16[32,128,128]{2,1,0:T(8,128)(2,1)} %broadcast_in_dim.25), calls=%async_computation | async-start | bytes 2097152 | tf_op jit(solution)/shard_map/all_to_all | solution.py:104
  42.0 1.0 copy-start.1
  46.8 31.4 %copy-start.2 = (bf16[1,128,256]{2,1,0:T(8,128)(2,1)S(1)}, bf16[1,128,256]{2,1,0:T(8,128)(2,1)}, u32[]{:S(2)}) copy-start(bf16[1,128,256]{2,1,0:T(8,128)(2,1)} %param.13) | copy-start | bytes 196612
  148.3 16.7 %all-to-all-start.4 = ((f32[16,8,256]{2,1,0:T(8,128)}), f32[16,8,256]{2,1,0:T(8,128)S(1)}, u32[]{:S(2)}, u32[]{:S(2)}) async-start(f32[16,8,256]{2,1,0:T(8,128)} %broadcast_in_dim.29), calls=%async_computation.4 | async-start | bytes 262144 | tf_op jit(solution)/shard_map/all_to_all | solution.py:145

commit v12 on v10

--- a/solution.py
+++ b/solution.py
@@ -27,17 +27,12 @@
         out_ref[...] = acc_ref[...].astype(out_ref.dtype)
     else:
         out_ref[:, :tb, :] = acc_ref[...].astype(out_ref.dtype)
-        words = src_ref.shape[1] - tb
-        half = words // 2
-        wg = jnp.zeros((half, src_ref.shape[2]), jnp.float32)
+        wg = jnp.zeros((src_ref.shape[1] - tb, src_ref.shape[2]), jnp.float32)
         for j in range(src_ref.shape[0]):
-            wg = wg + src_ref[j, tb:tb + half, :].astype(jnp.float32)
-            wg = wg + src_ref[j, tb + half:, :].astype(jnp.float32)
-        hi = wg.astype(out_ref.dtype)
-        lo = (wg - hi.astype(jnp.float32)).astype(out_ref.dtype)
+            wg = wg + src_ref[j, tb:, :].astype(jnp.float32)
+        words = wg.astype(out_ref.dtype)
         for j in range(out_ref.shape[0]):
-            out_ref[j, tb:tb + half, :] = hi
-            out_ref[j, tb + half:, :] = lo
+            out_ref[j, tb:, :] = words
 
 
 def spread(tiles, target_ids, source_ids, count, source, out_blocks, transpose, out_dtype, carry_words=False):
@@ -57,12 +52,6 @@
             flops=2 * slots * tb * tb * width, transcendentals=0,
             bytes_accessed=tiles.size * 2 + source.size * 2 + out_blocks * out_rows * width * 2),
     )(*args)
-
-
-def split_f32(x):
-    hi = x.astype(jnp.bfloat16)
-    lo = (x - hi.astype(jnp.float32)).astype(jnp.bfloat16)
-    return hi, lo
 
 
 def on_device(features, weight, tile_values, tile_rows, tile_cols, tile_count, cotangent):
@@ -103,10 +92,7 @@
     ).astype(jnp.bfloat16)
 
     wg_rows = width_in // n_col
-    hi, lo = split_f32(local_grad.reshape(n_col, wg_rows, width_out))
-    wg_words = jnp.concatenate(
-        [hi.reshape(n_col, -1, width_in), lo.reshape(n_col, -1, width_in)], axis=1
-    )
+    wg_words = local_grad.reshape(n_col, -1, width_in).astype(jnp.bfloat16)
     payload = jnp.concatenate(
         [jnp.broadcast_to(grad_agg[None], (n_col,) + grad_agg.shape), wg_words], axis=1
     )
@@ -118,8 +104,7 @@
     )
     got = lax.all_to_all(payload, "row", 0, 0, tiled=False)
     grad_features = got[:, :rows_dev].astype(jnp.float32).sum(0).astype(jnp.bfloat16)[None]
-    wg_got = got[:, rows_dev:].reshape(n_row, 2, -1, width_in).astype(jnp.float32)
-    wg_part = (wg_got[:, 0] + wg_got[:, 1]).sum(0) * node_total ** (-0.5)
+    wg_part = got[:, rows_dev:].astype(jnp.float32).sum(0) * node_total ** (-0.5)
     wg_part = wg_part.reshape(wg_rows, width_out)
 
     everyone = lax.all_to_all(

time: 164 us -> 161 us (0.982)
  blocking collectives: 94.9 us -> 92.6 us
where the time goes in v12:
time: 161 us; the launch traced here: 160 us
  blocking collectives  92.6 us (58%)
  waiting for transfers between devices  34.7 us (22%)
  starting transfers between devices  19 us (12%)
  Pallas kernels  6.04 us (4%)
  local copies, waits for them, and re-layouts  4.47 us (3%)
    all_to_all x1, blocking collectives, on_device(): got = lax.all_to_all(payload, 'row', 0, 0, tiled=False)  39 us
    all_to_all x1, blocking collectives, on_device(): got = lax.all_to_all(sent, 'col', 0, 0, tiled=False)  31.2 us
    all_to_all x1, waiting for transfers between devices, on_device(): lax.all_to_all(jnp.broadcast_to(own[None], (n_row,) + own.shape), 'row',...  25.2 us
    all_to_all x1, blocking collectives, on_device(): got = lax.all_to_all(payload, 'col', 0, 0, tiled=False)  22.4 us
    all_to_all x1, starting transfers between devices, on_device(): lax.all_to_all(jnp.broadcast_to(own[None], (n_row,) + own.shape), 'row',...  13.5 us
    all_to_all x1, waiting for transfers between devices, on_device(): lax.all_to_all(jnp.broadcast_to(wg_part[None], (n_col,) + wg_part.shape),...  9.44 us
    pallas_call x2, Pallas kernels, spread(): pl.pallas_call(functools.partial(spread_kernel, transpose, carry_words),...  6.04 us
    all_to_all x1, starting transfers between devices, on_device(): lax.all_to_all(jnp.broadcast_to(wg_part[None], (n_col,) + wg_part.shape),...  5.56 us
  transfers between devices with their start and end apart: 2, of which 2 were waited for; matrix products, arithmetic and copies ran while one was open for 0% of the time, Pallas kernels for 0%

profile of v12, /device:TPU:1, one launch (start us, length us, event | category | flops | bytes accessed | tf_op | source)
XLA Modules:
  0.0 160.3 jit_solution(4008302719307805486)
XLA Ops:
  0.6 0.0 copy-start
  0.6 2.0 %broadcast_in_dim.25 = bf16[32,128,128]{2,1,0:T(8,128)(2,1)} broadcast(bf16[128,128]{1,0:T(8,128)(2,1)} %bitcast.23), dimensions={1,2} | broadcast | bytes 1081344 | tf_op jit(solution)/shard_map/broadcast_in_dim | solution.py:74
  2.7 13.5 %all-to-all-start = ((bf16[32,128,128]{2,1,0:T(8,128)(2,1)}), bf16[32,128,128]{2,1,0:T(8,128)(2,1)S(1)}, u32[]{:S(2)}, u32[]{:S(2)}) async-start(bf16[32,128,128]{2,1,0:T(8,128)(2,1)} %broadcast_in_dim.25), calls=%async_computation | async-start | bytes 2097152 | tf_op jit(solution)/shard_map/all_to_all | solution.py:73
  16.8 25.2 %all-to-all-done.src_ref = bf16[32,128,128]{2,1,0:T(8,128)(2,1)S(1)} async-done(((bf16[32,128,128]{2,1,0:T(8,128)(2,1)}), bf16[32,128,128]{2,1,0:T(8,128)(2,1)S(1)}, u32[]{:S(2)}, u32[]{:S(2)}) %all-to-all-start) | async-done | bytes 1048608 | tf_op jit(solution)/shard_map/all_to_all | solution.py:73
  42.0 0.0 copy-start.1
  42.0 1.0 copy-done.1
  43.0 2.9 %shard_map.94 = bf16[16,128,128]{2,1,0:T(8,128)(2,1)} custom-call(s32[32]{0:T(128)} %bitcast.25, s32[32]{0:T(128)} %bitcast.27, s32[1]{0:T(128)} %bitcast.18.count_ref, bf16[32,128,128]{2,1,0:T(8,128)(2,1)} %bitcast.20, bf16[32,128,128]{2,1,0:T(8,128)(2,1)} %copy-done.1), custom_call_target="tpu_custom_call" | custom-call | flops 134217728 | bytes 2621440 | tf_op jit(solution)/shard_map/pallas_call | solution.py:45
  45.9 0.0 copy-start.2
  45.9 31.2 %all_to_all.25 = bf16[16,128,128]{2,1,0:T(8,128)(2,1)S(1)} all-to-all(bf16[16,128,128]{2,1,0:T(8,128)(2,1)} %shard_map.94), channel_id=1, replica_groups=mesh['row'=32,'col'=16] {'col'}, dimensions={0} | all-to-all | bytes 1048576 | tf_op jit(solution)/shard_map/all_to_all | solution.py:79
  77.1 0.1 reduce_sum.33
  77.2 0.0 copy-done
  77.2 0.0 copy-done.2
  77.2 0.8 fusion
  78.0 0.2 convolution_convert_fusion
  78.2 0.2 convolution_convert_fusion.1
  78.4 0.1 broadcast_in_dim.27
  78.6 22.4 %all_to_all.26.src_ref = bf16[16,144,128]{2,1,0:T(8,128)(2,1)} all-to-all(bf16[16,144,128]{2,1,0:T(8,128)(2,1)S(1)} %pad_maximum_fusion), channel_id=1, replica_groups=mesh['row'=32,'col'=16] {'col'}, dimensions={0} | all-to-all | bytes 1179648 | tf_op jit(solution)/shard_map/all_to_all | solution.py:99
  100.9 3.2 %shard_map.95 = bf16[32,144,128]{2,1,0:T(8,128)(2,1)} custom-call(s32[32]{0:T(128)} %bitcast.28, s32[32]{0:T(128)} %bitcast.26, s32[1]{0:T(128)} %bitcast.19.count_ref, bf16[32,128,128]{2,1,0:T(8,128)(2,1)} %bitcast.21, bf16[16,144,128]{2,1,0:T(8,128)(2,1)} %all_to_all.26.src_ref), custom_call_target="tpu_custom_call" | custom-call | flops 134217728 | bytes 2818048 | tf_op jit(solution)/shard_map/pallas_call | solution.py:45
  104.1 39.0 %all_to_all.27 = bf16[32,144,128]{2,1,0:T(8,128)(2,1)S(1)} all-to-all(bf16[32,144,128]{2,1,0:T(8,128)(2,1)} %shard_map.95), channel_id=1, replica_groups=mesh['row'=32,'col'=16] {'row'}, dimensions={0} | all-to-all | bytes 2359296 | tf_op jit(solution)/shard_map/all_to_all | solution.py:105
  143.2 0.7 broadcast_in_dim.29
  143.9 5.6 %all-to-all-start.4 = ((f32[16,8,256]{2,1,0:T(8,128)}), f32[16,8,256]{2,1,0:T(8,128)S(1)}, u32[]{:S(2)}, u32[]{:S(2)}) async-start(f32[16,8,256]{2,1,0:T(8,128)} %broadcast_in_dim.29), calls=%async_computation.4 | async-start | bytes 262144 | tf_op jit(solution)/shard_map/all_to_all | solution.py:110
  149.4 0.8 slice_reduce_fusion
  150.2 9.4 %all-to-all-done.4 = f32[16,8,256]{2,1,0:T(8,128)S(1)} async-done(((f32[16,8,256]{2,1,0:T(8,128)}), f32[16,8,256]{2,1,0:T(8,128)S(1)}, u32[]{:S(2)}, u32[]{:S(2)}) %all-to-all-start.4) | async-done | bytes 131104 | tf_op jit(solution)/shard_map/all_to_all | solution.py:110
  159.6 0.7 copy.12
  (5 shorter events, 0.1 us)
Async XLA Ops:
  0.6 76.5 %copy-start = (bf16[128,256]{1,0:T(8,128)(2,1)S(1)}, bf16[128,256]{1,0:T(8,128)(2,1)}, u32[]{:S(2)}) copy-start(bf16[128,256]{1,0:T(8,128)(2,1)} %param.8) | copy-start | bytes 196612
  2.7 39.3 %all-to-all-start = ((bf16[32,128,128]{2,1,0:T(8,128)(2,1)}), bf16[32,128,128]{2,1,0:T(8,128)(2,1)S(1)}, u32[]{:S(2)}, u32[]{:S(2)}) async-start(bf16[32,128,128]{2,1,0:T(8,128)(2,1)} %broadcast_in_dim.25), calls=%async_computation | async-start | bytes 2097152 | tf_op jit(solution)/shard_map/all_to_all | solution.py:73
  42.0 1.0 copy-start.1
  45.9 31.3 %copy-start.2 = (bf16[1,128,256]{2,1,0:T(8,128)(2,1)S(1)}, bf16[1,128,256]{2,1,0:T(8,128)(2,1)}, u32[]{:S(2)}) copy-start(bf16[1,128,256]{2,1,0:T(8,128)(2,1)} %param.13) | copy-start | bytes 196612
  143.9 15.8 %all-to-all-start.4 = ((f32[16,8,256]{2,1,0:T(8,128)}), f32[16,8,256]{2,1,0:T(8,128)S(1)}, u32[]{:S(2)}, u32[]{:S(2)}) async-start(f32[16,8,256]{2,1,0:T(8,128)} %broadcast_in_dim.29), calls=%async_computation.4 | async-start | bytes 262144 | tf_op jit(solution)/shard_map/all_to_all | solution.py:110

commit v13 on v12

--- a/solution.py
+++ b/solution.py
@@ -14,15 +14,21 @@
     live = count_ref[0]
     n_src = src_ref.shape[0] - 1
     n_acc = acc_ref.shape[0] - 1
-    for t in range(tiles_ref.shape[0]):
-        tile = tiles_ref[t]
-        src = src_ref[jnp.clip(cols_ref[t], 0, n_src), :tb, :]
-        if transpose:
-            term = lax.dot_general(tile, src, (((0,), (0,)), ((), ())),
-                                   preferred_element_type=jnp.float32)
-        else:
-            term = jnp.dot(tile, src, preferred_element_type=jnp.float32)
-        acc_ref[jnp.clip(rows_ref[t], 0, n_acc)] += jnp.where(t < live, term, 0.0)
+    slots = tiles_ref.shape[0]
+    group = 2 if slots % 2 == 0 else 1
+    for first in range(0, slots, group):
+        terms = []
+        for t in range(first, first + group):
+            tile = tiles_ref[t]
+            src = src_ref[jnp.clip(cols_ref[t], 0, n_src), :tb, :]
+            if transpose:
+                term = lax.dot_general(tile, src, (((0,), (0,)), ((), ())),
+                                       preferred_element_type=jnp.float32)
+            else:
+                term = jnp.dot(tile, src, preferred_element_type=jnp.float32)
+            terms.append(jnp.where(t < live, term, 0.0))
+        for t, term in zip(range(first, first + group), terms):
+            acc_ref[jnp.clip(rows_ref[t], 0, n_acc)] += term
     if not carry_words:
         out_ref[...] = acc_ref[...].astype(out_ref.dtype)
     else:

time: 161 us -> 161 us (level)
  no operation moved by 1% of the time
where the time goes in v13:
time: 161 us; the launch traced here: 160 us
  blocking collectives  92.6 us (58%)
  waiting for transfers between devices  34.7 us (22%)
  starting transfers between devices  19 us (12%)
  Pallas kernels  6.03 us (4%)
  local copies, waits for them, and re-layouts  4.47 us (3%)
    all_to_all x1, blocking collectives, on_device(): got = lax.all_to_all(payload, 'row', 0, 0, tiled=False)  39.1 us
    all_to_all x1, blocking collectives, on_device(): got = lax.all_to_all(sent, 'col', 0, 0, tiled=False)  31.2 us
    all_to_all x1, waiting for transfers between devices, on_device(): lax.all_to_all(jnp.broadcast_to(own[None], (n_row,) + own.shape), 'row',...  25.2 us
    all_to_all x1, blocking collectives, on_device(): got = lax.all_to_all(payload, 'col', 0, 0, tiled=False)  22.4 us
    all_to_all x1, starting transfers between devices, on_device(): lax.all_to_all(jnp.broadcast_to(own[None], (n_row,) + own.shape), 'row',...  13.5 us
    all_to_all x1, waiting for transfers between devices, on_device(): lax.all_to_all(jnp.broadcast_to(wg_part[None], (n_col,) + wg_part.shape),...  9.44 us
    pallas_call x2, Pallas kernels, spread(): pl.pallas_call(functools.partial(spread_kernel, transpose, carry_words),...  6.03 us
    all_to_all x1, starting transfers between devices, on_device(): lax.all_to_all(jnp.broadcast_to(wg_part[None], (n_col,) + wg_part.shape),...  5.54 us
  transfers between devices with their start and end apart: 2, of which 2 were waited for; matrix products, arithmetic and copies ran while one was open for 0% of the time, Pallas kernels for 0%

profile of v13, /device:TPU:1, one launch (start us, length us, event | category | flops | bytes accessed | tf_op | source)
XLA Modules:
  0.0 160.3 jit_solution(4096173392090522677)
XLA Ops:
  0.6 0.0 copy-start
  0.6 2.0 %broadcast_in_dim.25 = bf16[32,128,128]{2,1,0:T(8,128)(2,1)} broadcast(bf16[128,128]{1,0:T(8,128)(2,1)} %bitcast.23), dimensions={1,2} | broadcast | bytes 1081344 | tf_op jit(solution)/shard_map/broadcast_in_dim | solution.py:80
  2.7 13.5 %all-to-all-start = ((bf16[32,128,128]{2,1,0:T(8,128)(2,1)}), bf16[32,128,128]{2,1,0:T(8,128)(2,1)S(1)}, u32[]{:S(2)}, u32[]{:S(2)}) async-start(bf16[32,128,128]{2,1,0:T(8,128)(2,1)} %broadcast_in_dim.25), calls=%async_computation | async-start | bytes 2097152 | tf_op jit(solution)/shard_map/all_to_all | solution.py:79
  16.8 25.2 %all-to-all-done.src_ref = bf16[32,128,128]{2,1,0:T(8,128)(2,1)S(1)} async-done(((bf16[32,128,128]{2,1,0:T(8,128)(2,1)}), bf16[32,128,128]{2,1,0:T(8,128)(2,1)S(1)}, u32[]{:S(2)}, u32[]{:S(2)}) %all-to-all-start) | async-done | bytes 1048608 | tf_op jit(solution)/shard_map/all_to_all | solution.py:79
  42.0 0.0 copy-start.1
  42.0 1.0 copy-done.1
  43.0 2.9 %shard_map.94 = bf16[16,128,128]{2,1,0:T(8,128)(2,1)} custom-call(s32[32]{0:T(128)} %bitcast.25, s32[32]{0:T(128)} %bitcast.27, s32[1]{0:T(128)} %bitcast.18.count_ref, bf16[32,128,128]{2,1,0:T(8,128)(2,1)} %bitcast.20, bf16[32,128,128]{2,1,0:T(8,128)(2,1)} %copy-done.1), custom_call_target="tpu_custom_call" | custom-call | flops 134217728 | bytes 2621440 | tf_op jit(solution)/shard_map/pallas_call | solution.py:51
  45.9 0.0 copy-start.2
  45.9 31.2 %all_to_all.25 = bf16[16,128,128]{2,1,0:T(8,128)(2,1)S(1)} all-to-all(bf16[16,128,128]{2,1,0:T(8,128)(2,1)} %shard_map.94), channel_id=1, replica_groups=mesh['row'=32,'col'=16] {'col'}, dimensions={0} | all-to-all | bytes 1048576 | tf_op jit(solution)/shard_map/all_to_all | solution.py:85
  77.1 0.1 reduce_sum.33
  77.2 0.0 copy-done
  77.2 0.0 copy-done.2
  77.2 0.8 fusion
  78.0 0.2 convolution_convert_fusion
  78.2 0.2 convolution_convert_fusion.1
  78.4 0.1 broadcast_in_dim.27
  78.6 22.4 %all_to_all.26.src_ref = bf16[16,144,128]{2,1,0:T(8,128)(2,1)} all-to-all(bf16[16,144,128]{2,1,0:T(8,128)(2,1)S(1)} %pad_maximum_fusion), channel_id=1, replica_groups=mesh['row'=32,'col'=16] {'col'}, dimensions={0} | all-to-all | bytes 1179648 | tf_op jit(solution)/shard_map/all_to_all | solution.py:105
  100.9 3.1 %shard_map.95 = bf16[32,144,128]{2,1,0:T(8,128)(2,1)} custom-call(s32[32]{0:T(128)} %bitcast.28, s32[32]{0:T(128)} %bitcast.26, s32[1]{0:T(128)} %bitcast.19.count_ref, bf16[32,128,128]{2,1,0:T(8,128)(2,1)} %bitcast.21, bf16[16,144,128]{2,1,0:T(8,128)(2,1)} %all_to_all.26.src_ref), custom_call_target="tpu_custom_call" | custom-call | flops 134217728 | bytes 2818048 | tf_op jit(solution)/shard_map/pallas_call | solution.py:51
  104.1 39.1 %all_to_all.27 = bf16[32,144,128]{2,1,0:T(8,128)(2,1)S(1)} all-to-all(bf16[32,144,128]{2,1,0:T(8,128)(2,1)} %shard_map.95), channel_id=1, replica_groups=mesh['row'=32,'col'=16] {'row'}, dimensions={0} | all-to-all | bytes 2359296 | tf_op jit(solution)/shard_map/all_to_all | solution.py:111
  143.2 0.7 broadcast_in_dim.29
  143.9 5.5 %all-to-all-start.4 = ((f32[16,8,256]{2,1,0:T(8,128)}), f32[16,8,256]{2,1,0:T(8,128)S(1)}, u32[]{:S(2)}, u32[]{:S(2)}) async-start(f32[16,8,256]{2,1,0:T(8,128)} %broadcast_in_dim.29), calls=%async_computation.4 | async-start | bytes 262144 | tf_op jit(solution)/shard_map/all_to_all | solution.py:116
  149.4 0.8 slice_reduce_fusion
  150.2 9.4 %all-to-all-done.4 = f32[16,8,256]{2,1,0:T(8,128)S(1)} async-done(((f32[16,8,256]{2,1,0:T(8,128)}), f32[16,8,256]{2,1,0:T(8,128)S(1)}, u32[]{:S(2)}, u32[]{:S(2)}) %all-to-all-start.4) | async-done | bytes 131104 | tf_op jit(solution)/shard_map/all_to_all | solution.py:116
  159.6 0.7 copy.12
  (5 shorter events, 0.1 us)
Async XLA Ops:
  0.6 76.5 %copy-start = (bf16[128,256]{1,0:T(8,128)(2,1)S(1)}, bf16[128,256]{1,0:T(8,128)(2,1)}, u32[]{:S(2)}) copy-start(bf16[128,256]{1,0:T(8,128)(2,1)} %param.8) | copy-start | bytes 196612
  2.7 39.3 %all-to-all-start = ((bf16[32,128,128]{2,1,0:T(8,128)(2,1)}), bf16[32,128,128]{2,1,0:T(8,128)(2,1)S(1)}, u32[]{:S(2)}, u32[]{:S(2)}) async-start(bf16[32,128,128]{2,1,0:T(8,128)(2,1)} %broadcast_in_dim.25), calls=%async_computation | async-start | bytes 2097152 | tf_op jit(solution)/shard_map/all_to_all | solution.py:79
  42.0 1.0 copy-start.1
  45.9 31.3 %copy-start.2 = (bf16[1,128,256]{2,1,0:T(8,128)(2,1)S(1)}, bf16[1,128,256]{2,1,0:T(8,128)(2,1)}, u32[]{:S(2)}) copy-start(bf16[1,128,256]{2,1,0:T(8,128)(2,1)} %param.13) | copy-start | bytes 196612
  143.9 15.8 %all-to-all-start.4 = ((f32[16,8,256]{2,1,0:T(8,128)}), f32[16,8,256]{2,1,0:T(8,128)S(1)}, u32[]{:S(2)}, u32[]{:S(2)}) async-start(f32[16,8,256]{2,1,0:T(8,128)} %broadcast_in_dim.29), calls=%async_computation.4 | async-start | bytes 262144 | tf_op jit(solution)/shard_map/all_to_all | solution.py:116

commit v14 on v13

--- a/solution.py
+++ b/solution.py
@@ -60,6 +60,49 @@
     )(*args)
 
 
+def dense_kernel(recv_ref, w_ref, cot_ref, out_ref, pay_ref):
+    agg = recv_ref[...].astype(jnp.float32).sum(0).astype(jnp.bfloat16)
+    weight = w_ref[...]
+    pre = jnp.dot(agg, weight, preferred_element_type=jnp.float32)
+    sigma = jax.nn.sigmoid(pre)
+    out_ref[...] = (pre * sigma).astype(out_ref.dtype)
+    slope = sigma * (1.0 + pre * (1.0 - sigma))
+    grad_pre = (cot_ref[...].astype(jnp.float32) * slope).astype(jnp.bfloat16)
+    local_grad = lax.dot_general(agg, grad_pre, (((0,), (0,)), ((), ())),
+                                 preferred_element_type=jnp.float32)
+    grad_agg = lax.dot_general(grad_pre, weight, (((1,), (1,)), ((), ())),
+                               preferred_element_type=jnp.float32).astype(pay_ref.dtype)
+    tb = grad_agg.shape[0]
+    blocks = pay_ref.shape[0]
+    rows = local_grad.shape[0] // blocks
+    half = local_grad.shape[1] // 2
+    for j in range(blocks):
+        pay_ref[j, :tb, :] = grad_agg
+        part = local_grad[j * rows:(j + 1) * rows, :].astype(pay_ref.dtype)
+        pay_ref[j, tb:tb + rows, :] = part[:, :half]
+        pay_ref[j, tb + rows:tb + 2 * rows, :] = part[:, half:]
+
+
+def dense(recv, weight, cot):
+    blocks, tb, width_in = recv.shape
+    width_out = weight.shape[1]
+    rows = width_in // blocks
+    vmem = pl.BlockSpec(memory_space=pltpu.VMEM)
+    return pl.pallas_call(
+        dense_kernel,
+        out_shape=(
+            jax.ShapeDtypeStruct((tb, width_out), jnp.bfloat16),
+            jax.ShapeDtypeStruct((blocks, tb + 2 * rows, width_in), jnp.bfloat16),
+        ),
+        in_specs=[vmem, vmem, vmem],
+        out_specs=(vmem, vmem),
+        cost_estimate=pl.CostEstimate(
+            flops=6 * tb * width_in * width_out, transcendentals=tb * width_out,
+            bytes_accessed=recv.size * 2 + weight.size * 2 + cot.size * 2 + tb * width_out * 2
+            + blocks * (tb + 2 * rows) * width_in * 2),
+    )(recv, weight, cot)
+
+
 def on_device(features, weight, tile_values, tile_rows, tile_cols, tile_count, cotangent):
     rows_dev = features.shape[1]
     width_in = features.shape[2]
@@ -83,25 +126,9 @@
     partial_value = spread(tile_block, row_ids, col_ids, tile_total, col_source, row_tiles, False, jnp.bfloat16)
     sent = partial_value.reshape(n_col, rows_dev, width_in)
     got = lax.all_to_all(sent, "col", 0, 0, tiled=False)
-    aggregated = got.astype(jnp.float32).sum(0).astype(jnp.bfloat16)
-
-    pre = jnp.dot(aggregated, weight, preferred_element_type=jnp.float32)
-    sigma = jax.nn.sigmoid(pre)
-    output = (pre * sigma).astype(jnp.bfloat16)[None]
-    slope = sigma * (1.0 + pre * (1.0 - sigma))
-    grad_pre = (cotangent[0].astype(jnp.float32) * slope).astype(jnp.bfloat16)
-    local_grad = lax.dot_general(
-        aggregated, grad_pre, (((0,), (0,)), ((), ())), preferred_element_type=jnp.float32
-    )
-    grad_agg = lax.dot_general(
-        grad_pre, weight, (((1,), (1,)), ((), ())), preferred_element_type=jnp.float32
-    ).astype(jnp.bfloat16)
-
+    out_block, payload = dense(got, weight, cotangent[0])
+    output = out_block[None]
     wg_rows = width_in // n_col
-    wg_words = local_grad.reshape(n_col, -1, width_in).astype(jnp.bfloat16)
-    payload = jnp.concatenate(
-        [jnp.broadcast_to(grad_agg[None], (n_col,) + grad_agg.shape), wg_words], axis=1
-    )
     got = lax.all_to_all(payload, "col", 0, 0, tiled=False)
     row_source = got
 
@@ -111,7 +138,7 @@
     got = lax.all_to_all(payload, "row", 0, 0, tiled=False)
     grad_features = got[:, :rows_dev].astype(jnp.float32).sum(0).astype(jnp.bfloat16)[None]
     wg_part = got[:, rows_dev:].astype(jnp.float32).sum(0) * node_total ** (-0.5)
-    wg_part = wg_part.reshape(wg_rows, width_out)
+    wg_part = wg_part.reshape(2, wg_rows, width_in).transpose(1, 0, 2).reshape(wg_rows, width_out)
 
     everyone = lax.all_to_all(
         jnp.broadcast_to(wg_part[None], (n_col,) + wg_part.shape), "col", 0, 0, tiled=False

time: 161 us -> 163 us (1.012)
  Pallas kernels: 6.03 us -> 8.31 us
    pallas_call x0 -> x1, Pallas kernels: none -> 2.28 us  [dense(): pl.pallas_call(dense_kernel, out_shape=(jax.ShapeDtypeStruct((tb, width_o...]
where the time goes in v14:
time: 163 us; the launch traced here: 162 us
  blocking collectives  93.3 us (57%)
  waiting for transfers between devices  34.7 us (21%)
  starting transfers between devices  19.1 us (12%)
  Pallas kernels  8.31 us (5%)
  local copies, waits for them, and re-layouts  4.29 us (3%)
    all_to_all x1, blocking collectives, on_device(): got = lax.all_to_all(payload, 'row', 0, 0, tiled=False)  38.8 us
    all_to_all x1, blocking collectives, on_device(): got = lax.all_to_all(sent, 'col', 0, 0, tiled=False)  31.2 us
    all_to_all x1, waiting for transfers between devices, on_device(): lax.all_to_all(jnp.broadcast_to(own[None], (n_row,) + own.shape), 'row',...  25.2 us
    all_to_all x1, blocking collectives, on_device(): got = lax.all_to_all(payload, 'col', 0, 0, tiled=False)  23.3 us
    all_to_all x1, starting transfers between devices, on_device(): lax.all_to_all(jnp.broadcast_to(own[None], (n_row,) + own.shape), 'row',...  13.5 us
    all_to_all x1, waiting for transfers between devices, on_device(): lax.all_to_all(jnp.broadcast_to(wg_part[None], (n_col,) + wg_part.shape),...  9.53 us
    pallas_call x2, Pallas kernels, spread(): pl.pallas_call(functools.partial(spread_kernel, transpose, carry_words),...  6.03 us
    all_to_all x1, starting transfers between devices, on_device(): lax.all_to_all(jnp.broadcast_to(wg_part[None], (n_col,) + wg_part.shape),...  5.66 us
  transfers between devices with their start and end apart: 2, of which 2 were waited for; matrix products, arithmetic and copies ran while one was open for 0% of the time, Pallas kernels for 0%

profile of v14, /device:TPU:1, one launch (start us, length us, event | category | flops | bytes accessed | tf_op | source)
XLA Modules:
  0.0 161.8 jit_solution(8945946203392575561)
XLA Ops:
  0.6 2.0 %broadcast_in_dim.21 = bf16[32,128,128]{2,1,0:T(8,128)(2,1)} broadcast(bf16[128,128]{1,0:T(8,128)(2,1)} %bitcast.21), dimensions={1,2} | broadcast | bytes 1081344 | tf_op jit(solution)/shard_map/broadcast_in_dim | solution.py:123
  2.6 13.5 %all-to-all-start = ((bf16[32,128,128]{2,1,0:T(8,128)(2,1)}), bf16[32,128,128]{2,1,0:T(8,128)(2,1)S(1)}, u32[]{:S(2)}, u32[]{:S(2)}) async-start(bf16[32,128,128]{2,1,0:T(8,128)(2,1)} %broadcast_in_dim.21), calls=%async_computation | async-start | bytes 2097152 | tf_op jit(solution)/shard_map/all_to_all | solution.py:122
  16.7 25.2 %all-to-all-done.src_ref = bf16[32,128,128]{2,1,0:T(8,128)(2,1)S(1)} async-done(((bf16[32,128,128]{2,1,0:T(8,128)(2,1)}), bf16[32,128,128]{2,1,0:T(8,128)(2,1)S(1)}, u32[]{:S(2)}, u32[]{:S(2)}) %all-to-all-start) | async-done | bytes 1048608 | tf_op jit(solution)/shard_map/all_to_all | solution.py:122
  41.9 0.0 copy-start
  41.9 1.0 copy-done
  42.9 2.9 %shard_map.94 = bf16[16,128,128]{2,1,0:T(8,128)(2,1)} custom-call(s32[32]{0:T(128)} %bitcast.23, s32[32]{0:T(128)} %bitcast.25, s32[1]{0:T(128)} %bitcast.15.count_ref, bf16[32,128,128]{2,1,0:T(8,128)(2,1)} %bitcast.17, bf16[32,128,128]{2,1,0:T(8,128)(2,1)} %copy-done), custom_call_target="tpu_custom_call" | custom-call | flops 134217728 | bytes 2621440 | tf_op jit(solution)/shard_map/pallas_call | solution.py:51
  45.8 31.2 %all_to_all.25.recv_ref = bf16[16,128,128]{2,1,0:T(8,128)(2,1)} all-to-all(bf16[16,128,128]{2,1,0:T(8,128)(2,1)} %shard_map.94), channel_id=1, replica_groups=mesh['row'=32,'col'=16] {'col'}, dimensions={0} | all-to-all | bytes 1048576 | tf_op jit(solution)/shard_map/all_to_all | solution.py:128
  77.0 2.3 %shard_map.95 = (bf16[128,256]{1,0:T(8,128)(2,1)}, bf16[16,144,128]{2,1,0:T(8,128)(2,1)}) custom-call(bf16[16,128,128]{2,1,0:T(8,128)(2,1)} %all_to_all.25.recv_ref, bf16[128,256]{1,0:T(8,128)(2,1)} %w_ref.1, bf16[128,256]{1,0:T(8,128)(2,1)} %bitcast.20), custom_call_target="tpu_custom_call" | custom-call | flops 25165824 | bytes 1310720 | tf_op jit(solution)/shard_map/pallas_call | solution.py:91
  79.3 23.3 %all_to_all.26.src_ref = bf16[16,144,128]{2,1,0:T(8,128)(2,1)} all-to-all(bf16[16,144,128]{2,1,0:T(8,128)(2,1)} %get-tuple-element.6), channel_id=1, replica_groups=mesh['row'=32,'col'=16] {'col'}, dimensions={0} | all-to-all | bytes 1179648 | tf_op jit(solution)/shard_map/all_to_all | solution.py:132
  102.6 3.2 %shard_map.96 = bf16[32,144,128]{2,1,0:T(8,128)(2,1)} custom-call(s32[32]{0:T(128)} %bitcast.26, s32[32]{0:T(128)} %bitcast.24, s32[1]{0:T(128)} %bitcast.16.count_ref, bf16[32,128,128]{2,1,0:T(8,128)(2,1)} %bitcast.18, bf16[16,144,128]{2,1,0:T(8,128)(2,1)} %all_to_all.26.src_ref), custom_call_target="tpu_custom_call" | custom-call | flops 134217728 | bytes 2818048 | tf_op jit(solution)/shard_map/pallas_call | solution.py:51
  105.8 38.8 %all_to_all.27 = bf16[32,144,128]{2,1,0:T(8,128)(2,1)S(1)} all-to-all(bf16[32,144,128]{2,1,0:T(8,128)(2,1)} %shard_map.96), channel_id=1, replica_groups=mesh['row'=32,'col'=16] {'row'}, dimensions={0} | all-to-all | bytes 2359296 | tf_op jit(solution)/shard_map/all_to_all | solution.py:138
  144.6 0.7 broadcast_in_dim.25
  145.2 5.7 %all-to-all-start.4 = ((f32[16,8,256]{2,1,0:T(8,128)}), f32[16,8,256]{2,1,0:T(8,128)S(1)}, u32[]{:S(2)}, u32[]{:S(2)}) async-start(f32[16,8,256]{2,1,0:T(8,128)} %broadcast_in_dim.25), calls=%async_computation.4 | async-start | bytes 262144 | tf_op jit(solution)/shard_map/all_to_all | solution.py:143
  150.9 0.8 slice_reduce_fusion
  151.7 9.5 %all-to-all-done.4 = f32[16,8,256]{2,1,0:T(8,128)S(1)} async-done(((f32[16,8,256]{2,1,0:T(8,128)}), f32[16,8,256]{2,1,0:T(8,128)S(1)}, u32[]{:S(2)}, u32[]{:S(2)}) %all-to-all-start.4) | async-done | bytes 131104 | tf_op jit(solution)/shard_map/all_to_all | solution.py:143
  161.2 0.7 copy.12
  (2 shorter events, 0.0 us)
Async XLA Ops:
  2.6 39.3 %all-to-all-start = ((bf16[32,128,128]{2,1,0:T(8,128)(2,1)}), bf16[32,128,128]{2,1,0:T(8,128)(2,1)S(1)}, u32[]{:S(2)}, u32[]{:S(2)}) async-start(bf16[32,128,128]{2,1,0:T(8,128)(2,1)} %broadcast_in_dim.21), calls=%async_computation | async-start | bytes 2097152 | tf_op jit(solution)/shard_map/all_to_all | solution.py:122
  41.9 1.0 copy-start
  145.2 16.0 %all-to-all-start.4 = ((f32[16,8,256]{2,1,0:T(8,128)}), f32[16,8,256]{2,1,0:T(8,128)S(1)}, u32[]{:S(2)}, u32[]{:S(2)}) async-start(f32[16,8,256]{2,1,0:T(8,128)} %broadcast_in_dim.25), calls=%async_computation.4 | async-start | bytes 262144 | tf_op jit(solution)/shard_map/all_to_all | solution.py:143

commit v15 on v13

--- a/solution.py
+++ b/solution.py
@@ -46,6 +46,8 @@
     width = source.shape[-1]
     smem = pl.BlockSpec(memory_space=pltpu.SMEM)
     vmem = pl.BlockSpec(memory_space=pltpu.VMEM)
+    tiles = pltpu.with_memory_space_constraint(tiles, pltpu.VMEM)
+    source = pltpu.with_memory_space_constraint(source, pltpu.VMEM)
     args = [target_ids, source_ids, count.reshape(1), tiles, source]
     out_rows = source.shape[1] if carry_words else tb
     return pl.pallas_call(

time: 161 us -> 158 us (0.981)
  no operation moved by 1% of the time
where the time goes in v15:
time: 158 us
  blocking collectives  92.6 us (59%)
  waiting for transfers between devices  34.8 us (22%)
  starting transfers between devices  19.1 us (12%)
  Pallas kernels  4.43 us (3%)
  local copies, waits for them, and re-layouts  3.48 us (2%)
    all_to_all x1, blocking collectives, on_device(): got = lax.all_to_all(payload, 'row', 0, 0, tiled=False)  39.7 us
    all_to_all x1, blocking collectives, on_device(): got = lax.all_to_all(sent, 'col', 0, 0, tiled=False)  31.2 us
    all_to_all x1, waiting for transfers between devices, on_device(): lax.all_to_all(jnp.broadcast_to(own[None], (n_row,) + own.shape), 'row',...  25.2 us
    all_to_all x1, blocking collectives, on_device(): got = lax.all_to_all(payload, 'col', 0, 0, tiled=False)  21.7 us
    all_to_all x1, starting transfers between devices, on_device(): lax.all_to_all(jnp.broadcast_to(own[None], (n_row,) + own.shape), 'row',...  13.6 us
    all_to_all x1, waiting for transfers between devices, on_device(): lax.all_to_all(jnp.broadcast_to(wg_part[None], (n_col,) + wg_part.shape),...  9.56 us
    all_to_all x1, starting transfers between devices, on_device(): lax.all_to_all(jnp.broadcast_to(wg_part[None], (n_col,) + wg_part.shape),...  5.51 us
    pallas_call x2, Pallas kernels, spread(): pl.pallas_call(functools.partial(spread_kernel, transpose, carry_words),...  4.43 us
  transfers between devices with their start and end apart: 2, of which 2 were waited for; matrix products, arithmetic and copies ran while one was open for 0% of the time, Pallas kernels for 0%

profile of v15, /device:TPU:1, one launch (start us, length us, event | category | flops | bytes accessed | tf_op | source)
XLA Modules:
  0.0 157.8 jit_solution(7665387378169327162)
XLA Ops:
  0.6 0.0 copy-start
  0.6 2.0 %broadcast_in_dim.25 = bf16[32,128,128]{2,1,0:T(8,128)(2,1)} broadcast(bf16[128,128]{1,0:T(8,128)(2,1)} %bitcast.23), dimensions={1,2} | broadcast | bytes 1081344 | tf_op jit(solution)/shard_map/broadcast_in_dim | solution.py:82
  2.7 0.0 copy-start.1
  2.7 13.6 %all-to-all-start = ((bf16[32,128,128]{2,1,0:T(8,128)(2,1)}), bf16[32,128,128]{2,1,0:T(8,128)(2,1)S(1)}, u32[]{:S(2)}, u32[]{:S(2)}) async-start(bf16[32,128,128]{2,1,0:T(8,128)(2,1)} %broadcast_in_dim.25), calls=%async_computation | async-start | bytes 2097152 | tf_op jit(solution)/shard_map/all_to_all | solution.py:81
  16.9 25.2 %all-to-all-done.src_ref = bf16[32,128,128]{2,1,0:T(8,128)(2,1)S(1)} async-done(((bf16[32,128,128]{2,1,0:T(8,128)(2,1)}), bf16[32,128,128]{2,1,0:T(8,128)(2,1)S(1)}, u32[]{:S(2)}, u32[]{:S(2)}) %all-to-all-start) | async-done | bytes 1048608 | tf_op jit(solution)/shard_map/all_to_all | solution.py:81
  42.1 0.0 copy-done.1
  42.1 2.0 %shard_map.94 = bf16[16,128,128]{2,1,0:T(8,128)(2,1)} custom-call(s32[32]{0:T(128)} %bitcast.25, s32[32]{0:T(128)} %bitcast.27, s32[1]{0:T(128)} %bitcast.18.count_ref, bf16[32,128,128]{2,1,0:T(8,128)(2,1)S(1)} %bitcast.20, bf16[32,128,128]{2,1,0:T(8,128)(2,1)S(1)} %all-to-all-done.src_ref), custom_call_target="tpu_custom_call" | custom-call | flops 134217728 | bytes 2621440 | tf_op jit(solution)/shard_map/pallas_call | solution.py:53
  44.1 0.0 copy-start.2
  44.1 31.2 %all_to_all.25 = bf16[16,128,128]{2,1,0:T(8,128)(2,1)S(1)} all-to-all(bf16[16,128,128]{2,1,0:T(8,128)(2,1)} %shard_map.94), channel_id=1, replica_groups=mesh['row'=32,'col'=16] {'col'}, dimensions={0} | all-to-all | bytes 1048576 | tf_op jit(solution)/shard_map/all_to_all | solution.py:87
  75.3 0.1 reduce_sum.33
  75.4 0.0 copy-done
  75.4 0.0 copy-done.2
  75.4 0.8 fusion
  76.3 0.2 convolution_convert_fusion
  76.5 0.2 convolution_convert_fusion.1
  76.7 0.1 broadcast_in_dim.27
  76.8 21.7 %all_to_all.26.src_ref = bf16[16,144,128]{2,1,0:T(8,128)(2,1)S(1)} all-to-all(bf16[16,144,128]{2,1,0:T(8,128)(2,1)S(1)} %pad_maximum_fusion), channel_id=1, replica_groups=mesh['row'=32,'col'=16] {'col'}, dimensions={0} | all-to-all | bytes 1179648 | tf_op jit(solution)/shard_map/all_to_all | solution.py:107
  98.5 2.4 %shard_map.95 = bf16[32,144,128]{2,1,0:T(8,128)(2,1)} custom-call(s32[32]{0:T(128)} %bitcast.28, s32[32]{0:T(128)} %bitcast.26, s32[1]{0:T(128)} %bitcast.19.count_ref, bf16[32,128,128]{2,1,0:T(8,128)(2,1)S(1)} %bitcast.21, bf16[16,144,128]{2,1,0:T(8,128)(2,1)S(1)} %all_to_all.26.src_ref), custom_call_target="tpu_custom_call" | custom-call | flops 134217728 | bytes 2818048 | tf_op jit(solution)/shard_map/pallas_call | solution.py:53
  100.9 39.7 %all_to_all.27 = bf16[32,144,128]{2,1,0:T(8,128)(2,1)S(1)} all-to-all(bf16[32,144,128]{2,1,0:T(8,128)(2,1)} %shard_map.95), channel_id=1, replica_groups=mesh['row'=32,'col'=16] {'row'}, dimensions={0} | all-to-all | bytes 2359296 | tf_op jit(solution)/shard_map/all_to_all | solution.py:113
  140.7 0.7 broadcast_in_dim.29
  141.3 5.5 %all-to-all-start.4 = ((f32[16,8,256]{2,1,0:T(8,128)}), f32[16,8,256]{2,1,0:T(8,128)S(1)}, u32[]{:S(2)}, u32[]{:S(2)}) async-start(f32[16,8,256]{2,1,0:T(8,128)} %broadcast_in_dim.29), calls=%async_computation.4 | async-start | bytes 262144 | tf_op jit(solution)/shard_map/all_to_all | solution.py:118
  146.8 0.8 slice_reduce_fusion
  147.6 9.6 %all-to-all-done.4 = f32[16,8,256]{2,1,0:T(8,128)S(1)} async-done(((f32[16,8,256]{2,1,0:T(8,128)}), f32[16,8,256]{2,1,0:T(8,128)S(1)}, u32[]{:S(2)}, u32[]{:S(2)}) %all-to-all-start.4) | async-done | bytes 131104 | tf_op jit(solution)/shard_map/all_to_all | solution.py:118
  157.2 0.7 copy.12
  (5 shorter events, 0.1 us)
Async XLA Ops:
  0.6 74.8 %copy-start = (bf16[128,256]{1,0:T(8,128)(2,1)S(1)}, bf16[128,256]{1,0:T(8,128)(2,1)}, u32[]{:S(2)}) copy-start(bf16[128,256]{1,0:T(8,128)(2,1)} %param.8) | copy-start | bytes 196612
  2.7 39.5 %copy-start.1 = (bf16[1,1,32,128,128]{4,3,2,1,0:T(8,128)(2,1)S(1)}, bf16[1,1,32,128,128]{4,3,2,1,0:T(8,128)(2,1)}, u32[]{:S(2)}) copy-start(bf16[1,1,32,128,128]{4,3,2,1,0:T(8,128)(2,1)} %param.9) | copy-start | bytes 3145732
  2.7 39.5 %all-to-all-start = ((bf16[32,128,128]{2,1,0:T(8,128)(2,1)}), bf16[32,128,128]{2,1,0:T(8,128)(2,1)S(1)}, u32[]{:S(2)}, u32[]{:S(2)}) async-start(bf16[32,128,128]{2,1,0:T(8,128)(2,1)} %broadcast_in_dim.25), calls=%async_computation | async-start | bytes 2097152 | tf_op jit(solution)/shard_map/all_to_all | solution.py:81
  44.1 31.3 %copy-start.2 = (bf16[1,128,256]{2,1,0:T(8,128)(2,1)S(1)}, bf16[1,128,256]{2,1,0:T(8,128)(2,1)}, u32[]{:S(2)}) copy-start(bf16[1,128,256]{2,1,0:T(8,128)(2,1)} %param.13) | copy-start | bytes 196612
  141.3 15.8 %all-to-all-start.4 = ((f32[16,8,256]{2,1,0:T(8,128)}), f32[16,8,256]{2,1,0:T(8,128)S(1)}, u32[]{:S(2)}, u32[]{:S(2)}) async-start(f32[16,8,256]{2,1,0:T(8,128)} %broadcast_in_dim.29), calls=%async_computation.4 | async-start | bytes 262144 | tf_op jit(solution)/shard_map/all_to_all | solution.py:118

commit v16 on v14

--- a/solution.py
+++ b/solution.py
@@ -46,6 +46,8 @@
     width = source.shape[-1]
     smem = pl.BlockSpec(memory_space=pltpu.SMEM)
     vmem = pl.BlockSpec(memory_space=pltpu.VMEM)
+    tiles = pltpu.with_memory_space_constraint(tiles, pltpu.VMEM)
+    source = pltpu.with_memory_space_constraint(source, pltpu.VMEM)
     args = [target_ids, source_ids, count.reshape(1), tiles, source]
     out_rows = source.shape[1] if carry_words else tb
     return pl.pallas_call(
@@ -100,7 +102,7 @@
             flops=6 * tb * width_in * width_out, transcendentals=tb * width_out,
             bytes_accessed=recv.size * 2 + weight.size * 2 + cot.size * 2 + tb * width_out * 2
             + blocks * (tb + 2 * rows) * width_in * 2),
-    )(recv, weight, cot)
+    )(*(pltpu.with_memory_space_constraint(x, pltpu.VMEM) for x in (recv, weight, cot)))
 
 
 def on_device(features, weight, tile_values, tile_rows, tile_cols, tile_count, cotangent):

time: 163 us -> 158 us (0.969)
  Pallas kernels: 8.31 us -> 5.76 us
where the time goes in v16:
time: 158 us
  blocking collectives  92.6 us (59%)
  waiting for transfers between devices  34.7 us (22%)
  starting transfers between devices  19.1 us (12%)
  Pallas kernels  5.76 us (4%)
  local copies, waits for them, and re-layouts  3.3 us (2%)
    all_to_all x1, blocking collectives, on_device(): got = lax.all_to_all(payload, 'row', 0, 0, tiled=False)  39 us
    all_to_all x1, blocking collectives, on_device(): got = lax.all_to_all(sent, 'col', 0, 0, tiled=False)  31.1 us
    all_to_all x1, waiting for transfers between devices, on_device(): lax.all_to_all(jnp.broadcast_to(own[None], (n_row,) + own.shape), 'row',...  25.2 us
    all_to_all x1, blocking collectives, on_device(): got = lax.all_to_all(payload, 'col', 0, 0, tiled=False)  22.6 us
    all_to_all x1, starting transfers between devices, on_device(): lax.all_to_all(jnp.broadcast_to(own[None], (n_row,) + own.shape), 'row',...  13.6 us
    all_to_all x1, waiting for transfers between devices, on_device(): lax.all_to_all(jnp.broadcast_to(wg_part[None], (n_col,) + wg_part.shape),...  9.48 us
    all_to_all x1, starting transfers between devices, on_device(): lax.all_to_all(jnp.broadcast_to(wg_part[None], (n_col,) + wg_part.shape),...  5.54 us
    pallas_call x2, Pallas kernels, spread(): pl.pallas_call(functools.partial(spread_kernel, transpose, carry_words),...  4.57 us
  transfers between devices with their start and end apart: 2, of which 2 were waited for; matrix products, arithmetic and copies ran while one was open for 0% of the time, Pallas kernels for 0%

profile of v16, /device:TPU:1, one launch (start us, length us, event | category | flops | bytes accessed | tf_op | source)
XLA Modules:
  0.0 157.6 jit_solution(6391608194219501543)
XLA Ops:
  0.6 2.0 %broadcast_in_dim.21 = bf16[32,128,128]{2,1,0:T(8,128)(2,1)} broadcast(bf16[128,128]{1,0:T(8,128)(2,1)} %bitcast.21), dimensions={1,2} | broadcast | bytes 1081344 | tf_op jit(solution)/shard_map/broadcast_in_dim | solution.py:125
  2.6 0.0 copy-start
  2.6 13.6 %all-to-all-start = ((bf16[32,128,128]{2,1,0:T(8,128)(2,1)}), bf16[32,128,128]{2,1,0:T(8,128)(2,1)S(1)}, u32[]{:S(2)}, u32[]{:S(2)}) async-start(bf16[32,128,128]{2,1,0:T(8,128)(2,1)} %broadcast_in_dim.21), calls=%async_computation | async-start | bytes 2097152 | tf_op jit(solution)/shard_map/all_to_all | solution.py:124
  16.9 25.2 %all-to-all-done.src_ref = bf16[32,128,128]{2,1,0:T(8,128)(2,1)S(1)} async-done(((bf16[32,128,128]{2,1,0:T(8,128)(2,1)}), bf16[32,128,128]{2,1,0:T(8,128)(2,1)S(1)}, u32[]{:S(2)}, u32[]{:S(2)}) %all-to-all-start) | async-done | bytes 1048608 | tf_op jit(solution)/shard_map/all_to_all | solution.py:124
  42.1 0.0 copy-done
  42.1 0.0 copy-start.1
  42.1 0.0 copy-start.2
  42.1 2.1 %shard_map.94 = bf16[16,128,128]{2,1,0:T(8,128)(2,1)} custom-call(s32[32]{0:T(128)} %bitcast.23, s32[32]{0:T(128)} %bitcast.25, s32[1]{0:T(128)} %bitcast.15.count_ref, bf16[32,128,128]{2,1,0:T(8,128)(2,1)S(1)} %bitcast.17, bf16[32,128,128]{2,1,0:T(8,128)(2,1)S(1)} %all-to-all-done.src_ref), custom_call_target="tpu_custom_call" | custom-call | flops 134217728 | bytes 2621440 | tf_op jit(solution)/shard_map/pallas_call | solution.py:53
  44.2 31.1 %all_to_all.25.recv_ref = bf16[16,128,128]{2,1,0:T(8,128)(2,1)S(1)} all-to-all(bf16[16,128,128]{2,1,0:T(8,128)(2,1)} %shard_map.94), channel_id=1, replica_groups=mesh['row'=32,'col'=16] {'col'}, dimensions={0} | all-to-all | bytes 1048576 | tf_op jit(solution)/shard_map/all_to_all | solution.py:130
  75.3 0.0 copy-done.1
  75.3 0.0 copy-done.2
  75.3 1.2 shard_map.95
  76.5 22.6 %all_to_all.26.src_ref = bf16[16,144,128]{2,1,0:T(8,128)(2,1)S(1)} all-to-all(bf16[16,144,128]{2,1,0:T(8,128)(2,1)} %get-tuple-element.6), channel_id=1, replica_groups=mesh['row'=32,'col'=16] {'col'}, dimensions={0} | all-to-all | bytes 1179648 | tf_op jit(solution)/shard_map/all_to_all | solution.py:134
  99.0 2.4 %shard_map.96 = bf16[32,144,128]{2,1,0:T(8,128)(2,1)} custom-call(s32[32]{0:T(128)} %bitcast.26, s32[32]{0:T(128)} %bitcast.24, s32[1]{0:T(128)} %bitcast.16.count_ref, bf16[32,128,128]{2,1,0:T(8,128)(2,1)S(1)} %bitcast.18, bf16[16,144,128]{2,1,0:T(8,128)(2,1)S(1)} %all_to_all.26.src_ref), custom_call_target="tpu_custom_call" | custom-call | flops 134217728 | bytes 2818048 | tf_op jit(solution)/shard_map/pallas_call | solution.py:53
  101.5 39.0 %all_to_all.27 = bf16[32,144,128]{2,1,0:T(8,128)(2,1)S(1)} all-to-all(bf16[32,144,128]{2,1,0:T(8,128)(2,1)} %shard_map.96), channel_id=1, replica_groups=mesh['row'=32,'col'=16] {'row'}, dimensions={0} | all-to-all | bytes 2359296 | tf_op jit(solution)/shard_map/all_to_all | solution.py:140
  140.5 0.7 broadcast_in_dim.25
  141.2 5.5 %all-to-all-start.4 = ((f32[16,8,256]{2,1,0:T(8,128)}), f32[16,8,256]{2,1,0:T(8,128)S(1)}, u32[]{:S(2)}, u32[]{:S(2)}) async-start(f32[16,8,256]{2,1,0:T(8,128)} %broadcast_in_dim.25), calls=%async_computation.4 | async-start | bytes 262144 | tf_op jit(solution)/shard_map/all_to_all | solution.py:145
  146.7 0.8 slice_reduce_fusion
  147.5 9.5 %all-to-all-done.4 = f32[16,8,256]{2,1,0:T(8,128)S(1)} async-done(((f32[16,8,256]{2,1,0:T(8,128)}), f32[16,8,256]{2,1,0:T(8,128)S(1)}, u32[]{:S(2)}, u32[]{:S(2)}) %all-to-all-start.4) | async-done | bytes 131104 | tf_op jit(solution)/shard_map/all_to_all | solution.py:145
  156.9 0.7 copy.12
  (2 shorter events, 0.0 us)
Async XLA Ops:
  2.6 39.5 %copy-start = (bf16[1,1,32,128,128]{4,3,2,1,0:T(8,128)(2,1)S(1)}, bf16[1,1,32,128,128]{4,3,2,1,0:T(8,128)(2,1)}, u32[]{:S(2)}) copy-start(bf16[1,1,32,128,128]{4,3,2,1,0:T(8,128)(2,1)} %param.9) | copy-start | bytes 3145732
  2.6 39.5 %all-to-all-start = ((bf16[32,128,128]{2,1,0:T(8,128)(2,1)}), bf16[32,128,128]{2,1,0:T(8,128)(2,1)S(1)}, u32[]{:S(2)}, u32[]{:S(2)}) async-start(bf16[32,128,128]{2,1,0:T(8,128)(2,1)} %broadcast_in_dim.21), calls=%async_computation | async-start | bytes 2097152 | tf_op jit(solution)/shard_map/all_to_all | solution.py:124
  42.1 33.2 %copy-start.1 = (bf16[128,256]{1,0:T(8,128)(2,1)S(1)}, bf16[128,256]{1,0:T(8,128)(2,1)}, u32[]{:S(2)}) copy-start(bf16[128,256]{1,0:T(8,128)(2,1)} %w_ref.1) | copy-start | bytes 196612
  42.1 33.2 %copy-start.2 = (bf16[1,128,256]{2,1,0:T(8,128)(2,1)S(1)}, bf16[1,128,256]{2,1,0:T(8,128)(2,1)}, u32[]{:S(2)}) copy-start(bf16[1,128,256]{2,1,0:T(8,128)(2,1)} %param.13) | copy-start | bytes 196612
  141.2 15.8 %all-to-all-start.4 = ((f32[16,8,256]{2,1,0:T(8,128)}), f32[16,8,256]{2,1,0:T(8,128)S(1)}, u32[]{:S(2)}, u32[]{:S(2)}) async-start(f32[16,8,256]{2,1,0:T(8,128)} %broadcast_in_dim.25), calls=%async_computation.4 | async-start | bytes 262144 | tf_op jit(solution)/shard_map/all_to_all | solution.py:145

commit v17 on v16

--- a/solution.py
+++ b/solution.py
@@ -105,6 +105,31 @@
     )(*(pltpu.with_memory_space_constraint(x, pltpu.VMEM) for x in (recv, weight, cot)))
 
 
+def weight_part_kernel(tb, rows, scale, got_ref, out_ref):
+    wg = jnp.zeros((2 * rows, got_ref.shape[2]), jnp.float32)
+    for j in range(got_ref.shape[0]):
+        wg = wg + got_ref[j, tb:, :].astype(jnp.float32)
+    wg = wg * scale
+    half = got_ref.shape[2]
+    for j in range(out_ref.shape[0]):
+        out_ref[j, :, :half] = wg[:rows]
+        out_ref[j, :, half:] = wg[rows:]
+
+
+def weight_part(got, tb, rows, copies, scale):
+    width = got.shape[2]
+    vmem = pl.BlockSpec(memory_space=pltpu.VMEM)
+    return pl.pallas_call(
+        functools.partial(weight_part_kernel, tb, rows, scale),
+        out_shape=jax.ShapeDtypeStruct((copies, rows, 2 * width), jnp.float32),
+        in_specs=[vmem],
+        out_specs=vmem,
+        cost_estimate=pl.CostEstimate(
+            flops=got.shape[0] * 2 * rows * width, transcendentals=0,
+            bytes_accessed=got.shape[0] * 2 * rows * width * 2 + copies * rows * 2 * width * 4),
+    )(pltpu.with_memory_space_constraint(got, pltpu.VMEM))
+
+
 def on_device(features, weight, tile_values, tile_rows, tile_cols, tile_count, cotangent):
     rows_dev = features.shape[1]
     width_in = features.shape[2]
@@ -139,12 +164,9 @@
     )
     got = lax.all_to_all(payload, "row", 0, 0, tiled=False)
     grad_features = got[:, :rows_dev].astype(jnp.float32).sum(0).astype(jnp.bfloat16)[None]
-    wg_part = got[:, rows_dev:].astype(jnp.float32).sum(0) * node_total ** (-0.5)
-    wg_part = wg_part.reshape(2, wg_rows, width_in).transpose(1, 0, 2).reshape(wg_rows, width_out)
+    parts = weight_part(got, rows_dev, wg_rows, n_col, node_total ** (-0.5))
 
-    everyone = lax.all_to_all(
-        jnp.broadcast_to(wg_part[None], (n_col,) + wg_part.shape), "col", 0, 0, tiled=False
-    )
+    everyone = lax.all_to_all(parts, "col", 0, 0, tiled=False)
     weight_grad = everyone.reshape(width_in, width_out)
     return (output, grad_features, weight_grad)
 

time: 158 us -> 158 us (level)
  no operation moved by 1% of the time
where the time goes in v17:
time: 158 us
  blocking collectives  92.6 us (59%)
  waiting for transfers between devices  34.7 us (22%)
  starting transfers between devices  19.2 us (12%)
  Pallas kernels  6.46 us (4%)
  local copies, waits for them, and re-layouts  2.64 us (2%)
    all_to_all x1, blocking collectives, on_device(): got = lax.all_to_all(payload, 'row', 0, 0, tiled=False)  38.9 us
    all_to_all x1, blocking collectives, on_device(): got = lax.all_to_all(sent, 'col', 0, 0, tiled=False)  31.1 us
    all_to_all x1, waiting for transfers between devices, on_device(): lax.all_to_all(jnp.broadcast_to(own[None], (n_row,) + own.shape), 'row',...  25.2 us
    all_to_all x1, blocking collectives, on_device(): got = lax.all_to_all(payload, 'col', 0, 0, tiled=False)  22.6 us
    all_to_all x1, starting transfers between devices, on_device(): lax.all_to_all(jnp.broadcast_to(own[None], (n_row,) + own.shape), 'row',...  13.6 us
    all_to_all x1, waiting for transfers between devices, on_device(): everyone = lax.all_to_all(parts, 'col', 0, 0, tiled=False)  9.48 us
    all_to_all x1, starting transfers between devices, on_device(): everyone = lax.all_to_all(parts, 'col', 0, 0, tiled=False)  5.56 us
    pallas_call x2, Pallas kernels, spread(): pl.pallas_call(functools.partial(spread_kernel, transpose, carry_words),...  4.56 us
  transfers between devices with their start and end apart: 2, of which 2 were waited for; matrix products, arithmetic and copies ran while one was open for 0% of the time, Pallas kernels for 0%

profile of v17, /device:TPU:1, one launch (start us, length us, event | category | flops | bytes accessed | tf_op | source)
XLA Modules:
  0.0 157.6 jit_solution(1432491606479051451)
XLA Ops:
  0.6 2.0 %broadcast_in_dim.14 = bf16[32,128,128]{2,1,0:T(8,128)(2,1)} broadcast(bf16[128,128]{1,0:T(8,128)(2,1)} %bitcast.15), dimensions={1,2} | broadcast | bytes 1081344 | tf_op jit(solution)/shard_map/broadcast_in_dim | solution.py:150
  2.6 0.0 copy-start
  2.6 13.6 %all-to-all-start = ((bf16[32,128,128]{2,1,0:T(8,128)(2,1)}), bf16[32,128,128]{2,1,0:T(8,128)(2,1)S(1)}, u32[]{:S(2)}, u32[]{:S(2)}) async-start(bf16[32,128,128]{2,1,0:T(8,128)(2,1)} %broadcast_in_dim.14), calls=%async_computation | async-start | bytes 2097152 | tf_op jit(solution)/shard_map/all_to_all | solution.py:149
  16.9 25.2 %all-to-all-done.src_ref = bf16[32,128,128]{2,1,0:T(8,128)(2,1)S(1)} async-done(((bf16[32,128,128]{2,1,0:T(8,128)(2,1)}), bf16[32,128,128]{2,1,0:T(8,128)(2,1)S(1)}, u32[]{:S(2)}, u32[]{:S(2)}) %all-to-all-start) | async-done | bytes 1048608 | tf_op jit(solution)/shard_map/all_to_all | solution.py:149
  42.1 0.0 copy-done
  42.1 0.0 copy-start.1
  42.1 0.0 copy-start.2
  42.1 2.1 %shard_map.94 = bf16[16,128,128]{2,1,0:T(8,128)(2,1)} custom-call(s32[32]{0:T(128)} %bitcast.17, s32[32]{0:T(128)} %bitcast.19, s32[1]{0:T(128)} %bitcast.9.count_ref, bf16[32,128,128]{2,1,0:T(8,128)(2,1)S(1)} %bitcast.11, bf16[32,128,128]{2,1,0:T(8,128)(2,1)S(1)} %all-to-all-done.src_ref), custom_call_target="tpu_custom_call" | custom-call | flops 134217728 | bytes 2621440 | tf_op jit(solution)/shard_map/pallas_call | solution.py:53
  44.2 31.1 %all_to_all.25.recv_ref = bf16[16,128,128]{2,1,0:T(8,128)(2,1)S(1)} all-to-all(bf16[16,128,128]{2,1,0:T(8,128)(2,1)} %shard_map.94), channel_id=1, replica_groups=mesh['row'=32,'col'=16] {'col'}, dimensions={0} | all-to-all | bytes 1048576 | tf_op jit(solution)/shard_map/all_to_all | solution.py:155
  75.3 0.0 copy-done.1
  75.3 0.0 copy-done.2
  75.3 1.2 shard_map.95
  76.5 22.6 %all_to_all.26.src_ref = bf16[16,144,128]{2,1,0:T(8,128)(2,1)S(1)} all-to-all(bf16[16,144,128]{2,1,0:T(8,128)(2,1)} %get-tuple-element.6), channel_id=1, replica_groups=mesh['row'=32,'col'=16] {'col'}, dimensions={0} | all-to-all | bytes 1179648 | tf_op jit(solution)/shard_map/all_to_all | solution.py:159
  99.0 2.4 %shard_map.96 = bf16[32,144,128]{2,1,0:T(8,128)(2,1)} custom-call(s32[32]{0:T(128)} %bitcast.20, s32[32]{0:T(128)} %bitcast.18, s32[1]{0:T(128)} %bitcast.10.count_ref, bf16[32,128,128]{2,1,0:T(8,128)(2,1)S(1)} %bitcast.12, bf16[16,144,128]{2,1,0:T(8,128)(2,1)S(1)} %all_to_all.26.src_ref), custom_call_target="tpu_custom_call" | custom-call | flops 134217728 | bytes 2818048 | tf_op jit(solution)/shard_map/pallas_call | solution.py:53
  101.5 38.9 %all_to_all.27.got_ref = bf16[32,144,128]{2,1,0:T(8,128)(2,1)S(1)} all-to-all(bf16[32,144,128]{2,1,0:T(8,128)(2,1)} %shard_map.96), channel_id=1, replica_groups=mesh['row'=32,'col'=16] {'row'}, dimensions={0} | all-to-all | bytes 2359296 | tf_op jit(solution)/shard_map/all_to_all | solution.py:165
  140.4 0.7 shard_map.97
  141.1 5.6 %all-to-all-start.4 = ((f32[16,8,256]{2,1,0:T(8,128)}), f32[16,8,256]{2,1,0:T(8,128)S(1)}, u32[]{:S(2)}, u32[]{:S(2)}) async-start(f32[16,8,256]{2,1,0:T(8,128)} %shard_map.97), calls=%async_computation.4 | async-start | bytes 262144 | tf_op jit(solution)/shard_map/all_to_all | solution.py:169
  146.7 0.8 slice_reduce_fusion
  147.5 9.5 %all-to-all-done.4 = f32[16,8,256]{2,1,0:T(8,128)S(1)} async-done(((f32[16,8,256]{2,1,0:T(8,128)}), f32[16,8,256]{2,1,0:T(8,128)S(1)}, u32[]{:S(2)}, u32[]{:S(2)}) %all-to-all-start.4) | async-done | bytes 131104 | tf_op jit(solution)/shard_map/all_to_all | solution.py:169
  156.9 0.7 copy.12
Async XLA Ops:
  2.6 39.5 %copy-start = (bf16[1,1,32,128,128]{4,3,2,1,0:T(8,128)(2,1)S(1)}, bf16[1,1,32,128,128]{4,3,2,1,0:T(8,128)(2,1)}, u32[]{:S(2)}) copy-start(bf16[1,1,32,128,128]{4,3,2,1,0:T(8,128)(2,1)} %param.9) | copy-start | bytes 3145732
  2.6 39.5 %all-to-all-start = ((bf16[32,128,128]{2,1,0:T(8,128)(2,1)}), bf16[32,128,128]{2,1,0:T(8,128)(2,1)S(1)}, u32[]{:S(2)}, u32[]{:S(2)}) async-start(bf16[32,128,128]{2,1,0:T(8,128)(2,1)} %broadcast_in_dim.14), calls=%async_computation | async-start | bytes 2097152 | tf_op jit(solution)/shard_map/all_to_all | solution.py:149
  42.1 33.2 %copy-start.1 = (bf16[128,256]{1,0:T(8,128)(2,1)S(1)}, bf16[128,256]{1,0:T(8,128)(2,1)}, u32[]{:S(2)}) copy-start(bf16[128,256]{1,0:T(8,128)(2,1)} %w_ref.1) | copy-start | bytes 196612
  42.1 33.2 %copy-start.2 = (bf16[1,128,256]{2,1,0:T(8,128)(2,1)S(1)}, bf16[1,128,256]{2,1,0:T(8,128)(2,1)}, u32[]{:S(2)}) copy-start(bf16[1,128,256]{2,1,0:T(8,128)(2,1)} %param.13) | copy-start | bytes 196612
  141.1 15.8 %all-to-all-start.4 = ((f32[16,8,256]{2,1,0:T(8,128)}), f32[16,8,256]{2,1,0:T(8,128)S(1)}, u32[]{:S(2)}, u32[]{:S(2)}) async-start(f32[16,8,256]{2,1,0:T(8,128)} %shard_map.97), calls=%async_computation.4 | async-start | bytes 262144 | tf_op jit(solution)/shard_map/all_to_all | solution.py:169

commit v18 on v16

--- a/solution.py
+++ b/solution.py
@@ -19,14 +19,14 @@
     for first in range(0, slots, group):
         terms = []
         for t in range(first, first + group):
-            tile = tiles_ref[t]
+            tile = jnp.where(t < live, tiles_ref[t], jnp.zeros((), tiles_ref.dtype))
             src = src_ref[jnp.clip(cols_ref[t], 0, n_src), :tb, :]
             if transpose:
                 term = lax.dot_general(tile, src, (((0,), (0,)), ((), ())),
                                        preferred_element_type=jnp.float32)
             else:
                 term = jnp.dot(tile, src, preferred_element_type=jnp.float32)
-            terms.append(jnp.where(t < live, term, 0.0))
+            terms.append(term)
         for t, term in zip(range(first, first + group), terms):
             acc_ref[jnp.clip(rows_ref[t], 0, n_acc)] += term
     if not carry_words:

time: 158 us -> 158 us (level)
  no operation moved by 1% of the time
where the time goes in v18:
time: 158 us
  blocking collectives  92.6 us (59%)
  waiting for transfers between devices  34.7 us (22%)
  starting transfers between devices  19.2 us (12%)
  Pallas kernels  5.88 us (4%)
  local copies, waits for them, and re-layouts  3.3 us (2%)
    all_to_all x1, blocking collectives, on_device(): got = lax.all_to_all(payload, 'row', 0, 0, tiled=False)  38.9 us
    all_to_all x1, blocking collectives, on_device(): got = lax.all_to_all(sent, 'col', 0, 0, tiled=False)  31.1 us
    all_to_all x1, waiting for transfers between devices, on_device(): lax.all_to_all(jnp.broadcast_to(own[None], (n_row,) + own.shape), 'row',...  25.2 us
    all_to_all x1, blocking collectives, on_device(): got = lax.all_to_all(payload, 'col', 0, 0, tiled=False)  22.6 us
    all_to_all x1, starting transfers between devices, on_device(): lax.all_to_all(jnp.broadcast_to(own[None], (n_row,) + own.shape), 'row',...  13.6 us
    all_to_all x1, waiting for transfers between devices, on_device(): lax.all_to_all(jnp.broadcast_to(wg_part[None], (n_col,) + wg_part.shape),...  9.45 us
    all_to_all x1, starting transfers between devices, on_device(): lax.all_to_all(jnp.broadcast_to(wg_part[None], (n_col,) + wg_part.shape),...  5.56 us
    pallas_call x2, Pallas kernels, spread(): pl.pallas_call(functools.partial(spread_kernel, transpose, carry_words),...  4.69 us
  transfers between devices with their start and end apart: 2, of which 2 were waited for; matrix products, arithmetic and copies ran while one was open for 0% of the time, Pallas kernels for 0%

profile of v18, /device:TPU:1, one launch (start us, length us, event | category | flops | bytes accessed | tf_op | source)
XLA Modules:
  0.0 157.7 jit_solution(6688378660321695967)
XLA Ops:
  0.6 2.0 %broadcast_in_dim.21 = bf16[32,128,128]{2,1,0:T(8,128)(2,1)} broadcast(bf16[128,128]{1,0:T(8,128)(2,1)} %bitcast.21), dimensions={1,2} | broadcast | bytes 1081344 | tf_op jit(solution)/shard_map/broadcast_in_dim | solution.py:125
  2.6 0.0 copy-start
  2.6 13.6 %all-to-all-start = ((bf16[32,128,128]{2,1,0:T(8,128)(2,1)}), bf16[32,128,128]{2,1,0:T(8,128)(2,1)S(1)}, u32[]{:S(2)}, u32[]{:S(2)}) async-start(bf16[32,128,128]{2,1,0:T(8,128)(2,1)} %broadcast_in_dim.21), calls=%async_computation | async-start | bytes 2097152 | tf_op jit(solution)/shard_map/all_to_all | solution.py:124
  16.9 25.2 %all-to-all-done.src_ref = bf16[32,128,128]{2,1,0:T(8,128)(2,1)S(1)} async-done(((bf16[32,128,128]{2,1,0:T(8,128)(2,1)}), bf16[32,128,128]{2,1,0:T(8,128)(2,1)S(1)}, u32[]{:S(2)}, u32[]{:S(2)}) %all-to-all-start) | async-done | bytes 1048608 | tf_op jit(solution)/shard_map/all_to_all | solution.py:124
  42.1 0.0 copy-done
  42.1 0.0 copy-start.1
  42.1 0.0 copy-start.2
  42.1 2.2 %shard_map.94 = bf16[16,128,128]{2,1,0:T(8,128)(2,1)} custom-call(s32[32]{0:T(128)} %bitcast.23, s32[32]{0:T(128)} %bitcast.25, s32[1]{0:T(128)} %bitcast.15.count_ref, bf16[32,128,128]{2,1,0:T(8,128)(2,1)S(1)} %bitcast.17, bf16[32,128,128]{2,1,0:T(8,128)(2,1)S(1)} %all-to-all-done.src_ref), custom_call_target="tpu_custom_call" | custom-call | flops 134217728 | bytes 2621440 | tf_op jit(solution)/shard_map/pallas_call | solution.py:53
  44.3 31.1 %all_to_all.25.recv_ref = bf16[16,128,128]{2,1,0:T(8,128)(2,1)S(1)} all-to-all(bf16[16,128,128]{2,1,0:T(8,128)(2,1)} %shard_map.94), channel_id=1, replica_groups=mesh['row'=32,'col'=16] {'col'}, dimensions={0} | all-to-all | bytes 1048576 | tf_op jit(solution)/shard_map/all_to_all | solution.py:130
  75.3 0.0 copy-done.1
  75.3 0.0 copy-done.2
  75.3 1.2 shard_map.95
  76.5 22.6 %all_to_all.26.src_ref = bf16[16,144,128]{2,1,0:T(8,128)(2,1)S(1)} all-to-all(bf16[16,144,128]{2,1,0:T(8,128)(2,1)} %get-tuple-element.6), channel_id=1, replica_groups=mesh['row'=32,'col'=16] {'col'}, dimensions={0} | all-to-all | bytes 1179648 | tf_op jit(solution)/shard_map/all_to_all | solution.py:134
  99.1 2.5 %shard_map.96 = bf16[32,144,128]{2,1,0:T(8,128)(2,1)} custom-call(s32[32]{0:T(128)} %bitcast.26, s32[32]{0:T(128)} %bitcast.24, s32[1]{0:T(128)} %bitcast.16.count_ref, bf16[32,128,128]{2,1,0:T(8,128)(2,1)S(1)} %bitcast.18, bf16[16,144,128]{2,1,0:T(8,128)(2,1)S(1)} %all_to_all.26.src_ref), custom_call_target="tpu_custom_call" | custom-call | flops 134217728 | bytes 2818048 | tf_op jit(solution)/shard_map/pallas_call | solution.py:53
  101.6 38.9 %all_to_all.27 = bf16[32,144,128]{2,1,0:T(8,128)(2,1)S(1)} all-to-all(bf16[32,144,128]{2,1,0:T(8,128)(2,1)} %shard_map.96), channel_id=1, replica_groups=mesh['row'=32,'col'=16] {'row'}, dimensions={0} | all-to-all | bytes 2359296 | tf_op jit(solution)/shard_map/all_to_all | solution.py:140
  140.6 0.7 broadcast_in_dim.25
  141.3 5.6 %all-to-all-start.4 = ((f32[16,8,256]{2,1,0:T(8,128)}), f32[16,8,256]{2,1,0:T(8,128)S(1)}, u32[]{:S(2)}, u32[]{:S(2)}) async-start(f32[16,8,256]{2,1,0:T(8,128)} %broadcast_in_dim.25), calls=%async_computation.4 | async-start | bytes 262144 | tf_op jit(solution)/shard_map/all_to_all | solution.py:145
  146.8 0.8 slice_reduce_fusion
  147.6 9.4 %all-to-all-done.4 = f32[16,8,256]{2,1,0:T(8,128)S(1)} async-done(((f32[16,8,256]{2,1,0:T(8,128)}), f32[16,8,256]{2,1,0:T(8,128)S(1)}, u32[]{:S(2)}, u32[]{:S(2)}) %all-to-all-start.4) | async-done | bytes 131104 | tf_op jit(solution)/shard_map/all_to_all | solution.py:145
  157.0 0.7 copy.12
  (2 shorter events, 0.0 us)
Async XLA Ops:
  2.6 39.5 %copy-start = (bf16[1,1,32,128,128]{4,3,2,1,0:T(8,128)(2,1)S(1)}, bf16[1,1,32,128,128]{4,3,2,1,0:T(8,128)(2,1)}, u32[]{:S(2)}) copy-start(bf16[1,1,32,128,128]{4,3,2,1,0:T(8,128)(2,1)} %param.9) | copy-start | bytes 3145732
  2.6 39.5 %all-to-all-start = ((bf16[32,128,128]{2,1,0:T(8,128)(2,1)}), bf16[32,128,128]{2,1,0:T(8,128)(2,1)S(1)}, u32[]{:S(2)}, u32[]{:S(2)}) async-start(bf16[32,128,128]{2,1,0:T(8,128)(2,1)} %broadcast_in_dim.21), calls=%async_computation | async-start | bytes 2097152 | tf_op jit(solution)/shard_map/all_to_all | solution.py:124
  42.1 33.3 %copy-start.1 = (bf16[128,256]{1,0:T(8,128)(2,1)S(1)}, bf16[128,256]{1,0:T(8,128)(2,1)}, u32[]{:S(2)}) copy-start(bf16[128,256]{1,0:T(8,128)(2,1)} %w_ref.1) | copy-start | bytes 196612
  42.1 33.3 %copy-start.2 = (bf16[1,128,256]{2,1,0:T(8,128)(2,1)S(1)}, bf16[1,128,256]{2,1,0:T(8,128)(2,1)}, u32[]{:S(2)}) copy-start(bf16[1,128,256]{2,1,0:T(8,128)(2,1)} %param.13) | copy-start | bytes 196612
  141.3 15.8 %all-to-all-start.4 = ((f32[16,8,256]{2,1,0:T(8,128)}), f32[16,8,256]{2,1,0:T(8,128)S(1)}, u32[]{:S(2)}, u32[]{:S(2)}) async-start(f32[16,8,256]{2,1,0:T(8,128)} %broadcast_in_dim.25), calls=%async_computation.4 | async-start | bytes 262144 | tf_op jit(solution)/shard_map/all_to_all | solution.py:145

commit v19 on v16

--- a/solution.py
+++ b/solution.py
@@ -105,6 +105,22 @@
     )(*(pltpu.with_memory_space_constraint(x, pltpu.VMEM) for x in (recv, weight, cot)))
 
 
+def replicate_kernel(x_ref, out_ref):
+    out_ref[...] = jnp.broadcast_to(x_ref[...], out_ref.shape)
+
+
+def replicate(x, copies):
+    vmem = pl.BlockSpec(memory_space=pltpu.VMEM)
+    return pl.pallas_call(
+        replicate_kernel,
+        out_shape=jax.ShapeDtypeStruct((copies,) + x.shape[1:], x.dtype),
+        in_specs=[vmem],
+        out_specs=vmem,
+        cost_estimate=pl.CostEstimate(
+            flops=0, transcendentals=0, bytes_accessed=(copies + 1) * x.size * x.dtype.itemsize),
+    )(pltpu.with_memory_space_constraint(x, pltpu.VMEM))
+
+
 def on_device(features, weight, tile_values, tile_rows, tile_cols, tile_count, cotangent):
     rows_dev = features.shape[1]
     width_in = features.shape[2]
@@ -120,10 +136,7 @@
     col_ids = tile_cols[0, 0]
     tile_total = tile_count[0, 0]
 
-    own = features[0]
-    gathered = lax.all_to_all(
-        jnp.broadcast_to(own[None], (n_row,) + own.shape), "row", 0, 0, tiled=False
-    )
+    gathered = lax.all_to_all(replicate(features, n_row), "row", 0, 0, tiled=False)
     col_source = gathered.reshape(col_tiles, tile_size, width_in)
     partial_value = spread(tile_block, row_ids, col_ids, tile_total, col_source, row_tiles, False, jnp.bfloat16)
     sent = partial_value.reshape(n_col, rows_dev, width_in)

time: 158 us -> 158 us (level)
    broadcast_in_dim x1 -> x0, local copies, waits for them, and re-layouts: 1.97 us -> none  [on_device(): jnp.broadcast_to(own[None], (n_row,) + own.shape)]
where the time goes in v19:
time: 158 us
  blocking collectives  92.6 us (59%)
  waiting for transfers between devices  34.7 us (22%)
  starting transfers between devices  19.2 us (12%)
  Pallas kernels  6.97 us (4%)
  local copies, waits for them, and re-layouts  2.08 us (1%)
    all_to_all x1, blocking collectives, on_device(): got = lax.all_to_all(payload, 'row', 0, 0, tiled=False)  38.9 us
    all_to_all x1, blocking collectives, on_device(): got = lax.all_to_all(sent, 'col', 0, 0, tiled=False)  31.1 us
    all_to_all x1, waiting for transfers between devices, on_device(): lax.all_to_all(replicate(features, n_row), 'row', 0, 0, tiled=False)  25.2 us
    all_to_all x1, blocking collectives, on_device(): got = lax.all_to_all(payload, 'col', 0, 0, tiled=False)  22.6 us
    all_to_all x1, starting transfers between devices, on_device(): lax.all_to_all(replicate(features, n_row), 'row', 0, 0, tiled=False)  13.6 us
    all_to_all x1, waiting for transfers between devices, on_device(): lax.all_to_all(jnp.broadcast_to(wg_part[None], (n_col,) + wg_part.shape),...  9.44 us
    all_to_all x1, starting transfers between devices, on_device(): lax.all_to_all(jnp.broadcast_to(wg_part[None], (n_col,) + wg_part.shape),...  5.56 us
    pallas_call x2, Pallas kernels, spread(): pl.pallas_call(functools.partial(spread_kernel, transpose, carry_words),...  4.56 us
  transfers between devices with their start and end apart: 2, of which 2 were waited for; matrix products, arithmetic and copies ran while one was open for 0% of the time, Pallas kernels for 0%

profile of v19, /device:TPU:1, one launch (start us, length us, event | category | flops | bytes accessed | tf_op | source)
XLA Modules:
  0.0 157.6 jit_solution(12188738065763647114)
XLA Ops:
  0.6 0.0 copy-start.3
  0.6 0.7 copy-done.3
  1.4 1.2 shard_map.94
  2.6 0.0 copy-start
  2.6 13.6 %all-to-all-start = ((bf16[32,128,128]{2,1,0:T(8,128)(2,1)}), bf16[32,128,128]{2,1,0:T(8,128)(2,1)S(1)}, u32[]{:S(2)}, u32[]{:S(2)}) async-start(bf16[32,128,128]{2,1,0:T(8,128)(2,1)} %shard_map.94), calls=%async_computation | async-start | bytes 2097152 | tf_op jit(solution)/shard_map/all_to_all | solution.py:139
  16.8 25.2 %all-to-all-done.src_ref = bf16[32,128,128]{2,1,0:T(8,128)(2,1)S(1)} async-done(((bf16[32,128,128]{2,1,0:T(8,128)(2,1)}), bf16[32,128,128]{2,1,0:T(8,128)(2,1)S(1)}, u32[]{:S(2)}, u32[]{:S(2)}) %all-to-all-start) | async-done | bytes 1048608 | tf_op jit(solution)/shard_map/all_to_all | solution.py:139
  42.1 0.0 copy-done
  42.1 0.0 copy-start.1
  42.1 0.0 copy-start.2
  42.1 2.1 %shard_map.95 = bf16[16,128,128]{2,1,0:T(8,128)(2,1)} custom-call(s32[32]{0:T(128)} %bitcast.21, s32[32]{0:T(128)} %bitcast.23, s32[1]{0:T(128)} %bitcast.14.count_ref, bf16[32,128,128]{2,1,0:T(8,128)(2,1)S(1)} %bitcast.16, bf16[32,128,128]{2,1,0:T(8,128)(2,1)S(1)} %all-to-all-done.src_ref), custom_call_target="tpu_custom_call" | custom-call | flops 134217728 | bytes 2621440 | tf_op jit(solution)/shard_map/pallas_call | solution.py:53
  44.2 31.1 %all_to_all.25.recv_ref = bf16[16,128,128]{2,1,0:T(8,128)(2,1)S(1)} all-to-all(bf16[16,128,128]{2,1,0:T(8,128)(2,1)} %shard_map.95), channel_id=1, replica_groups=mesh['row'=32,'col'=16] {'col'}, dimensions={0} | all-to-all | bytes 1048576 | tf_op jit(solution)/shard_map/all_to_all | solution.py:143
  75.3 0.0 copy-done.1
  75.3 0.0 copy-done.2
  75.3 1.2 shard_map.96
  76.5 22.6 %all_to_all.26.src_ref = bf16[16,144,128]{2,1,0:T(8,128)(2,1)S(1)} all-to-all(bf16[16,144,128]{2,1,0:T(8,128)(2,1)} %get-tuple-element.6), channel_id=1, replica_groups=mesh['row'=32,'col'=16] {'col'}, dimensions={0} | all-to-all | bytes 1179648 | tf_op jit(solution)/shard_map/all_to_all | solution.py:147
  99.0 2.4 %shard_map.97 = bf16[32,144,128]{2,1,0:T(8,128)(2,1)} custom-call(s32[32]{0:T(128)} %bitcast.24, s32[32]{0:T(128)} %bitcast.22, s32[1]{0:T(128)} %bitcast.15.count_ref, bf16[32,128,128]{2,1,0:T(8,128)(2,1)S(1)} %bitcast.17, bf16[16,144,128]{2,1,0:T(8,128)(2,1)S(1)} %all_to_all.26.src_ref), custom_call_target="tpu_custom_call" | custom-call | flops 134217728 | bytes 2818048 | tf_op jit(solution)/shard_map/pallas_call | solution.py:53
  101.5 38.9 %all_to_all.27 = bf16[32,144,128]{2,1,0:T(8,128)(2,1)S(1)} all-to-all(bf16[32,144,128]{2,1,0:T(8,128)(2,1)} %shard_map.97), channel_id=1, replica_groups=mesh['row'=32,'col'=16] {'row'}, dimensions={0} | all-to-all | bytes 2359296 | tf_op jit(solution)/shard_map/all_to_all | solution.py:153
  140.5 0.7 broadcast_in_dim.16
  141.1 5.6 %all-to-all-start.4 = ((f32[16,8,256]{2,1,0:T(8,128)}), f32[16,8,256]{2,1,0:T(8,128)S(1)}, u32[]{:S(2)}, u32[]{:S(2)}) async-start(f32[16,8,256]{2,1,0:T(8,128)} %broadcast_in_dim.16), calls=%async_computation.4 | async-start | bytes 262144 | tf_op jit(solution)/shard_map/all_to_all | solution.py:158
  146.7 0.8 slice_reduce_fusion
  147.5 9.4 %all-to-all-done.4 = f32[16,8,256]{2,1,0:T(8,128)S(1)} async-done(((f32[16,8,256]{2,1,0:T(8,128)}), f32[16,8,256]{2,1,0:T(8,128)S(1)}, u32[]{:S(2)}, u32[]{:S(2)}) %all-to-all-start.4) | async-done | bytes 131104 | tf_op jit(solution)/shard_map/all_to_all | solution.py:158
  156.9 0.7 copy.12
  (2 shorter events, 0.0 us)
Async XLA Ops:
  0.6 0.8 copy-start.3
  2.6 39.5 %copy-start = (bf16[1,1,32,128,128]{4,3,2,1,0:T(8,128)(2,1)S(1)}, bf16[1,1,32,128,128]{4,3,2,1,0:T(8,128)(2,1)}, u32[]{:S(2)}) copy-start(bf16[1,1,32,128,128]{4,3,2,1,0:T(8,128)(2,1)} %param.9) | copy-start | bytes 3145732
  2.6 39.5 %all-to-all-start = ((bf16[32,128,128]{2,1,0:T(8,128)(2,1)}), bf16[32,128,128]{2,1,0:T(8,128)(2,1)S(1)}, u32[]{:S(2)}, u32[]{:S(2)}) async-start(bf16[32,128,128]{2,1,0:T(8,128)(2,1)} %shard_map.94), calls=%async_computation | async-start | bytes 2097152 | tf_op jit(solution)/shard_map/all_to_all | solution.py:139
  42.1 33.2 %copy-start.1 = (bf16[128,256]{1,0:T(8,128)(2,1)S(1)}, bf16[128,256]{1,0:T(8,128)(2,1)}, u32[]{:S(2)}) copy-start(bf16[128,256]{1,0:T(8,128)(2,1)} %w_ref.1) | copy-start | bytes 196612
  42.1 33.2 %copy-start.2 = (bf16[1,128,256]{2,1,0:T(8,128)(2,1)S(1)}, bf16[1,128,256]{2,1,0:T(8,128)(2,1)}, u32[]{:S(2)}) copy-start(bf16[1,128,256]{2,1,0:T(8,128)(2,1)} %param.13) | copy-start | bytes 196612
  141.1 15.8 %all-to-all-start.4 = ((f32[16,8,256]{2,1,0:T(8,128)}), f32[16,8,256]{2,1,0:T(8,128)S(1)}, u32[]{:S(2)}, u32[]{:S(2)}) async-start(f32[16,8,256]{2,1,0:T(8,128)} %broadcast_in_dim.16), calls=%async_computation.4 | async-start | bytes 262144 | tf_op jit(solution)/shard_map/all_to_all | solution.py:158

commit v20 on v19

--- a/solution.py
+++ b/solution.py
@@ -15,7 +15,7 @@
     n_src = src_ref.shape[0] - 1
     n_acc = acc_ref.shape[0] - 1
     slots = tiles_ref.shape[0]
-    group = 2 if slots % 2 == 0 else 1
+    group = 4 if slots % 4 == 0 else 1
     for first in range(0, slots, group):
         terms = []
         for t in range(first, first + group):

time: 158 us -> 158 us (level)
  no operation moved by 1% of the time
where the time goes in v20:
time: 158 us
  blocking collectives  92.6 us (59%)
  waiting for transfers between devices  34.7 us (22%)
  starting transfers between devices  19.1 us (12%)
  Pallas kernels  6.96 us (4%)
  local copies, waits for them, and re-layouts  2.08 us (1%)
    all_to_all x1, blocking collectives, on_device(): got = lax.all_to_all(payload, 'row', 0, 0, tiled=False)  39 us
    all_to_all x1, blocking collectives, on_device(): got = lax.all_to_all(sent, 'col', 0, 0, tiled=False)  31.1 us
    all_to_all x1, waiting for transfers between devices, on_device(): lax.all_to_all(replicate(features, n_row), 'row', 0, 0, tiled=False)  25.2 us
    all_to_all x1, blocking collectives, on_device(): got = lax.all_to_all(payload, 'col', 0, 0, tiled=False)  22.6 us
    all_to_all x1, starting transfers between devices, on_device(): lax.all_to_all(replicate(features, n_row), 'row', 0, 0, tiled=False)  13.6 us
    all_to_all x1, waiting for transfers between devices, on_device(): lax.all_to_all(jnp.broadcast_to(wg_part[None], (n_col,) + wg_part.shape),...  9.48 us
    all_to_all x1, starting transfers between devices, on_device(): lax.all_to_all(jnp.broadcast_to(wg_part[None], (n_col,) + wg_part.shape),...  5.54 us
    pallas_call x2, Pallas kernels, spread(): pl.pallas_call(functools.partial(spread_kernel, transpose, carry_words),...  4.55 us
  transfers between devices with their start and end apart: 2, of which 2 were waited for; matrix products, arithmetic and copies ran while one was open for 0% of the time, Pallas kernels for 0%

profile of v20, /device:TPU:1, one launch (start us, length us, event | category | flops | bytes accessed | tf_op | source)
XLA Modules:
  0.0 157.6 jit_solution(8987183521040290016)
XLA Ops:
  0.6 0.0 copy-start.3
  0.6 0.7 copy-done.3
  1.4 1.2 shard_map.94
  2.6 0.0 copy-start
  2.6 13.6 %all-to-all-start = ((bf16[32,128,128]{2,1,0:T(8,128)(2,1)}), bf16[32,128,128]{2,1,0:T(8,128)(2,1)S(1)}, u32[]{:S(2)}, u32[]{:S(2)}) async-start(bf16[32,128,128]{2,1,0:T(8,128)(2,1)} %shard_map.94), calls=%async_computation | async-start | bytes 2097152 | tf_op jit(solution)/shard_map/all_to_all | solution.py:139
  16.8 25.2 %all-to-all-done.src_ref = bf16[32,128,128]{2,1,0:T(8,128)(2,1)S(1)} async-done(((bf16[32,128,128]{2,1,0:T(8,128)(2,1)}), bf16[32,128,128]{2,1,0:T(8,128)(2,1)S(1)}, u32[]{:S(2)}, u32[]{:S(2)}) %all-to-all-start) | async-done | bytes 1048608 | tf_op jit(solution)/shard_map/all_to_all | solution.py:139
  42.1 0.0 copy-done
  42.1 0.0 copy-start.1
  42.1 0.0 copy-start.2
  42.1 2.1 %shard_map.95 = bf16[16,128,128]{2,1,0:T(8,128)(2,1)} custom-call(s32[32]{0:T(128)} %bitcast.21, s32[32]{0:T(128)} %bitcast.23, s32[1]{0:T(128)} %bitcast.14.count_ref, bf16[32,128,128]{2,1,0:T(8,128)(2,1)S(1)} %bitcast.16, bf16[32,128,128]{2,1,0:T(8,128)(2,1)S(1)} %all-to-all-done.src_ref), custom_call_target="tpu_custom_call" | custom-call | flops 134217728 | bytes 2621440 | tf_op jit(solution)/shard_map/pallas_call | solution.py:53
  44.2 31.1 %all_to_all.25.recv_ref = bf16[16,128,128]{2,1,0:T(8,128)(2,1)S(1)} all-to-all(bf16[16,128,128]{2,1,0:T(8,128)(2,1)} %shard_map.95), channel_id=1, replica_groups=mesh['row'=32,'col'=16] {'col'}, dimensions={0} | all-to-all | bytes 1048576 | tf_op jit(solution)/shard_map/all_to_all | solution.py:143
  75.3 0.0 copy-done.1
  75.3 0.0 copy-done.2
  75.3 1.2 shard_map.96
  76.5 22.6 %all_to_all.26.src_ref = bf16[16,144,128]{2,1,0:T(8,128)(2,1)S(1)} all-to-all(bf16[16,144,128]{2,1,0:T(8,128)(2,1)} %get-tuple-element.6), channel_id=1, replica_groups=mesh['row'=32,'col'=16] {'col'}, dimensions={0} | all-to-all | bytes 1179648 | tf_op jit(solution)/shard_map/all_to_all | solution.py:147
  99.0 2.4 %shard_map.97 = bf16[32,144,128]{2,1,0:T(8,128)(2,1)} custom-call(s32[32]{0:T(128)} %bitcast.24, s32[32]{0:T(128)} %bitcast.22, s32[1]{0:T(128)} %bitcast.15.count_ref, bf16[32,128,128]{2,1,0:T(8,128)(2,1)S(1)} %bitcast.17, bf16[16,144,128]{2,1,0:T(8,128)(2,1)S(1)} %all_to_all.26.src_ref), custom_call_target="tpu_custom_call" | custom-call | flops 134217728 | bytes 2818048 | tf_op jit(solution)/shard_map/pallas_call | solution.py:53
  101.5 39.0 %all_to_all.27 = bf16[32,144,128]{2,1,0:T(8,128)(2,1)S(1)} all-to-all(bf16[32,144,128]{2,1,0:T(8,128)(2,1)} %shard_map.97), channel_id=1, replica_groups=mesh['row'=32,'col'=16] {'row'}, dimensions={0} | all-to-all | bytes 2359296 | tf_op jit(solution)/shard_map/all_to_all | solution.py:153
  140.5 0.7 broadcast_in_dim.16
  141.2 5.5 %all-to-all-start.4 = ((f32[16,8,256]{2,1,0:T(8,128)}), f32[16,8,256]{2,1,0:T(8,128)S(1)}, u32[]{:S(2)}, u32[]{:S(2)}) async-start(f32[16,8,256]{2,1,0:T(8,128)} %broadcast_in_dim.16), calls=%async_computation.4 | async-start | bytes 262144 | tf_op jit(solution)/shard_map/all_to_all | solution.py:158
  146.7 0.8 slice_reduce_fusion
  147.5 9.5 %all-to-all-done.4 = f32[16,8,256]{2,1,0:T(8,128)S(1)} async-done(((f32[16,8,256]{2,1,0:T(8,128)}), f32[16,8,256]{2,1,0:T(8,128)S(1)}, u32[]{:S(2)}, u32[]{:S(2)}) %all-to-all-start.4) | async-done | bytes 131104 | tf_op jit(solution)/shard_map/all_to_all | solution.py:158
  156.9 0.7 copy.12
  (2 shorter events, 0.0 us)
Async XLA Ops:
  0.6 0.8 copy-start.3
  2.6 39.5 %copy-start = (bf16[1,1,32,128,128]{4,3,2,1,0:T(8,128)(2,1)S(1)}, bf16[1,1,32,128,128]{4,3,2,1,0:T(8,128)(2,1)}, u32[]{:S(2)}) copy-start(bf16[1,1,32,128,128]{4,3,2,1,0:T(8,128)(2,1)} %param.9) | copy-start | bytes 3145732
  2.6 39.5 %all-to-all-start = ((bf16[32,128,128]{2,1,0:T(8,128)(2,1)}), bf16[32,128,128]{2,1,0:T(8,128)(2,1)S(1)}, u32[]{:S(2)}, u32[]{:S(2)}) async-start(bf16[32,128,128]{2,1,0:T(8,128)(2,1)} %shard_map.94), calls=%async_computation | async-start | bytes 2097152 | tf_op jit(solution)/shard_map/all_to_all | solution.py:139
  42.1 33.2 %copy-start.1 = (bf16[128,256]{1,0:T(8,128)(2,1)S(1)}, bf16[128,256]{1,0:T(8,128)(2,1)}, u32[]{:S(2)}) copy-start(bf16[128,256]{1,0:T(8,128)(2,1)} %w_ref.1) | copy-start | bytes 196612
  42.1 33.2 %copy-start.2 = (bf16[1,128,256]{2,1,0:T(8,128)(2,1)S(1)}, bf16[1,128,256]{2,1,0:T(8,128)(2,1)}, u32[]{:S(2)}) copy-start(bf16[1,128,256]{2,1,0:T(8,128)(2,1)} %param.13) | copy-start | bytes 196612
  141.2 15.8 %all-to-all-start.4 = ((f32[16,8,256]{2,1,0:T(8,128)}), f32[16,8,256]{2,1,0:T(8,128)S(1)}, u32[]{:S(2)}, u32[]{:S(2)}) async-start(f32[16,8,256]{2,1,0:T(8,128)} %broadcast_in_dim.16), calls=%async_computation.4 | async-start | bytes 262144 | tf_op jit(solution)/shard_map/all_to_all | solution.py:158

commit v21 on v17

--- a/solution.py
+++ b/solution.py
@@ -15,7 +15,7 @@
     n_src = src_ref.shape[0] - 1
     n_acc = acc_ref.shape[0] - 1
     slots = tiles_ref.shape[0]
-    group = 2 if slots % 2 == 0 else 1
+    group = 4 if slots % 4 == 0 else 1
     for first in range(0, slots, group):
         terms = []
         for t in range(first, first + group):
@@ -105,6 +105,22 @@
     )(*(pltpu.with_memory_space_constraint(x, pltpu.VMEM) for x in (recv, weight, cot)))
 
 
+def replicate_kernel(x_ref, out_ref):
+    out_ref[...] = jnp.broadcast_to(x_ref[...], out_ref.shape)
+
+
+def replicate(x, copies):
+    vmem = pl.BlockSpec(memory_space=pltpu.VMEM)
+    return pl.pallas_call(
+        replicate_kernel,
+        out_shape=jax.ShapeDtypeStruct((copies,) + x.shape[1:], x.dtype),
+        in_specs=[vmem],
+        out_specs=vmem,
+        cost_estimate=pl.CostEstimate(
+            flops=0, transcendentals=0, bytes_accessed=(copies + 1) * x.size * x.dtype.itemsize),
+    )(pltpu.with_memory_space_constraint(x, pltpu.VMEM))
+
+
 def weight_part_kernel(tb, rows, scale, got_ref, out_ref):
     wg = jnp.zeros((2 * rows, got_ref.shape[2]), jnp.float32)
     for j in range(got_ref.shape[0]):
@@ -145,10 +161,7 @@
     col_ids = tile_cols[0, 0]
     tile_total = tile_count[0, 0]
 
-    own = features[0]
-    gathered = lax.all_to_all(
-        jnp.broadcast_to(own[None], (n_row,) + own.shape), "row", 0, 0, tiled=False
-    )
+    gathered = lax.all_to_all(replicate(features, n_row), "row", 0, 0, tiled=False)
     col_source = gathered.reshape(col_tiles, tile_size, width_in)
     partial_value = spread(tile_block, row_ids, col_ids, tile_total, col_source, row_tiles, False, jnp.bfloat16)
     sent = partial_value.reshape(n_col, rows_dev, width_in)

time: 158 us -> 158 us (level)
    broadcast_in_dim x1 -> x0, local copies, waits for them, and re-layouts: 1.97 us -> none  [on_device(): jnp.broadcast_to(own[None], (n_row,) + own.shape)]
where the time goes in v21:
time: 158 us
  blocking collectives  92.5 us (59%)
  waiting for transfers between devices  34.7 us (22%)
  starting transfers between devices  19.2 us (12%)
  Pallas kernels  7.69 us (5%)
    all_to_all x1, blocking collectives, on_device(): got = lax.all_to_all(payload, 'row', 0, 0, tiled=False)  38.9 us
    all_to_all x1, blocking collectives, on_device(): got = lax.all_to_all(sent, 'col', 0, 0, tiled=False)  31.1 us
    all_to_all x1, waiting for transfers between devices, on_device(): lax.all_to_all(replicate(features, n_row), 'row', 0, 0, tiled=False)  25.2 us
    all_to_all x1, blocking collectives, on_device(): got = lax.all_to_all(payload, 'col', 0, 0, tiled=False)  22.6 us
    all_to_all x1, starting transfers between devices, on_device(): lax.all_to_all(replicate(features, n_row), 'row', 0, 0, tiled=False)  13.6 us
    all_to_all x1, waiting for transfers between devices, on_device(): everyone = lax.all_to_all(parts, 'col', 0, 0, tiled=False)  9.48 us
    all_to_all x1, starting transfers between devices, on_device(): everyone = lax.all_to_all(parts, 'col', 0, 0, tiled=False)  5.59 us
    pallas_call x2, Pallas kernels, spread(): pl.pallas_call(functools.partial(spread_kernel, transpose, carry_words),...  4.58 us
  transfers between devices with their start and end apart: 2, of which 2 were waited for; matrix products, arithmetic and copies ran while one was open for 0% of the time, Pallas kernels for 0%

profile of v21, /device:TPU:1, one launch (start us, length us, event | category | flops | bytes accessed | tf_op | source)
XLA Modules:
  0.0 157.6 jit_solution(14600443162450284800)
XLA Ops:
  0.6 0.0 copy-start.3
  0.6 0.7 copy-done.3
  1.4 1.2 shard_map.94
  2.6 0.0 copy-start
  2.6 13.6 %all-to-all-start = ((bf16[32,128,128]{2,1,0:T(8,128)(2,1)}), bf16[32,128,128]{2,1,0:T(8,128)(2,1)S(1)}, u32[]{:S(2)}, u32[]{:S(2)}) async-start(bf16[32,128,128]{2,1,0:T(8,128)(2,1)} %shard_map.94), calls=%async_computation | async-start | bytes 2097152 | tf_op jit(solution)/shard_map/all_to_all | solution.py:164
  16.9 25.2 %all-to-all-done.src_ref = bf16[32,128,128]{2,1,0:T(8,128)(2,1)S(1)} async-done(((bf16[32,128,128]{2,1,0:T(8,128)(2,1)}), bf16[32,128,128]{2,1,0:T(8,128)(2,1)S(1)}, u32[]{:S(2)}, u32[]{:S(2)}) %all-to-all-start) | async-done | bytes 1048608 | tf_op jit(solution)/shard_map/all_to_all | solution.py:164
  42.1 0.0 copy-done
  42.1 0.0 copy-start.1
  42.1 0.0 copy-start.2
  42.1 2.1 %shard_map.95 = bf16[16,128,128]{2,1,0:T(8,128)(2,1)} custom-call(s32[32]{0:T(128)} %bitcast.15, s32[32]{0:T(128)} %bitcast.17, s32[1]{0:T(128)} %bitcast.8.count_ref, bf16[32,128,128]{2,1,0:T(8,128)(2,1)S(1)} %bitcast.10, bf16[32,128,128]{2,1,0:T(8,128)(2,1)S(1)} %all-to-all-done.src_ref), custom_call_target="tpu_custom_call" | custom-call | flops 134217728 | bytes 2621440 | tf_op jit(solution)/shard_map/pallas_call | solution.py:53
  44.2 31.1 %all_to_all.25.recv_ref = bf16[16,128,128]{2,1,0:T(8,128)(2,1)S(1)} all-to-all(bf16[16,128,128]{2,1,0:T(8,128)(2,1)} %shard_map.95), channel_id=1, replica_groups=mesh['row'=32,'col'=16] {'col'}, dimensions={0} | all-to-all | bytes 1048576 | tf_op jit(solution)/shard_map/all_to_all | solution.py:168
  75.3 0.0 copy-done.1
  75.3 0.0 copy-done.2
  75.3 1.2 shard_map.96
  76.5 22.6 %all_to_all.26.src_ref = bf16[16,144,128]{2,1,0:T(8,128)(2,1)S(1)} all-to-all(bf16[16,144,128]{2,1,0:T(8,128)(2,1)} %get-tuple-element.6), channel_id=1, replica_groups=mesh['row'=32,'col'=16] {'col'}, dimensions={0} | all-to-all | bytes 1179648 | tf_op jit(solution)/shard_map/all_to_all | solution.py:172
  99.0 2.5 %shard_map.97 = bf16[32,144,128]{2,1,0:T(8,128)(2,1)} custom-call(s32[32]{0:T(128)} %bitcast.18, s32[32]{0:T(128)} %bitcast.16, s32[1]{0:T(128)} %bitcast.9.count_ref, bf16[32,128,128]{2,1,0:T(8,128)(2,1)S(1)} %bitcast.11, bf16[16,144,128]{2,1,0:T(8,128)(2,1)S(1)} %all_to_all.26.src_ref), custom_call_target="tpu_custom_call" | custom-call | flops 134217728 | bytes 2818048 | tf_op jit(solution)/shard_map/pallas_call | solution.py:53
  101.5 38.9 %all_to_all.27.got_ref = bf16[32,144,128]{2,1,0:T(8,128)(2,1)S(1)} all-to-all(bf16[32,144,128]{2,1,0:T(8,128)(2,1)} %shard_map.97), channel_id=1, replica_groups=mesh['row'=32,'col'=16] {'row'}, dimensions={0} | all-to-all | bytes 2359296 | tf_op jit(solution)/shard_map/all_to_all | solution.py:178
  140.4 0.7 shard_map.98
  141.1 5.6 %all-to-all-start.4 = ((f32[16,8,256]{2,1,0:T(8,128)}), f32[16,8,256]{2,1,0:T(8,128)S(1)}, u32[]{:S(2)}, u32[]{:S(2)}) async-start(f32[16,8,256]{2,1,0:T(8,128)} %shard_map.98), calls=%async_computation.4 | async-start | bytes 262144 | tf_op jit(solution)/shard_map/all_to_all | solution.py:182
  146.7 0.8 slice_reduce_fusion
  147.5 9.5 %all-to-all-done.4 = f32[16,8,256]{2,1,0:T(8,128)S(1)} async-done(((f32[16,8,256]{2,1,0:T(8,128)}), f32[16,8,256]{2,1,0:T(8,128)S(1)}, u32[]{:S(2)}, u32[]{:S(2)}) %all-to-all-start.4) | async-done | bytes 131104 | tf_op jit(solution)/shard_map/all_to_all | solution.py:182
  156.9 0.7 copy.12
Async XLA Ops:
  0.6 0.8 copy-start.3
  2.6 39.5 %copy-start = (bf16[1,1,32,128,128]{4,3,2,1,0:T(8,128)(2,1)S(1)}, bf16[1,1,32,128,128]{4,3,2,1,0:T(8,128)(2,1)}, u32[]{:S(2)}) copy-start(bf16[1,1,32,128,128]{4,3,2,1,0:T(8,128)(2,1)} %param.9) | copy-start | bytes 3145732
  2.6 39.5 %all-to-all-start = ((bf16[32,128,128]{2,1,0:T(8,128)(2,1)}), bf16[32,128,128]{2,1,0:T(8,128)(2,1)S(1)}, u32[]{:S(2)}, u32[]{:S(2)}) async-start(bf16[32,128,128]{2,1,0:T(8,128)(2,1)} %shard_map.94), calls=%async_computation | async-start | bytes 2097152 | tf_op jit(solution)/shard_map/all_to_all | solution.py:164
  42.1 33.2 %copy-start.1 = (bf16[128,256]{1,0:T(8,128)(2,1)S(1)}, bf16[128,256]{1,0:T(8,128)(2,1)}, u32[]{:S(2)}) copy-start(bf16[128,256]{1,0:T(8,128)(2,1)} %w_ref.1) | copy-start | bytes 196612
  42.1 33.2 %copy-start.2 = (bf16[1,128,256]{2,1,0:T(8,128)(2,1)S(1)}, bf16[1,128,256]{2,1,0:T(8,128)(2,1)}, u32[]{:S(2)}) copy-start(bf16[1,128,256]{2,1,0:T(8,128)(2,1)} %param.13) | copy-start | bytes 196612
  141.1 15.8 %all-to-all-start.4 = ((f32[16,8,256]{2,1,0:T(8,128)}), f32[16,8,256]{2,1,0:T(8,128)S(1)}, u32[]{:S(2)}, u32[]{:S(2)}) async-start(f32[16,8,256]{2,1,0:T(8,128)} %shard_map.98), calls=%async_computation.4 | async-start | bytes 262144 | tf_op jit(solution)/shard_map/all_to_all | solution.py:182
